TPU v7x, 32 devices: a whole 2x2x4 slice. The times are simulated.
32 devices in a mesh: wide: 8 (over y, x, core), narrow: 4 (over z).
Axes of the slice: x: 2, y: 2, z: 4, core: 2. Of those that a mesh axis runs over, the one named last changes fastest.
Arguments:
- tokens: bfloat16 [32, 256, 1536], P(('wide', 'narrow')), may hold values from -6 to 6
- cotangent: bfloat16 [32, 256, 1536], P(('wide', 'narrow')), may hold values from -6 to 6
- thresholds: float32 [32, 2], P(('wide', 'narrow')), may hold values from 0.5 to 4
- attn_norm_gain: bfloat16 [1536], P('narrow'), may hold values from 0.25 to 1.75
- attn_norm_shift: bfloat16 [1536], P('narrow'), may hold values from -4 to 4
- query_weight: bfloat16 [1536, 512], P('narrow'), may hold values from -0.15625 to 0.15625
- key_weight: bfloat16 [1536, 512], P('narrow'), may hold values from -0.15625 to 0.15625
- value_weight: bfloat16 [1536, 1536], P('narrow'), may hold values from -0.15625 to 0.15625
- relative_weight: bfloat16 [192, 512], P('narrow'), may hold values from -0.4375 to 0.4375
- content_bias: bfloat16 [512], P('narrow'), may hold values from -3 to 3
- position_bias: bfloat16 [512], P('narrow'), may hold values from -3 to 3
- out_weight: bfloat16 [1536, 1536], P('narrow'), may hold values from -1.25 to 1.25
- out_bias: bfloat16 [1536], P('narrow'), may hold values from -4 to 4
- mlp_norm_gain: bfloat16 [1536], P('narrow'), may hold values from 0.25 to 1.75
- mlp_norm_shift: bfloat16 [1536], P('narrow'), may hold values from -4 to 4
- inner_weight: bfloat16 [1536, 3072], P('narrow'), may hold values from -0.15625 to 0.15625
- inner_bias: bfloat16 [3072], P('narrow'), may hold values from -4 to 4
- outer_weight: bfloat16 [3072, 1536], P('narrow'), may hold values from -0.109375 to 0.109375
- outer_bias: bfloat16 [1536], P('narrow'), may hold values from -4 to 4
Outputs:
- layer_out: bfloat16 [32, 256, 1536], P(('wide', 'narrow'))
- tokens_grad: bfloat16 [32, 256, 1536], P(('wide', 'narrow'))
- attn_norm_gain_grad: float32 [1536], P('narrow')
- attn_norm_shift_grad: float32 [1536], P('narrow')
- query_weight_grad: float32 [1536, 512], P('narrow')
- key_weight_grad: float32 [1536, 512], P('narrow')
- value_weight_grad: float32 [1536, 1536], P('narrow')
- relative_weight_grad: float32 [192, 512], P('narrow')
- content_bias_grad: float32 [512], P('narrow')
- position_bias_grad: float32 [512], P('narrow')
- out_weight_grad: float32 [1536, 1536], P('narrow')
- out_bias_grad: float32 [1536], P('narrow')
- mlp_norm_gain_grad: float32 [1536], P('narrow')
- mlp_norm_shift_grad: float32 [1536], P('narrow')
- inner_weight_grad: float32 [1536, 3072], P('narrow')
- inner_bias_grad: float32 [3072], P('narrow')
- outer_weight_grad: float32 [3072, 1536], P('narrow')
- outer_bias_grad: float32 [1536], P('narrow')
All inputs are finite; a program needn't handle non-finite values.
Results may differ from a plain program's by a relative error of at most 0.023.
Values may be sent and summed in bfloat16 or wider, within the bound.
A program may use at most 256 MiB of HBM per device.

v0:
```python
import math

import jax
import jax.numpy as jnp
from jax import lax
from jax.sharding import PartitionSpec as P

H = 8
KEY = 64
VAL = 192
F = 192
WIN = 128


EPSILON = 1e-05


def basis_table(length, features):
    family = features // 6
    offsets = jnp.arange(2 * length - 1, dtype=jnp.float32) - (length - 1)
    distance = jnp.abs(offsets)[:, None]
    halves = 2.0 ** jnp.linspace(3.0, math.log2(length), family, dtype=jnp.float32)
    decays = jnp.exp(-math.log(2.0) / halves[None, :] * distance)
    widths = 2.0 ** jnp.arange(1, family + 1, dtype=jnp.float32) - 1.0
    central = jnp.where(widths[None, :] > distance, 1.0, 0.0).astype(jnp.float32)
    centers = jnp.linspace(0.0, float(length), family, dtype=jnp.float32)
    spread = length / family
    bump_rows = jnp.exp(-0.5 * ((distance - centers[None, :]) / spread) ** 2)
    positive = jnp.concatenate([decays, central, bump_rows], axis=1)
    return jnp.concatenate([positive, jnp.sign(offsets)[:, None] * positive], axis=1)


def shift_offsets(raw_scores, length):
    leading = raw_scores.shape[:-2]
    padded = jnp.pad(raw_scores, [(0, 0)] * len(leading) + [(0, 0), (0, 1)])
    flatten = padded.reshape(leading + (2 * length * length,))
    window = flatten[..., length - 1 : length - 1 + length * (2 * length - 1)]
    return window.reshape(leading + (length, 2 * length - 1))[..., :length]


def unshift_offsets(grad_scores, length):
    leading = grad_scores.shape[:-2]
    widened = jnp.pad(grad_scores, [(0, 0)] * len(leading) + [(0, 0), (0, length - 1)])
    flatten = widened.reshape(leading + (length * (2 * length - 1),))
    flatten = jnp.pad(flatten, [(0, 0)] * len(leading) + [(length - 1, 1)])
    return flatten.reshape(leading + (length, 2 * length))[..., : 2 * length - 1]


def layer_norm(values, gain, shift):
    center = values - jnp.mean(values, axis=-1, keepdims=True)
    spread = jnp.mean(center * center, axis=-1, keepdims=True)
    return center * lax.rsqrt(spread + EPSILON) * gain + shift


def gelu_exact(values):
    return jax.nn.gelu(values, approximate=False)


def column_sums(values):
    return jnp.sum(values.astype(jnp.float32), axis=0)


def per_device(
    tokens,
    cotangent,
    thresholds,
    attn_norm_gain,
    attn_norm_shift,
    query_weight,
    key_weight,
    value_weight,
    relative_weight,
    content_bias,
    position_bias,
    out_weight,
    out_bias,
    mlp_norm_gain,
    mlp_norm_shift,
    inner_weight,
    inner_bias,
    outer_weight,
    outer_bias,
):
    seq_count, length, model_width = tokens.shape
    row_count = seq_count * length
    span = 2 * length - 1
    query_scale = KEY ** (-0.5)
    (
        attn_gain,
        attn_shift,
        query_full,
        key_full,
        value_full,
        relative_full,
        content_full,
        position_full,
        exit_full,
        exit_bias,
    ) = (
        lax.all_gather(attn_norm_gain, "narrow", axis=0, tiled=True),
        lax.all_gather(attn_norm_shift, "narrow", axis=0, tiled=True),
        lax.all_gather(query_weight, "narrow", axis=0, tiled=True),
        lax.all_gather(key_weight, "narrow", axis=0, tiled=True),
        lax.all_gather(value_weight, "narrow", axis=0, tiled=True),
        lax.all_gather(relative_weight, "narrow", axis=0, tiled=True),
        lax.all_gather(content_bias, "narrow", axis=0, tiled=True),
        lax.all_gather(position_bias, "narrow", axis=0, tiled=True),
        lax.all_gather(out_weight, "narrow", axis=0, tiled=True),
        lax.all_gather(out_bias, "narrow", axis=0, tiled=True),
    )
    mlp_gain, mlp_shift, inner_full, inner_offset, outer_full, outer_offset = (
        lax.all_gather(mlp_norm_gain, "narrow", axis=0, tiled=True),
        lax.all_gather(mlp_norm_shift, "narrow", axis=0, tiled=True),
        lax.all_gather(inner_weight, "narrow", axis=0, tiled=True),
        lax.all_gather(inner_bias, "narrow", axis=0, tiled=True),
        lax.all_gather(outer_weight, "narrow", axis=0, tiled=True),
        lax.all_gather(outer_bias, "narrow", axis=0, tiled=True),
    )
    flat_tokens = tokens.reshape(row_count, model_width).astype(jnp.float32)
    attn_gain_f = attn_gain.astype(jnp.float32)
    attn_shift_f = attn_shift.astype(jnp.float32)
    normed = layer_norm(flat_tokens, attn_gain_f, attn_shift_f).astype(jnp.bfloat16)
    queries = jnp.dot(normed, query_full, preferred_element_type=jnp.float32) * query_scale
    content_query = (
        (queries + content_full.astype(jnp.float32))
        .astype(jnp.bfloat16)
        .reshape(seq_count, length, H, KEY)
    )
    position_query = (
        (queries + position_full.astype(jnp.float32))
        .astype(jnp.bfloat16)
        .reshape(seq_count, length, H, KEY)
    )
    key_rows = (
        jnp.dot(normed, key_full, preferred_element_type=jnp.float32)
        .astype(jnp.bfloat16)
        .reshape(seq_count, length, H, KEY)
    )
    value_rows = (
        jnp.dot(normed, value_full, preferred_element_type=jnp.float32)
        .astype(jnp.bfloat16)
        .reshape(seq_count, length, H, VAL)
    )
    basis = basis_table(length, F).astype(jnp.bfloat16)
    rel_keys = (
        jnp.dot(basis, relative_full, preferred_element_type=jnp.float32)
        .astype(jnp.bfloat16)
        .reshape(span, H, KEY)
    )

    def attention_logits():
        content = jnp.einsum(
            "bihe,bjhe->bhij", content_query, key_rows, preferred_element_type=jnp.float32
        )
        raw_scores = jnp.einsum(
            "bihe,the->bhit", position_query, rel_keys, preferred_element_type=jnp.float32
        )
        return content + shift_offsets(raw_scores, length)

    logits = attention_logits()
    row_peak = jnp.max(logits, axis=-1, keepdims=True)
    log_total = row_peak + jnp.log(jnp.sum(jnp.exp(logits - row_peak), axis=-1, keepdims=True))
    attention = jnp.exp(logits - log_total).astype(jnp.bfloat16)
    mixed_heads = jnp.einsum(
        "bhij,bjhd->bihd", attention, value_rows, preferred_element_type=jnp.float32
    )
    mixed_heads = mixed_heads.astype(jnp.bfloat16).reshape(row_count, H * VAL)
    hidden = flat_tokens + (
        jnp.dot(mixed_heads, exit_full, preferred_element_type=jnp.float32)
        + exit_bias.astype(jnp.float32)
    )
    mlp_gain_f = mlp_gain.astype(jnp.float32)
    mlp_shift_f = mlp_shift.astype(jnp.float32)
    normed_mid = layer_norm(hidden, mlp_gain_f, mlp_shift_f).astype(jnp.bfloat16)
    inner_pre = jnp.dot(
        normed_mid, inner_full, preferred_element_type=jnp.float32
    ) + inner_offset.astype(jnp.float32)
    active, gelu_pull = jax.vjp(gelu_exact, inner_pre)
    active_low = active.astype(jnp.bfloat16)
    result = hidden + (
        jnp.dot(active_low, outer_full, preferred_element_type=jnp.float32)
        + outer_offset.astype(jnp.float32)
    )
    layer_out = result.astype(jnp.bfloat16).reshape(seq_count, length, model_width)
    clip_limit = jnp.repeat(thresholds, WIN, axis=1).reshape(row_count, 1)
    clipped = jnp.clip(
        cotangent.reshape(row_count, model_width).astype(jnp.float32), -clip_limit, clip_limit
    )
    mlp_gain, mlp_shift, inner_full, inner_offset, outer_full, outer_offset = (
        lax.all_gather(mlp_norm_gain, "narrow", axis=0, tiled=True),
        lax.all_gather(mlp_norm_shift, "narrow", axis=0, tiled=True),
        lax.all_gather(inner_weight, "narrow", axis=0, tiled=True),
        lax.all_gather(inner_bias, "narrow", axis=0, tiled=True),
        lax.all_gather(outer_weight, "narrow", axis=0, tiled=True),
        lax.all_gather(outer_bias, "narrow", axis=0, tiled=True),
    )
    mlp_gain_f = mlp_gain.astype(jnp.float32)
    outer_delta = clipped.astype(jnp.bfloat16)
    outer_bias_grad = column_sums(outer_delta)
    outer_weight_grad = jnp.einsum(
        "nk,nm->km", active_low, outer_delta, preferred_element_type=jnp.float32
    )
    active_delta = jnp.einsum(
        "nm,km->nk", outer_delta, outer_full, preferred_element_type=jnp.float32
    )
    (inner_grad_pre,) = gelu_pull(active_delta)
    inner_delta = inner_grad_pre.astype(jnp.bfloat16)
    inner_bias_grad = column_sums(inner_delta)
    inner_weight_grad = jnp.einsum(
        "nd,nf->df", normed_mid, inner_delta, preferred_element_type=jnp.float32
    )
    mid_delta = jnp.einsum("nf,df->nd", inner_delta, inner_full, preferred_element_type=jnp.float32)
    norm_out, norm_pull = jax.vjp(layer_norm, hidden, mlp_gain_f, mlp_shift_f)
    hidden_part, mlp_gain_grad, mlp_shift_grad = norm_pull(mid_delta)
    hidden_delta = clipped + hidden_part
    (
        attn_gain,
        attn_shift,
        query_full,
        key_full,
        value_full,
        relative_full,
        content_full,
        position_full,
        exit_full,
        exit_bias,
    ) = (
        lax.all_gather(attn_norm_gain, "narrow", axis=0, tiled=True),
        lax.all_gather(attn_norm_shift, "narrow", axis=0, tiled=True),
        lax.all_gather(query_weight, "narrow", axis=0, tiled=True),
        lax.all_gather(key_weight, "narrow", axis=0, tiled=True),
        lax.all_gather(value_weight, "narrow", axis=0, tiled=True),
        lax.all_gather(relative_weight, "narrow", axis=0, tiled=True),
        lax.all_gather(content_bias, "narrow", axis=0, tiled=True),
        lax.all_gather(position_bias, "narrow", axis=0, tiled=True),
        lax.all_gather(out_weight, "narrow", axis=0, tiled=True),
        lax.all_gather(out_bias, "narrow", axis=0, tiled=True),
    )
    attn_gain_f = attn_gain.astype(jnp.float32)
    branch_delta = hidden_delta.astype(jnp.bfloat16)
    out_bias_grad = column_sums(branch_delta)
    out_weight_grad = jnp.einsum(
        "nk,nd->kd", mixed_heads, branch_delta, preferred_element_type=jnp.float32
    )
    mixed_delta = jnp.einsum(
        "nd,kd->nk", branch_delta, exit_full, preferred_element_type=jnp.float32
    )
    mixed_delta = mixed_delta.astype(jnp.bfloat16).reshape(seq_count, length, H, VAL)
    logits = attention_logits()
    soft_rows = jnp.exp(logits - log_total)
    attention = soft_rows.astype(jnp.bfloat16)
    attention_delta = jnp.einsum(
        "bihd,bjhd->bhij", mixed_delta, value_rows, preferred_element_type=jnp.float32
    )
    value_delta = jnp.einsum(
        "bhij,bihd->bjhd", attention, mixed_delta, preferred_element_type=jnp.float32
    )
    value_delta = value_delta.astype(jnp.bfloat16).reshape(row_count, H * VAL)
    logit_delta = soft_rows * (
        attention_delta - jnp.sum(soft_rows * attention_delta, axis=-1, keepdims=True)
    )
    logit_delta = logit_delta.astype(jnp.bfloat16)
    content_delta = jnp.einsum(
        "bhij,bjhe->bihe", logit_delta, key_rows, preferred_element_type=jnp.float32
    )
    key_delta = jnp.einsum(
        "bhij,bihe->bjhe", logit_delta, content_query, preferred_element_type=jnp.float32
    )
    key_delta = key_delta.astype(jnp.bfloat16).reshape(row_count, H * KEY)
    offset_delta = unshift_offsets(logit_delta, length)
    position_delta = jnp.einsum(
        "bhit,the->bihe", offset_delta, rel_keys, preferred_element_type=jnp.float32
    )
    rel_delta = jnp.einsum(
        "bhit,bihe->the", offset_delta, position_query, preferred_element_type=jnp.float32
    )
    rel_delta = rel_delta.astype(jnp.bfloat16).reshape(span, H * KEY)
    relative_weight_grad = jnp.einsum(
        "tf,tk->fk", basis, rel_delta, preferred_element_type=jnp.float32
    )
    content_delta = content_delta.reshape(row_count, H * KEY)
    position_delta = position_delta.reshape(row_count, H * KEY)
    content_bias_grad = jnp.sum(content_delta, axis=0)
    position_bias_grad = jnp.sum(position_delta, axis=0)
    query_delta = (content_delta + position_delta).astype(jnp.bfloat16) * jnp.asarray(
        query_scale, jnp.bfloat16
    )
    query_weight_grad = jnp.einsum(
        "nd,nk->dk", normed, query_delta, preferred_element_type=jnp.float32
    )
    key_weight_grad = jnp.einsum("nd,nk->dk", normed, key_delta, preferred_element_type=jnp.float32)
    value_weight_grad = jnp.einsum(
        "nd,nk->dk", normed, value_delta, preferred_element_type=jnp.float32
    )
    normed_delta = (
        jnp.einsum("nk,dk->nd", query_delta, query_full, preferred_element_type=jnp.float32)
        + jnp.einsum("nk,dk->nd", key_delta, key_full, preferred_element_type=jnp.float32)
        + jnp.einsum("nk,dk->nd", value_delta, value_full, preferred_element_type=jnp.float32)
    )
    first_out, first_pull = jax.vjp(layer_norm, flat_tokens, attn_gain_f, attn_shift_f)
    tokens_part, attn_gain_grad, attn_shift_grad = first_pull(normed_delta)
    tokens_grad = (
        (hidden_delta + tokens_part).astype(jnp.bfloat16).reshape(seq_count, length, model_width)
    )
    (
        query_weight_grad,
        key_weight_grad,
        value_weight_grad,
        relative_weight_grad,
        out_weight_grad,
        inner_weight_grad,
        outer_weight_grad,
    ) = (
        lax.psum_scatter(
            query_weight_grad.astype(jnp.bfloat16), "wide", scatter_dimension=1, tiled=True
        ).astype(jnp.float32),
        lax.psum_scatter(
            key_weight_grad.astype(jnp.bfloat16), "wide", scatter_dimension=1, tiled=True
        ).astype(jnp.float32),
        lax.psum_scatter(
            value_weight_grad.astype(jnp.bfloat16), "wide", scatter_dimension=1, tiled=True
        ).astype(jnp.float32),
        lax.psum_scatter(
            relative_weight_grad.astype(jnp.bfloat16), "wide", scatter_dimension=1, tiled=True
        ).astype(jnp.float32),
        lax.psum_scatter(
            out_weight_grad.astype(jnp.bfloat16), "wide", scatter_dimension=1, tiled=True
        ).astype(jnp.float32),
        lax.psum_scatter(
            inner_weight_grad.astype(jnp.bfloat16), "wide", scatter_dimension=1, tiled=True
        ).astype(jnp.float32),
        lax.psum_scatter(
            outer_weight_grad.astype(jnp.bfloat16), "wide", scatter_dimension=1, tiled=True
        ).astype(jnp.float32),
    )
    (
        query_weight_grad,
        key_weight_grad,
        value_weight_grad,
        relative_weight_grad,
        out_weight_grad,
        inner_weight_grad,
        outer_weight_grad,
        attn_gain_grad,
        attn_shift_grad,
        content_bias_grad,
        position_bias_grad,
        out_bias_grad,
        mlp_gain_grad,
        mlp_shift_grad,
        inner_bias_grad,
        outer_bias_grad,
    ) = (
        lax.psum_scatter(
            query_weight_grad.astype(jnp.bfloat16), "narrow", scatter_dimension=0, tiled=True
        ).astype(jnp.float32),
        lax.psum_scatter(
            key_weight_grad.astype(jnp.bfloat16), "narrow", scatter_dimension=0, tiled=True
        ).astype(jnp.float32),
        lax.psum_scatter(
            value_weight_grad.astype(jnp.bfloat16), "narrow", scatter_dimension=0, tiled=True
        ).astype(jnp.float32),
        lax.psum_scatter(
            relative_weight_grad.astype(jnp.bfloat16), "narrow", scatter_dimension=0, tiled=True
        ).astype(jnp.float32),
        lax.psum_scatter(
            out_weight_grad.astype(jnp.bfloat16), "narrow", scatter_dimension=0, tiled=True
        ).astype(jnp.float32),
        lax.psum_scatter(
            inner_weight_grad.astype(jnp.bfloat16), "narrow", scatter_dimension=0, tiled=True
        ).astype(jnp.float32),
        lax.psum_scatter(
            outer_weight_grad.astype(jnp.bfloat16), "narrow", scatter_dimension=0, tiled=True
        ).astype(jnp.float32),
        lax.psum_scatter(
            attn_gain_grad.astype(jnp.bfloat16), "narrow", scatter_dimension=0, tiled=True
        ).astype(jnp.float32),
        lax.psum_scatter(
            attn_shift_grad.astype(jnp.bfloat16), "narrow", scatter_dimension=0, tiled=True
        ).astype(jnp.float32),
        lax.psum_scatter(
            content_bias_grad.astype(jnp.bfloat16), "narrow", scatter_dimension=0, tiled=True
        ).astype(jnp.float32),
        lax.psum_scatter(
            position_bias_grad.astype(jnp.bfloat16), "narrow", scatter_dimension=0, tiled=True
        ).astype(jnp.float32),
        lax.psum_scatter(
            out_bias_grad.astype(jnp.bfloat16), "narrow", scatter_dimension=0, tiled=True
        ).astype(jnp.float32),
        lax.psum_scatter(
            mlp_gain_grad.astype(jnp.bfloat16), "narrow", scatter_dimension=0, tiled=True
        ).astype(jnp.float32),
        lax.psum_scatter(
            mlp_shift_grad.astype(jnp.bfloat16), "narrow", scatter_dimension=0, tiled=True
        ).astype(jnp.float32),
        lax.psum_scatter(
            inner_bias_grad.astype(jnp.bfloat16), "narrow", scatter_dimension=0, tiled=True
        ).astype(jnp.float32),
        lax.psum_scatter(
            outer_bias_grad.astype(jnp.bfloat16), "narrow", scatter_dimension=0, tiled=True
        ).astype(jnp.float32),
    )
    (
        query_weight_grad,
        key_weight_grad,
        value_weight_grad,
        relative_weight_grad,
        out_weight_grad,
        inner_weight_grad,
        outer_weight_grad,
    ) = (
        lax.all_gather(query_weight_grad.astype(jnp.bfloat16), "wide", axis=1, tiled=True).astype(
            query_weight_grad.dtype
        ),
        lax.all_gather(key_weight_grad.astype(jnp.bfloat16), "wide", axis=1, tiled=True).astype(
            key_weight_grad.dtype
        ),
        lax.all_gather(value_weight_grad.astype(jnp.bfloat16), "wide", axis=1, tiled=True).astype(
            value_weight_grad.dtype
        ),
        lax.all_gather(
            relative_weight_grad.astype(jnp.bfloat16), "wide", axis=1, tiled=True
        ).astype(relative_weight_grad.dtype),
        lax.all_gather(out_weight_grad.astype(jnp.bfloat16), "wide", axis=1, tiled=True).astype(
            out_weight_grad.dtype
        ),
        lax.all_gather(inner_weight_grad.astype(jnp.bfloat16), "wide", axis=1, tiled=True).astype(
            inner_weight_grad.dtype
        ),
        lax.all_gather(outer_weight_grad.astype(jnp.bfloat16), "wide", axis=1, tiled=True).astype(
            outer_weight_grad.dtype
        ),
    )
    (
        attn_gain_grad,
        attn_shift_grad,
        content_bias_grad,
        position_bias_grad,
        out_bias_grad,
        mlp_gain_grad,
        mlp_shift_grad,
        inner_bias_grad,
        outer_bias_grad,
    ) = lax.psum(
        (
            attn_gain_grad,
            attn_shift_grad,
            content_bias_grad,
            position_bias_grad,
            out_bias_grad,
            mlp_gain_grad,
            mlp_shift_grad,
            inner_bias_grad,
            outer_bias_grad,
        ),
        "wide",
    )
    return (
        layer_out,
        tokens_grad,
        attn_gain_grad,
        attn_shift_grad,
        query_weight_grad,
        key_weight_grad,
        value_weight_grad,
        relative_weight_grad,
        content_bias_grad,
        position_bias_grad,
        out_weight_grad,
        out_bias_grad,
        mlp_gain_grad,
        mlp_shift_grad,
        inner_weight_grad,
        inner_bias_grad,
        outer_weight_grad,
        outer_bias_grad,
    )


def solution(mesh):
    in_specs = (
        P(("wide", "narrow"), None, None),
        P(("wide", "narrow"), None, None),
        P(("wide", "narrow"), None),
        P("narrow"),
        P("narrow"),
        P("narrow", None),
        P("narrow", None),
        P("narrow", None),
        P("narrow", None),
        P("narrow"),
        P("narrow"),
        P("narrow", None),
        P("narrow"),
        P("narrow"),
        P("narrow"),
        P("narrow", None),
        P("narrow"),
        P("narrow", None),
        P("narrow"),
    )
    out_specs = (
        P(("wide", "narrow"), None, None),
        P(("wide", "narrow"), None, None),
        P("narrow"),
        P("narrow"),
        P("narrow", None),
        P("narrow", None),
        P("narrow", None),
        P("narrow", None),
        P("narrow"),
        P("narrow"),
        P("narrow", None),
        P("narrow"),
        P("narrow"),
        P("narrow"),
        P("narrow", None),
        P("narrow"),
        P("narrow", None),
        P("narrow"),
    )
    return jax.shard_map(
        per_device, mesh=mesh, in_specs=in_specs, out_specs=out_specs, check_vma=False
    )
```

profile of v0, /device:TPU:0, one launch (start us, length us, event | category | flops | bytes accessed | tf_op | source)
XLA Modules:
  0.0 1326.0 jit_solution(15802142088823861450)
XLA Ops:
  11.4 12.7 all-gather.2
  31.7 12.1 all-gather.6
  68.5 12.1 all-gather.1
  92.6 13.3 %all-gather.7 = bf16[4,1,768]{2,1,0:T(2,128)(2,1)S(1)} all-gather(bf16[1,1,768]{2,1,0:T(2,128)(2,1)S(1)} %reshape.391), channel_id=1, replica_groups=mesh['wide'=8,'narrow'=4] {'narrow'}, dimensions={0}, use_global_device_ids=true | all-gather | bytes 7680 | tf_op jit(solution)/shard_map/all_gather | solution.py:115
  106.5 16.2 %all_gather.83 = bf16[192,512]{1,0:T(8,128)(2,1)S(1)} all-gather(bf16[48,512]{1,0:T(8,128)(2,1)S(1)} %copy-done.23), channel_id=1, replica_groups=mesh['wide'=8,'narrow'=4] {'narrow'}, dimensions={0}, use_global_device_ids=true | all-gather | bytes 245760 | tf_op jit(solution)/shard_map/all_gather | solution.py:105
  188.5 79.7 %all-gather.27.cloned.1.call-done = bf16[1536,1536]{1,0:T(8,128)(2,1)} async-done(((bf16[384,1536]{1,0:T(8,128)(2,1)}), bf16[1536,1536]{1,0:T(8,128)(2,1)}) %all-gather.27.cloned.1.call-update) | async-done | bytes 4718608 | tf_op jit(solution)/shard_map/all_gather | solution.py:108
  274.9 160.1 %all-gather.29.cloned.1.call-done = bf16[1536,3072]{1,0:T(8,128)(2,1)} async-done(((bf16[384,3072]{1,0:T(8,128)(2,1)}), bf16[1536,3072]{1,0:T(8,128)(2,1)}) %all-gather.29.cloned.1.call-update) | async-done | bytes 9437200 | tf_op jit(solution)/shard_map/all_gather | solution.py:114
  434.9 14.2 %multiply_convert_fusion = (bf16[256,3072]{1,0:T(8,128)(2,1)}, f32[256,3072]{1,0:T(8,128)}, f32[256,3072]{1,0:T(8,128)}) fusion(f32[3072]{0:T(1024)} %bitcast.233, bf16[1536,3072]{1,0:T(8,128)(2,1)} %all-gather.29.cloned.1.call-done, f32[256,1536]{1,0:T(8,128)} %copy-done.1, f32[1536]{0:T(1024)S(1)} %reshape.403, f32[1536]{0:T(1024)S(1)} %reshape.402, ...), kind=kOutput, calls=%fused_computation.8 | convolution fusion | flops 2469789696 | bytes 18900992 | tf_op jit(solution)/shard_map/dot_general | solution.py:175
  449.1 152.2 %all-gather.31.cloned.1.call-done = bf16[3072,1536]{1,0:T(8,128)(2,1)} async-done(((bf16[768,1536]{1,0:T(8,128)(2,1)}), bf16[3072,1536]{1,0:T(8,128)(2,1)}) %all-gather.31.cloned.1.call-update) | async-done | bytes 9437200 | tf_op jit(solution)/shard_map/all_gather | solution.py:116
  646.4 12.4 copy.151
  697.3 45.7 %reduce-scatter.35.cloned.1.call-done = bf16[1536,192]{0,1:T(8,128)(2,1)} async-done(((bf16[1536,1536]{0,1:T(8,128)(2,1)}), bf16[1536,192]{0,1:T(8,128)(2,1)}) %reduce-scatter.35.cloned.1.call-update) | async-done | bytes 589840 | tf_op jit(solution)/shard_map/reduce_scatter | solution.py:326
  745.3 77.7 %reduce-scatter.53.cloned.1.call-done = bf16[384,1536]{1,0:T(8,128)(2,1)} async-done(((bf16[3072,1536]{1,0:T(8,128)(2,1)}), bf16[384,1536]{1,0:T(8,128)(2,1)}) %reduce-scatter.53.cloned.1.call-update) | async-done | bytes 1179664
  825.5 77.4 %reduce-scatter.39.cloned.1.call-done = bf16[3072,192]{0,1:T(8,128)(2,1)} async-done(((bf16[3072,1536]{0,1:T(8,128)(2,1)}), bf16[3072,192]{0,1:T(8,128)(2,1)}) %reduce-scatter.39.cloned.1.call-update) | async-done | bytes 1179664 | tf_op jit(solution)/shard_map/reduce_scatter | solution.py:332
  903.0 36.6 %reduce-scatter.33.cloned.1.call-done = bf16[192,64]{0,1:T(8,128)(2,1)} async-done(((bf16[192,512]{0,1:T(8,128)(2,1)}), bf16[192,64]{0,1:T(8,128)(2,1)}) %reduce-scatter.33.cloned.1.call-update) | async-done | bytes 24592 | tf_op jit(solution)/shard_map/reduce_scatter | solution.py:323
  941.2 40.4 %reduce-scatter.29.cloned.1.call-done = bf16[1536,64]{0,1:T(8,128)(2,1)} async-done(((bf16[1536,512]{0,1:T(8,128)(2,1)}), bf16[1536,64]{0,1:T(8,128)(2,1)}) %reduce-scatter.29.cloned.1.call-update) | async-done | bytes 196624 | tf_op jit(solution)/shard_map/reduce_scatter | solution.py:317
  983.5 40.8 %reduce-scatter.27.cloned.1.call-done = bf16[1536,64]{0,1:T(8,128)(2,1)} async-done(((bf16[1536,512]{0,1:T(8,128)(2,1)}), bf16[1536,64]{0,1:T(8,128)(2,1)}) %reduce-scatter.27.cloned.1.call-update) | async-done | bytes 196624 | tf_op jit(solution)/shard_map/reduce_scatter | solution.py:314
  1026.2 24.2 %reduce-scatter.47.cloned.1.call-done = bf16[384,192]{1,0:T(8,128)(2,1)} async-done(((bf16[1536,192]{1,0:T(8,128)(2,1)}), bf16[384,192]{1,0:T(8,128)(2,1)}) %reduce-scatter.47.cloned.1.call-update) | async-done | bytes 147472
  1052.2 23.6 %reduce-scatter.51.cloned.1.call-done = bf16[384,192]{1,0:T(8,128)(2,1)} async-done(((bf16[1536,192]{1,0:T(8,128)(2,1)}), bf16[384,192]{1,0:T(8,128)(2,1)}) %reduce-scatter.51.cloned.1.call-update) | async-done | bytes 147472
  1077.6 29.6 %reduce-scatter.37.cloned.1.call-done = bf16[384,384]{1,0:T(8,128)(2,1)} async-done(((bf16[1536,384]{1,0:T(8,128)(2,1)}), bf16[384,384]{1,0:T(8,128)(2,1)}) %reduce-scatter.37.cloned.1.call-update) | async-done | bytes 294928 | tf_op jit(solution)/shard_map/reduce_scatter | solution.py:369
  1142.2 16.9 %all-reduce.13 = (bf16[1536]{0:T(1024)(128)(2,1)S(1)}, bf16[1536]{0:T(1024)(128)(2,1)S(1)}, bf16[512]{0:T(512)(128)(2,1)S(1)}, bf16[512]{0:T(512)(128)(2,1)S(1)}...) all-reduce(bf16[1536]{0:T(1024)(128)(2,1)S(1)} %get-tuple-element.1, ...), channel_id=2, replica_groups=mesh['wide'=8,'narrow'=4] {'narrow'}, use_global_device_ids=true, to_apply=%region_12.15.clone | all-reduce | flops 13312 | bytes 53248
  1159.8 23.3 %all-reduce.12 = (f32[384]{0:T(512)}, f32[384]{0:T(512)}, f32[128]{0:T(128)}, f32[128]{0:T(128)}, f32[384]{0:T(512)}, /*index=5*/f32[384]{0:T(512)}, f32[384]{0:T(512)}, f32[768]{0:T(1024)}, f32[384]{0:T(512)}) all-reduce(f32[384]{0:T(512)S(1)} %dynamic-slice_convert_fusion.6, ...), channel_id=1, replica_groups=mesh['wide'=8,'narrow'=4] {'wide'}, use_global_device_ids=true, to_apply=%region_13.16 | all-reduce | flops 3328 | bytes 26624 | tf_op jit(solution)/shard_map/psum | solution.py:444
  1230.3 22.0 %all-gather.35.cloned.1.call-done = bf16[384,1536]{0,1:T(8,128)(2,1)} async-done(((bf16[384,192]{0,1:T(8,128)(2,1)}), bf16[384,1536]{0,1:T(8,128)(2,1)}) %all-gather.35.cloned.1.call-update) | async-done | bytes 1179664 | tf_op jit(solution)/shard_map/all_gather | solution.py:424
  1255.0 28.6 %all-gather.37.cloned.1.call-done = bf16[384,3072]{1,0:T(8,128)(2,1)} async-done(((bf16[384,384]{1,0:T(8,128)(2,1)}), bf16[384,3072]{1,0:T(8,128)(2,1)}) %all-gather.37.cloned.1.call-update) | async-done | bytes 2359312 | tf_op jit(solution)/shard_map/all_gather | solution.py:427
  1288.0 26.4 %all-gather.39.cloned.1.call-done = bf16[768,1536]{0,1:T(8,128)(2,1)} async-done(((bf16[768,192]{0,1:T(8,128)(2,1)}), bf16[768,1536]{0,1:T(8,128)(2,1)}) %all-gather.39.cloned.1.call-update) | async-done | bytes 2359312 | tf_op jit(solution)/shard_map/all_gather | solution.py:430
  (321 shorter events, 310.4 us)
Async XLA Ops:
  7.2 118.2 %all-gather.25.cloned.1.call-start = ((), (), s32[]{:S(2)}) async-start(), calls=%async_computation.16 | async-start | bytes 1966080 | tf_op jit(solution)/shard_map/all_gather | solution.py:103
  7.9 120.3 %all-gather.23.cloned.1.call-start = ((), (), s32[]{:S(2)}) async-start(), calls=%async_computation.15 | async-start | bytes 1966080 | tf_op jit(solution)/shard_map/all_gather | solution.py:102
  8.7 170.2 %all-gather.21.cloned.1.call-start = ((), (), s32[]{:S(2)}) async-start(), calls=%async_computation.14 | async-start | bytes 5898240 | tf_op jit(solution)/shard_map/all_gather | solution.py:104
  9.4 258.8 %all-gather.27.cloned.1.call-start = ((), (), s32[]{:S(2)}) async-start(), calls=%async_computation.17 | async-start | bytes 5898240 | tf_op jit(solution)/shard_map/all_gather | solution.py:108
  10.0 424.9 %all-gather.29.cloned.1.call-start = ((), (), s32[]{:S(2)}) async-start(), calls=%async_computation.18 | async-start | bytes 11796480 | tf_op jit(solution)/shard_map/all_gather | solution.py:114
  10.7 590.7 %all-gather.31.cloned.1.call-start = ((), (), s32[]{:S(2)}) async-start(), calls=%async_computation.19 | async-start | bytes 11796480 | tf_op jit(solution)/shard_map/all_gather | solution.py:116
  11.2 683.5 %reduce-scatter.31.cloned.1.call-start = ((), (), s32[]{:S(2)}) async-start(), calls=%async_computation.22 | async-start | bytes 5308416 | tf_op jit(solution)/shard_map/reduce_scatter | solution.py:320
  632.5 110.5 %reduce-scatter.35.cloned.1.call-start = ((), (), s32[]{:S(2)}) async-start(), calls=%async_computation.25 | async-start | bytes 5308416 | tf_op jit(solution)/shard_map/reduce_scatter | solution.py:326
  637.6 185.5 %reduce-scatter.53.cloned.1.call-start = ((), (), s32[]{:S(2)}) async-start(), calls=%async_computation.37 | async-start | bytes 10616832
  658.8 244.1 %reduce-scatter.39.cloned.1.call-start = ((), (), s32[]{:S(2)}) async-start(), calls=%async_computation.29 | async-start | bytes 10616832 | tf_op jit(solution)/shard_map/reduce_scatter | solution.py:332
  667.7 271.9 %reduce-scatter.33.cloned.1.call-start = ((), (), s32[]{:S(2)}) async-start(), calls=%async_computation.24 | async-start | bytes 294912 | tf_op jit(solution)/shard_map/reduce_scatter | solution.py:323
  686.8 294.7 %reduce-scatter.29.cloned.1.call-start = ((), (), s32[]{:S(2)}) async-start(), calls=%async_computation.21 | async-start | bytes 1769472 | tf_op jit(solution)/shard_map/reduce_scatter | solution.py:317
  691.2 333.0 %reduce-scatter.27.cloned.1.call-start = ((), (), s32[]{:S(2)}) async-start(), calls=%async_computation.20 | async-start | bytes 1769472 | tf_op jit(solution)/shard_map/reduce_scatter | solution.py:314
  694.7 355.7 %reduce-scatter.47.cloned.1.call-start = ((), (), s32[]{:S(2)}) async-start(), calls=%async_computation.34 | async-start | bytes 983040
  697.0 378.8 %reduce-scatter.51.cloned.1.call-start = ((), (), s32[]{:S(2)}) async-start(), calls=%async_computation.36 | async-start | bytes 983040
  745.3 361.9 %reduce-scatter.37.cloned.1.call-start = ((), (), s32[]{:S(2)}) async-start(), calls=%async_computation.27 | async-start | bytes 1474560 | tf_op jit(solution)/shard_map/reduce_scatter | solution.py:369
  825.4 311.9 %reduce-scatter.41.cloned.1.call-start = ((), (), s32[]{:S(2)}) async-start(), calls=%async_computation.30 | async-start | bytes 1474560 | tf_op jit(solution)/shard_map/reduce_scatter | solution.py:372
  903.0 290.6 %reduce-scatter.49.cloned.1.call-start = ((), (), s32[]{:S(2)}) async-start(), calls=%async_computation.35 | async-start | bytes 61440
  941.1 263.4 %reduce-scatter.45.cloned.1.call-start = ((), (), s32[]{:S(2)}) async-start(), calls=%async_computation.33 | async-start | bytes 491520
  983.4 232.1 %reduce-scatter.43.cloned.1.call-start = ((), (), s32[]{:S(2)}) async-start(), calls=%async_computation.32 | async-start | bytes 491520
  1026.1 201.5 %all-gather.33.cloned.1.call-start = ((), (), s32[]{:S(2)}) async-start(), calls=%async_computation.23 | async-start | bytes 1327104 | tf_op jit(solution)/shard_map/all_gather | solution.py:418
  1052.1 200.2 %all-gather.35.cloned.1.call-start = ((), (), s32[]{:S(2)}) async-start(), calls=%async_computation.26 | async-start | bytes 1327104 | tf_op jit(solution)/shard_map/all_gather | solution.py:424
  1077.5 206.1 %all-gather.37.cloned.1.call-start = ((), (), s32[]{:S(2)}) async-start(), calls=%async_computation.28 | async-start | bytes 2654208 | tf_op jit(solution)/shard_map/all_gather | solution.py:427
  1107.2 207.2 %all-gather.39.cloned.1.call-start = ((), (), s32[]{:S(2)}) async-start(), calls=%async_computation.31 | async-start | bytes 2654208 | tf_op jit(solution)/shard_map/all_gather | solution.py:430
  (63 other events, 946.1 us)
Sparse Core Ops, SparseCore 0:
  9.6 39.9 all-gather.24
  51.2 36.2 all-gather.22
  89.0 89.8 all-gather.20
  180.3 87.8 all-gather.26
  269.6 165.2 all-gather.28
  436.3 164.9 all-gather.30
  632.6 52.0 reduce-scatter.30
  689.1 53.8 reduce-scatter.34
  746.5 76.4 reduce-scatter.52
  826.4 76.4 reduce-scatter.38
  906.0 33.5 reduce-scatter.32
  943.1 38.4 reduce-scatter.28
  985.8 38.4 reduce-scatter.26
  1027.1 23.2 reduce-scatter.46
  1053.2 22.5 reduce-scatter.50
  1078.7 28.4 reduce-scatter.36
  1109.4 27.9 reduce-scatter.40
  1140.1 17.7 reduce-scatter.48
  1160.2 18.7 reduce-scatter.44
  1181.7 18.8 reduce-scatter.42
  1202.5 23.4 all-gather.32
  1227.9 24.3 all-gather.34
  1254.2 29.3 all-gather.36
  1285.3 29.0 all-gather.38
where the time goes:
time: 1330 us
  waiting for transfers between devices  889 us (67%)
  blocking collectives  190 us (14%)
  local copies, waits for them, and re-layouts  106 us (8%)
  matrix products  106 us (8%)
  between operations  17.5 us (1%)
  other arithmetic  15.8 us (1%)
    all_gather x1, waiting for transfers between devices, per_device(): lax.all_gather(inner_weight, 'narrow', axis=0, tiled=True)  160 us
    all_gather x1, waiting for transfers between devices, per_device(): lax.all_gather(outer_weight, 'narrow', axis=0, tiled=True)  152 us
    unnamed x30, waiting for transfers between devices  130 us
    all_gather x1, waiting for transfers between devices, per_device(): lax.all_gather(out_weight, 'narrow', axis=0, tiled=True)  79.7 us
    reduce_scatter x1, waiting for transfers between devices, per_device(): lax.psum_scatter(outer_weight_grad.astype(jnp.bfloat16), 'wide', scatter_...  77.4 us
    unnamed x155, local copies, waits for them, and re-layouts  67 us
    reduce_scatter x1, waiting for transfers between devices, per_device(): lax.psum_scatter(out_weight_grad.astype(jnp.bfloat16), 'wide', scatter_di...  45.7 us
    reduce_scatter x1, waiting for transfers between devices, per_device(): lax.psum_scatter(query_weight_grad.astype(jnp.bfloat16), 'wide', scatter_...  40.8 us
  transfers between devices with their start and end apart: 24, of which 17 were waited for; matrix products, arithmetic and copies ran while one was open for 14% of the time, Pallas kernels for 0%

commit v1 on v0

--- a/solution.py
+++ b/solution.py
@@ -1,8 +1,11 @@
 import math
+import types
 
 import jax
 import jax.numpy as jnp
 from jax import lax
+from jax.experimental import pallas as pl
+from jax.experimental.pallas import tpu as pltpu
 from jax.sharding import PartitionSpec as P
 
 H = 8
@@ -60,7 +63,30 @@
     return jnp.sum(values.astype(jnp.float32), axis=0)
 
 
-def per_device(
+WIDE = "wide"
+DEPTH = "narrow"
+
+
+def spread_rows(shard):
+    return lax.all_gather(shard, DEPTH, axis=0, tiled=True)
+
+
+def sum_columns(part):
+    low = part.astype(jnp.bfloat16)
+    return lax.psum_scatter(low, WIDE, scatter_dimension=1, tiled=True).astype(jnp.float32)
+
+
+def sum_rows(part):
+    low = part.astype(jnp.bfloat16)
+    return lax.psum_scatter(low, DEPTH, scatter_dimension=0, tiled=True).astype(jnp.float32)
+
+
+def spread_columns(part):
+    low = part.astype(jnp.bfloat16)
+    return lax.all_gather(low, WIDE, axis=1, tiled=True).astype(jnp.float32)
+
+
+def per_device_generic(
     tokens,
     cotangent,
     thresholds,
@@ -97,24 +123,24 @@
         exit_full,
         exit_bias,
     ) = (
-        lax.all_gather(attn_norm_gain, "narrow", axis=0, tiled=True),
-        lax.all_gather(attn_norm_shift, "narrow", axis=0, tiled=True),
-        lax.all_gather(query_weight, "narrow", axis=0, tiled=True),
-        lax.all_gather(key_weight, "narrow", axis=0, tiled=True),
-        lax.all_gather(value_weight, "narrow", axis=0, tiled=True),
-        lax.all_gather(relative_weight, "narrow", axis=0, tiled=True),
-        lax.all_gather(content_bias, "narrow", axis=0, tiled=True),
-        lax.all_gather(position_bias, "narrow", axis=0, tiled=True),
-        lax.all_gather(out_weight, "narrow", axis=0, tiled=True),
-        lax.all_gather(out_bias, "narrow", axis=0, tiled=True),
+        spread_rows(attn_norm_gain),
+        spread_rows(attn_norm_shift),
+        spread_rows(query_weight),
+        spread_rows(key_weight),
+        spread_rows(value_weight),
+        spread_rows(relative_weight),
+        spread_rows(content_bias),
+        spread_rows(position_bias),
+        spread_rows(out_weight),
+        spread_rows(out_bias),
     )
     mlp_gain, mlp_shift, inner_full, inner_offset, outer_full, outer_offset = (
-        lax.all_gather(mlp_norm_gain, "narrow", axis=0, tiled=True),
-        lax.all_gather(mlp_norm_shift, "narrow", axis=0, tiled=True),
-        lax.all_gather(inner_weight, "narrow", axis=0, tiled=True),
-        lax.all_gather(inner_bias, "narrow", axis=0, tiled=True),
-        lax.all_gather(outer_weight, "narrow", axis=0, tiled=True),
-        lax.all_gather(outer_bias, "narrow", axis=0, tiled=True),
+        spread_rows(mlp_norm_gain),
+        spread_rows(mlp_norm_shift),
+        spread_rows(inner_weight),
+        spread_rows(inner_bias),
+        spread_rows(outer_weight),
+        spread_rows(outer_bias),
     )
     flat_tokens = tokens.reshape(row_count, model_width).astype(jnp.float32)
     attn_gain_f = attn_gain.astype(jnp.float32)
@@ -187,12 +213,12 @@
         cotangent.reshape(row_count, model_width).astype(jnp.float32), -clip_limit, clip_limit
     )
     mlp_gain, mlp_shift, inner_full, inner_offset, outer_full, outer_offset = (
-        lax.all_gather(mlp_norm_gain, "narrow", axis=0, tiled=True),
-        lax.all_gather(mlp_norm_shift, "narrow", axis=0, tiled=True),
-        lax.all_gather(inner_weight, "narrow", axis=0, tiled=True),
-        lax.all_gather(inner_bias, "narrow", axis=0, tiled=True),
-        lax.all_gather(outer_weight, "narrow", axis=0, tiled=True),
-        lax.all_gather(outer_bias, "narrow", axis=0, tiled=True),
+        spread_rows(mlp_norm_gain),
+        spread_rows(mlp_norm_shift),
+        spread_rows(inner_weight),
+        spread_rows(inner_bias),
+        spread_rows(outer_weight),
+        spread_rows(outer_bias),
     )
     mlp_gain_f = mlp_gain.astype(jnp.float32)
     outer_delta = clipped.astype(jnp.bfloat16)
@@ -225,16 +251,16 @@
         exit_full,
         exit_bias,
     ) = (
-        lax.all_gather(attn_norm_gain, "narrow", axis=0, tiled=True),
-        lax.all_gather(attn_norm_shift, "narrow", axis=0, tiled=True),
-        lax.all_gather(query_weight, "narrow", axis=0, tiled=True),
-        lax.all_gather(key_weight, "narrow", axis=0, tiled=True),
-        lax.all_gather(value_weight, "narrow", axis=0, tiled=True),
-        lax.all_gather(relative_weight, "narrow", axis=0, tiled=True),
-        lax.all_gather(content_bias, "narrow", axis=0, tiled=True),
-        lax.all_gather(position_bias, "narrow", axis=0, tiled=True),
-        lax.all_gather(out_weight, "narrow", axis=0, tiled=True),
-        lax.all_gather(out_bias, "narrow", axis=0, tiled=True),
+        spread_rows(attn_norm_gain),
+        spread_rows(attn_norm_shift),
+        spread_rows(query_weight),
+        spread_rows(key_weight),
+        spread_rows(value_weight),
+        spread_rows(relative_weight),
+        spread_rows(content_bias),
+        spread_rows(position_bias),
+        spread_rows(out_weight),
+        spread_rows(out_bias),
     )
     attn_gain_f = attn_gain.astype(jnp.float32)
     branch_delta = hidden_delta.astype(jnp.bfloat16)
@@ -311,27 +337,13 @@
         inner_weight_grad,
         outer_weight_grad,
     ) = (
-        lax.psum_scatter(
-            query_weight_grad.astype(jnp.bfloat16), "wide", scatter_dimension=1, tiled=True
-        ).astype(jnp.float32),
-        lax.psum_scatter(
-            key_weight_grad.astype(jnp.bfloat16), "wide", scatter_dimension=1, tiled=True
-        ).astype(jnp.float32),
-        lax.psum_scatter(
-            value_weight_grad.astype(jnp.bfloat16), "wide", scatter_dimension=1, tiled=True
-        ).astype(jnp.float32),
-        lax.psum_scatter(
-            relative_weight_grad.astype(jnp.bfloat16), "wide", scatter_dimension=1, tiled=True
-        ).astype(jnp.float32),
-        lax.psum_scatter(
-            out_weight_grad.astype(jnp.bfloat16), "wide", scatter_dimension=1, tiled=True
-        ).astype(jnp.float32),
-        lax.psum_scatter(
-            inner_weight_grad.astype(jnp.bfloat16), "wide", scatter_dimension=1, tiled=True
-        ).astype(jnp.float32),
-        lax.psum_scatter(
-            outer_weight_grad.astype(jnp.bfloat16), "wide", scatter_dimension=1, tiled=True
-        ).astype(jnp.float32),
+        sum_columns(query_weight_grad),
+        sum_columns(key_weight_grad),
+        sum_columns(value_weight_grad),
+        sum_columns(relative_weight_grad),
+        sum_columns(out_weight_grad),
+        sum_columns(inner_weight_grad),
+        sum_columns(outer_weight_grad),
     )
     (
         query_weight_grad,
@@ -351,54 +363,22 @@
         inner_bias_grad,
         outer_bias_grad,
     ) = (
-        lax.psum_scatter(
-            query_weight_grad.astype(jnp.bfloat16), "narrow", scatter_dimension=0, tiled=True
-        ).astype(jnp.float32),
-        lax.psum_scatter(
-            key_weight_grad.astype(jnp.bfloat16), "narrow", scatter_dimension=0, tiled=True
-        ).astype(jnp.float32),
-        lax.psum_scatter(
-            value_weight_grad.astype(jnp.bfloat16), "narrow", scatter_dimension=0, tiled=True
-        ).astype(jnp.float32),
-        lax.psum_scatter(
-            relative_weight_grad.astype(jnp.bfloat16), "narrow", scatter_dimension=0, tiled=True
-        ).astype(jnp.float32),
-        lax.psum_scatter(
-            out_weight_grad.astype(jnp.bfloat16), "narrow", scatter_dimension=0, tiled=True
-        ).astype(jnp.float32),
-        lax.psum_scatter(
-            inner_weight_grad.astype(jnp.bfloat16), "narrow", scatter_dimension=0, tiled=True
-        ).astype(jnp.float32),
-        lax.psum_scatter(
-            outer_weight_grad.astype(jnp.bfloat16), "narrow", scatter_dimension=0, tiled=True
-        ).astype(jnp.float32),
-        lax.psum_scatter(
-            attn_gain_grad.astype(jnp.bfloat16), "narrow", scatter_dimension=0, tiled=True
-        ).astype(jnp.float32),
-        lax.psum_scatter(
-            attn_shift_grad.astype(jnp.bfloat16), "narrow", scatter_dimension=0, tiled=True
-        ).astype(jnp.float32),
-        lax.psum_scatter(
-            content_bias_grad.astype(jnp.bfloat16), "narrow", scatter_dimension=0, tiled=True
-        ).astype(jnp.float32),
-        lax.psum_scatter(
-            position_bias_grad.astype(jnp.bfloat16), "narrow", scatter_dimension=0, tiled=True
-        ).astype(jnp.float32),
-        lax.psum_scatter(
-            out_bias_grad.astype(jnp.bfloat16), "narrow", scatter_dimension=0, tiled=True
-        ).astype(jnp.float32),
-        lax.psum_scatter(
-            mlp_gain_grad.astype(jnp.bfloat16), "narrow", scatter_dimension=0, tiled=True
-        ).astype(jnp.float32),
-        lax.psum_scatter(
-            mlp_shift_grad.astype(jnp.bfloat16), "narrow", scatter_dimension=0, tiled=True
-        ).astype(jnp.float32),
-        lax.psum_scatter(
-            inner_bias_grad.astype(jnp.bfloat16), "narrow", scatter_dimension=0, tiled=True
-        ).astype(jnp.float32),
-        lax.psum_scatter(
-            outer_bias_grad.astype(jnp.bfloat16), "narrow", scatter_dimension=0, tiled=True
-        ).astype(jnp.float32),
+        sum_rows(query_weight_grad),
+        sum_rows(key_weight_grad),
+        sum_rows(value_weight_grad),
+        sum_rows(relative_weight_grad),
+        sum_rows(out_weight_grad),
+        sum_rows(inner_weight_grad),
+        sum_rows(outer_weight_grad),
+        sum_rows(attn_gain_grad),
+        sum_rows(attn_shift_grad),
+        sum_rows(content_bias_grad),
+        sum_rows(position_bias_grad),
+        sum_rows(out_bias_grad),
+        sum_rows(mlp_gain_grad),
+        sum_rows(mlp_shift_grad),
+        sum_rows(inner_bias_grad),
+        sum_rows(outer_bias_grad),
     )
     (
         query_weight_grad,
@@ -409,27 +389,13 @@
         inner_weight_grad,
         outer_weight_grad,
     ) = (
-        lax.all_gather(query_weight_grad.astype(jnp.bfloat16), "wide", axis=1, tiled=True).astype(
-            query_weight_grad.dtype
-        ),
-        lax.all_gather(key_weight_grad.astype(jnp.bfloat16), "wide", axis=1, tiled=True).astype(
-            key_weight_grad.dtype
-        ),
-        lax.all_gather(value_weight_grad.astype(jnp.bfloat16), "wide", axis=1, tiled=True).astype(
-            value_weight_grad.dtype
-        ),
-        lax.all_gather(
-            relative_weight_grad.astype(jnp.bfloat16), "wide", axis=1, tiled=True
-        ).astype(relative_weight_grad.dtype),
-        lax.all_gather(out_weight_grad.astype(jnp.bfloat16), "wide", axis=1, tiled=True).astype(
-            out_weight_grad.dtype
-        ),
-        lax.all_gather(inner_weight_grad.astype(jnp.bfloat16), "wide", axis=1, tiled=True).astype(
-            inner_weight_grad.dtype
-        ),
-        lax.all_gather(outer_weight_grad.astype(jnp.bfloat16), "wide", axis=1, tiled=True).astype(
-            outer_weight_grad.dtype
-        ),
+        spread_columns(query_weight_grad),
+        spread_columns(key_weight_grad),
+        spread_columns(value_weight_grad),
+        spread_columns(relative_weight_grad),
+        spread_columns(out_weight_grad),
+        spread_columns(inner_weight_grad),
+        spread_columns(outer_weight_grad),
     )
     (
         attn_gain_grad,
@@ -453,7 +419,7 @@
             inner_bias_grad,
             outer_bias_grad,
         ),
-        "wide",
+        WIDE,
     )
     return (
         layer_out,
@@ -477,48 +443,795 @@
     )
 
 
+MESH = pl.DeviceIdType.MESH
+NARROW = 4
+
+
+def position():
+    w = lax.axis_index(WIDE)
+    z = lax.axis_index(DEPTH)
+    c = lax.rem(w, 2)
+    p = lax.div(w, 2)
+    x = lax.rem(p, 2)
+    y = lax.div(p, 2)
+    chip = (lambda q: q * 2 + c)
+    return types.SimpleNamespace(
+        w=w,
+        z=z,
+        c=c,
+        p=p,
+        x=x,
+        y=y,
+        px=p + 1 - 2 * x,
+        py=p + 2 - 4 * y,
+        pd=3 - p,
+        sib=(w + 1 - 2 * c, z),
+        xn=(chip(p + 1 - 2 * x), z),
+        yn=(chip(p + 2 - 4 * y), z),
+    )
+
+
+def meet(partners):
+    barrier = pltpu.get_barrier_semaphore()
+    for partner in partners:
+        pl.semaphore_signal(barrier, inc=1, device_id=partner, device_id_type=MESH)
+    pl.semaphore_wait(barrier, len(partners))
+
+
+def remote(src, dst, send, recv, target):
+    return pltpu.make_async_remote_copy(
+        src_ref=src,
+        dst_ref=dst,
+        send_sem=send,
+        recv_sem=recv,
+        device_id=target,
+        device_id_type=MESH,
+    )
+
+
+def gather_kernel(count, *refs):
+    shards = refs[:count]
+    rel, small = refs[count : count + 2]
+    fulls = refs[count + 2 : 2 * count + 2]
+    rel_full, small_full = refs[2 * count + 2 : 2 * count + 4]
+    stage = refs[2 * count + 4 : 3 * count + 6]
+    zr, xr, yr, fxr, fyr, sr, snd, own, misc_s, misc_r = refs[3 * count + 6 :]
+    at = position()
+    w, z, c, p = at.w, at.z, at.c, at.p
+    me = (w, z)
+    depth = [(w, lax.rem(z + d, NARROW)) for d in range(1, NARROW)]
+    meet([at.sib, at.xn, at.yn] + depth)
+
+    def block(m, zz, pp, half=None):
+        full = fulls[m]
+        rows, cols = full.shape[1] // 4, full.shape[2] // 2
+        start = pp * rows
+        if half is not None:
+            rows = rows // 2
+            start = start + half * rows
+        return full.at[
+            zz, pl.ds(pl.multiple_of(start, 8), rows), pl.ds(pl.multiple_of(c * cols, 128), cols)
+        ]
+
+    def send(m, ref, recv, target):
+        remote(ref, ref, snd.at[m], recv, target).start()
+
+    for d in (1, 3, 2):
+        for k, (src, dst) in enumerate(((rel, rel_full), (small, small_full))):
+            remote(src, dst.at[z], misc_s.at[k], misc_r.at[k], depth[d - 1]).start()
+    for m in range(count):
+        shard = shards[m]
+        rows, cols = shard.shape[0] // 4, shard.shape[1] // 2
+        piece = shard.at[
+            pl.ds(pl.multiple_of(p * rows, 8), rows), pl.ds(pl.multiple_of(c * cols, 128), cols)
+        ]
+        for d in (1, 3, 2):
+            remote(piece, block(m, z, p), snd.at[m], zr.at[m, d - 1], depth[d - 1]).start()
+    local = [
+        (pltpu.make_async_copy(src, mid, own.at[k]), pltpu.make_async_copy(mid, dst.at[z], own.at[k]))
+        for k, (src, mid, dst) in enumerate(
+            zip((*shards, rel, small), stage, (*fulls, rel_full, small_full))
+        )
+    ]
+    for first, _ in local:
+        first.start()
+    for first, second in local:
+        first.wait()
+        second.start()
+
+    def arrive(ref, recv):
+        remote(ref, ref, recv, recv, me).wait_recv()
+
+    def spread(m, d):
+        zz = lax.rem(z + NARROW - d, NARROW)
+        mine = block(m, zz, p)
+        arrive(mine, zr.at[m, d - 1])
+        send(m, mine, xr.at[m, d - 1], at.xn)
+        send(m, mine, yr.at[m, d - 1], at.yn)
+        send(m, mine, sr.at[m], at.sib)
+
+    def forward(m, d):
+        zz = lax.rem(z + NARROW - d, NARROW)
+        arrive(block(m, zz, at.px), xr.at[m, d - 1])
+        send(m, block(m, zz, at.px, 0), fxr.at[m, d - 1], at.yn)
+        send(m, block(m, zz, at.px), sr.at[m], at.sib)
+        arrive(block(m, zz, at.py), yr.at[m, d - 1])
+        send(m, block(m, zz, at.py, 1), fyr.at[m, d - 1], at.xn)
+        send(m, block(m, zz, at.py), sr.at[m], at.sib)
+
+    def finish(m, d):
+        zz = lax.rem(z + NARROW - d, NARROW)
+        arrive(block(m, zz, at.pd, 0), fxr.at[m, d - 1])
+        arrive(block(m, zz, at.pd, 1), fyr.at[m, d - 1])
+        send(m, block(m, zz, at.pd), sr.at[m], at.sib)
+
+    units = [(m, d) for m in range(count) for d in (1, 3, 2)]
+    total = len(units)
+    for u in range(total + 4):
+        if u < total:
+            spread(*units[u])
+        if 0 <= u - 2 < total:
+            forward(*units[u - 2])
+        if 0 <= u - 4 < total:
+            finish(*units[u - 4])
+    for m in range(count):
+        cols = fulls[m].shape[2] // 2
+        theirs = fulls[m].at[pl.ds(0, 3), :, pl.ds(0, cols)]
+        arrive(theirs, sr.at[m])
+        sent = fulls[m].at[pl.ds(0, 3)]
+        remote(sent, sent, snd.at[m], snd.at[m], me).wait_send()
+    for k, full in enumerate((rel_full, small_full)):
+        others = full.at[pl.ds(0, 3)]
+        arrive(others, misc_r.at[k])
+        remote(others, others, misc_s.at[k], misc_s.at[k], me).wait_send()
+    for _, second in local:
+        second.wait()
+
+
+HBM = pl.BlockSpec(memory_space=pltpu.HBM)
+DMA = pltpu.SemaphoreType.DMA
+
+
+def gather_weights(shards, rel, small):
+    count = len(shards)
+    outs = pl.pallas_call(
+        lambda *refs: gather_kernel(count, *refs),
+        out_shape=tuple(
+            jax.ShapeDtypeStruct((NARROW,) + a.shape, a.dtype) for a in (*shards, rel, small)
+        ),
+        in_specs=[HBM] * (count + 2),
+        out_specs=(HBM,) * (count + 2),
+        scratch_shapes=[pltpu.VMEM(a.shape, a.dtype) for a in (*shards, rel, small)]
+        + [
+            DMA((count, 3)),
+            DMA((count, 3)),
+            DMA((count, 3)),
+            DMA((count, 3)),
+            DMA((count, 3)),
+            DMA((count,)),
+            DMA((count,)),
+            DMA((count + 2,)),
+            DMA((2,)),
+            DMA((2,)),
+        ],
+        compiler_params=pltpu.CompilerParams(
+            collective_id=1, has_side_effects=True, vmem_limit_bytes=24 << 20
+        ),
+        name="gather_weights",
+    )(*shards, rel, small)
+    fulls = [a.reshape(a.shape[0] * a.shape[1], a.shape[2]) for a in outs[:count]]
+    return fulls, outs[count].reshape(-1, rel.shape[1]), outs[count + 1]
+
+
+def pair_kernel(lefts, rights, *refs):
+    n = lefts + rights
+    ins, outs, stage = refs[:n], refs[n : 2 * n], refs[2 * n : 3 * n]
+    snd, rcv, own = refs[3 * n :]
+    at = position()
+    c = at.c
+    meet([at.sib])
+    copies = []
+    for k in range(n):
+        src, dst = ins[k], outs[k]
+        if k < lefts:
+            mine, theirs = src, src
+        else:
+            cols = src.shape[1] // 2
+            mine = src.at[:, pl.ds(pl.multiple_of(c * cols, 128), cols)]
+            theirs = src.at[:, pl.ds(pl.multiple_of((1 - c) * cols, 128), cols)]
+        away = remote(theirs, dst.at[c], snd.at[k], rcv.at[k], at.sib)
+        away.start()
+        first = pltpu.make_async_copy(mine, stage[k], own.at[k])
+        first.start()
+        second = pltpu.make_async_copy(stage[k], dst.at[c], own.at[k])
+        copies.append((away, first, second))
+    for _, first, second in copies:
+        first.wait()
+        second.start()
+    for away, _, second in copies:
+        away.wait()
+        second.wait()
+
+
+def pair_exchange(lefts, rights):
+    n = len(lefts) + len(rights)
+    shapes = [(2,) + a.shape for a in lefts] + [(2, a.shape[0], a.shape[1] // 2) for a in rights]
+    outs = pl.pallas_call(
+        lambda *refs: pair_kernel(len(lefts), len(rights), *refs),
+        out_shape=tuple(jax.ShapeDtypeStruct(s, jnp.bfloat16) for s in shapes),
+        in_specs=[HBM] * n,
+        out_specs=(HBM,) * n,
+        scratch_shapes=[pltpu.VMEM(s[1:], jnp.bfloat16) for s in shapes]
+        + [DMA((n,)), DMA((n,)), DMA((n,))],
+        compiler_params=pltpu.CompilerParams(
+            collective_id=2, has_side_effects=True, vmem_limit_bytes=24 << 20
+        ),
+        name="pair_exchange",
+    )(*lefts, *rights)
+    outs = [a.reshape(-1, a.shape[-1]) for a in outs]
+    return outs[: len(lefts)], outs[len(lefts) :]
+
+
+def reduce_kernel(count, *refs):
+    grads = refs[:count]
+    extra = refs[count]
+    outs = refs[count + 1 : 2 * count + 1]
+    extra_out = refs[2 * count + 1]
+    rest = refs[2 * count + 2 :]
+    take = iter(rest)
+    keep = [next(take) for _ in range(count)]
+    got1 = [next(take) for _ in range(count)]
+    got2 = [next(take) for _ in range(count)]
+    got3 = [next(take) for _ in range(count)]
+    last = [next(take) for _ in range(count)]
+    extra_in, extra_keep, extra_got, extra_sum = (next(take) for _ in range(4))
+    (ld, s1, r1, s2, r2, s3, r3, s4, r4, lo, es, er, el) = take
+    at = position()
+    w, z, c, p, x, y = at.w, at.z, at.c, at.p, at.x, at.y
+    me = (w, z)
+    depth = [(w, lax.rem(z + d, NARROW)) for d in range(1, NARROW)]
+    meet([at.sib, at.xn, at.yn] + depth)
+
+    def half(m, h, mine):
+        g = grads[m]
+        if h == 0:
+            return g.at[:, :, x if mine else 1 - x, 0]
+        return g.at[:, y if mine else 1 - y, :, 1]
+
+    def stage1(m):
+        for h, target in ((0, at.xn), (1, at.yn)):
+            remote(half(m, h, False), got1[m].at[h], s1.at[m, h], r1.at[m, h], target).start()
+            pltpu.make_async_copy(half(m, h, True), keep[m].at[h], ld.at[m, h]).start()
+
+    def wait_local(ref, sem):
+        pltpu.make_async_copy(ref, ref, sem).wait()
+
+    def arrive(ref, recv):
+        remote(ref, ref, recv, recv, me).wait_recv()
+
+    def left(ref, sem):
+        remote(ref, ref, sem, sem, me).wait_send()
+
+    def stage2(m):
+        for h, target, mine in ((0, at.yn, y), (1, at.xn, x)):
+            arrive(got1[m].at[h], r1.at[m, h])
+            wait_local(keep[m].at[h], ld.at[m, h])
+
+            def add(k, _, h=h):
+                zz, o = lax.div(k, 2), lax.rem(k, 2)
+                total = keep[m][h, zz, o].astype(jnp.float32) + got1[m][h, zz, o].astype(
+                    jnp.float32
+                )
+                keep[m][h, zz, o] = total.astype(jnp.bfloat16)
+                return 0
+
+            lax.fori_loop(0, 8, add, 0)
+            remote(
+                keep[m].at[h, :, 1 - mine], got2[m].at[h], s2.at[m, h], r2.at[m, h], target
+            ).start()
+
+    def stage3(m):
+        for h, mine in ((0, y), (1, x)):
+            arrive(got2[m].at[h], r2.at[m, h])
+
+            def add(zz, _, h=h, mine=mine):
+                total = keep[m][h, zz, mine].astype(jnp.float32) + got2[m][h, zz].astype(
+                    jnp.float32
+                )
+                got2[m][h, zz] = total.astype(jnp.bfloat16)
+                return 0
+
+            lax.fori_loop(0, 4, add, 0)
+        for d in (1, 3, 2):
+            zz = lax.rem(z + d, NARROW)
+            remote(
+                got2[m].at[:, zz], got3[m].at[d - 1], s3.at[m, d - 1], r3.at[m, d - 1], depth[d - 1]
+            ).start()
+
+    def piece(m, pp, half=None):
+        out = outs[m]
+        rows, cols = out.shape[0] // 4, out.shape[1] // 2
+        start = pp * rows
+        if half is not None:
+            rows = rows // 2
+            start = start + half * rows
+        return out.at[
+            pl.ds(pl.multiple_of(start, 8), rows), pl.ds(pl.multiple_of(c * cols, 128), cols)
+        ]
+
+    def stage4(m):
+        for d in (1, 3, 2):
+            arrive(got3[m].at[d - 1], r3.at[m, d - 1])
+        rows = last[m].shape[0] // 2
+        for h in range(2):
+            total = got2[m][h, z].astype(jnp.float32)
+            for d in range(3):
+                total = total + got3[m][d, h].astype(jnp.float32)
+            last[m][pl.ds(h * rows, rows), :] = total.astype(jnp.bfloat16)
+        mine = piece(m, p)
+        remote(last[m], mine, s4.at[m], r4.at[m, 0], at.xn).start()
+        remote(last[m], mine, s4.at[m], r4.at[m, 1], at.yn).start()
+        remote(last[m], mine, s4.at[m], r4.at[m, 4], at.sib).start()
+        pltpu.make_async_copy(last[m], mine, lo.at[m]).start()
+
+    def stage5(m):
+        arrive(piece(m, at.px), r4.at[m, 0])
+        part = piece(m, at.px, 0)
+        remote(part, part, s4.at[m], r4.at[m, 2], at.yn).start()
+        part = piece(m, at.px)
+        remote(part, part, s4.at[m], r4.at[m, 4], at.sib).start()
+        arrive(piece(m, at.py), r4.at[m, 1])
+        part = piece(m, at.py, 1)
+        remote(part, part, s4.at[m], r4.at[m, 3], at.xn).start()
+        part = piece(m, at.py)
+        remote(part, part, s4.at[m], r4.at[m, 4], at.sib).start()
+
+    def stage6(m):
+        arrive(piece(m, at.pd, 0), r4.at[m, 2])
+        arrive(piece(m, at.pd, 1), r4.at[m, 3])
+        part = piece(m, at.pd)
+        remote(part, part, s4.at[m], r4.at[m, 4], at.sib).start()
+
+    def extra_start():
+        cp = pltpu.make_async_copy(extra, extra_in, el.at[0])
+        cp.start()
+        cp.wait()
+        extra_keep[0] = extra_in[...]
+        remote(extra_keep.at[0], extra_got.at[0], es.at[0], er.at[0], at.sib).start()
+
+    def extra_step(k):
+        arrive(extra_got.at[k], er.at[k])
+        extra_keep[k + 1] = extra_keep[k] + extra_got[k]
+        if k < 2:
+            target = (at.xn, at.yn)[k]
+            remote(
+                extra_keep.at[k + 1], extra_got.at[k + 1], es.at[k + 1], er.at[k + 1], target
+            ).start()
+        else:
+            for d in (1, 3, 2):
+                zz = lax.rem(z + d, NARROW)
+                remote(
+                    extra_keep.at[3, zz],
+                    extra_sum.at[d - 1],
+                    es.at[2 + d],
+                    er.at[2 + d],
+                    depth[d - 1],
+                ).start()
+
+    def extra_end():
+        total = extra_keep[3, z]
+        for d in (1, 3, 2):
+            arrive(extra_sum.at[d - 1], er.at[2 + d])
+            total = total + extra_sum[d - 1]
+        extra_in[0] = total
+        cp = pltpu.make_async_copy(extra_in.at[0], extra_out, el.at[1])
+        cp.start()
+        cp.wait()
+
+    stage1(0)
+    if count > 1:
+        stage1(1)
+    extra_start()
+    for u in range(count + 5):
+        if u < count:
+            stage2(u)
+            if u + 2 < count:
+                stage1(u + 2)
+        if u < 3:
+            extra_step(u)
+        if 0 <= u - 1 < count:
+            stage3(u - 1)
+        if 0 <= u - 2 < count:
+            stage4(u - 2)
+        if 0 <= u - 3 < count:
+            stage5(u - 3)
+        if 0 <= u - 4 < count:
+            stage6(u - 4)
+        if u == 4:
+            extra_end()
+    for m in range(count):
+        cols = outs[m].shape[1] // 2
+        arrive(outs[m].at[:, pl.ds(0, cols)], r4.at[m, 4])
+        wait_local(last[m], lo.at[m])
+        for h in range(2):
+            left(got1[m].at[h], s1.at[m, h])
+            left(got2[m].at[h], s2.at[m, h])
+        for d in range(3):
+            left(got3[m].at[d], s3.at[m, d])
+        left(outs[m].at[:, pl.ds(0, cols)], s4.at[m])
+        rows = outs[m].shape[0] // 4
+        left(outs[m].at[pl.ds(0, 3 * rows), pl.ds(0, cols)], s4.at[m])
+    for k in range(3):
+        left(extra_got.at[k], es.at[k])
+    for d in range(3):
+        left(extra_sum.at[d], es.at[3 + d])
+
+
+def reduce_grads(grads, extra):
+    count = len(grads)
+    scratch = []
+    views = []
+    for g in grads:
+        rows, cols = g.shape
+        views.append(g.reshape(4, 2, 2, 2, rows // 32, cols))
+    for g in grads:
+        rows, cols = g.shape
+        scratch.append(pltpu.VMEM((2, 4, 2, rows // 32, cols), jnp.bfloat16))
+    for g in grads:
+        rows, cols = g.shape
+        scratch.append(pltpu.VMEM((2, 4, 2, rows // 32, cols), jnp.bfloat16))
+    for g in grads:
+        rows, cols = g.shape
+        scratch.append(pltpu.VMEM((2, 4, rows // 32, cols), jnp.bfloat16))
+    for g in grads:
+        rows, cols = g.shape
+        scratch.append(pltpu.VMEM((3, 2, rows // 32, cols), jnp.bfloat16))
+    for g in grads:
+        rows, cols = g.shape
+        scratch.append(pltpu.VMEM((rows // 16, cols), jnp.bfloat16))
+    scratch += [
+        pltpu.VMEM(extra.shape, jnp.float32),
+        pltpu.VMEM((4,) + extra.shape, jnp.float32),
+        pltpu.VMEM((3,) + extra.shape, jnp.float32),
+        pltpu.VMEM((3,) + extra.shape[1:], jnp.float32),
+    ]
+    scratch += [
+        DMA((count, 2)),
+        DMA((count, 2)),
+        DMA((count, 2)),
+        DMA((count, 2)),
+        DMA((count, 2)),
+        DMA((count, 3)),
+        DMA((count, 3)),
+        DMA((count,)),
+        DMA((count, 5)),
+        DMA((count,)),
+        DMA((6,)),
+        DMA((6,)),
+        DMA((2,)),
+    ]
+    outs = pl.pallas_call(
+        lambda *refs: reduce_kernel(count, *refs),
+        out_shape=tuple(
+            jax.ShapeDtypeStruct((g.shape[0] // 4, g.shape[1] * 2), jnp.bfloat16) for g in grads
+        )
+        + (jax.ShapeDtypeStruct(extra.shape[1:], jnp.float32),),
+        in_specs=[HBM] * (count + 1),
+        out_specs=(HBM,) * (count + 1),
+        scratch_shapes=scratch,
+        compiler_params=pltpu.CompilerParams(
+            collective_id=3, has_side_effects=True, vmem_limit_bytes=58 << 20
+        ),
+        name="reduce_grads",
+    )(*views, extra)
+    return outs[:count], outs[count]
+
+
+def per_device_linked(
+    tokens,
+    cotangent,
+    thresholds,
+    attn_norm_gain,
+    attn_norm_shift,
+    query_weight,
+    key_weight,
+    value_weight,
+    relative_weight,
+    content_bias,
+    position_bias,
+    out_weight,
+    out_bias,
+    mlp_norm_gain,
+    mlp_norm_shift,
+    inner_weight,
+    inner_bias,
+    outer_weight,
+    outer_bias,
+):
+    seq_count, length, model_width = tokens.shape
+    row_count = seq_count * length
+    span = 2 * length - 1
+    query_scale = KEY ** (-0.5)
+    vectors = (
+        attn_norm_gain,
+        attn_norm_shift,
+        content_bias,
+        position_bias,
+        out_bias,
+        mlp_norm_gain,
+        mlp_norm_shift,
+        inner_bias,
+        outer_bias,
+    )
+    sizes = [v.shape[0] for v in vectors]
+    small = jnp.concatenate(vectors).reshape(-1, 128)
+    small = jnp.pad(small, ((0, -small.shape[0] % 8), (0, 0)))
+    fulls, relative_full, small_full = gather_weights(
+        (query_weight, key_weight, value_weight, out_weight, inner_weight, outer_weight),
+        relative_weight,
+        small,
+    )
+    query_full, key_full, value_full, exit_full, inner_full, outer_full = fulls
+    flat_small = small_full.reshape(NARROW, -1)
+    spread = []
+    start = 0
+    for size in sizes:
+        spread.append(flat_small[:, start : start + size].reshape(-1).astype(jnp.float32))
+        start += size
+    (
+        attn_gain_f,
+        attn_shift_f,
+        content_f,
+        position_f,
+        exit_f,
+        mlp_gain_f,
+        mlp_shift_f,
+        inner_offset_f,
+        outer_offset_f,
+    ) = spread
+    flat_tokens = tokens.reshape(row_count, model_width).astype(jnp.float32)
+    normed = layer_norm(flat_tokens, attn_gain_f, attn_shift_f).astype(jnp.bfloat16)
+    queries = jnp.dot(normed, query_full, preferred_element_type=jnp.float32) * query_scale
+    content_query = (
+        (queries + content_f).astype(jnp.bfloat16).reshape(seq_count, length, H, KEY)
+    )
+    position_query = (
+        (queries + position_f).astype(jnp.bfloat16).reshape(seq_count, length, H, KEY)
+    )
+    key_rows = (
+        jnp.dot(normed, key_full, preferred_element_type=jnp.float32)
+        .astype(jnp.bfloat16)
+        .reshape(seq_count, length, H, KEY)
+    )
+    value_rows = (
+        jnp.dot(normed, value_full, preferred_element_type=jnp.float32)
+        .astype(jnp.bfloat16)
+        .reshape(seq_count, length, H, VAL)
+    )
+    basis = basis_table(length, F).astype(jnp.bfloat16)
+    rel_keys = (
+        jnp.dot(basis, relative_full, preferred_element_type=jnp.float32)
+        .astype(jnp.bfloat16)
+        .reshape(span, H, KEY)
+    )
+    content = jnp.einsum(
+        "bihe,bjhe->bhij", content_query, key_rows, preferred_element_type=jnp.float32
+    )
+    raw_scores = jnp.einsum(
+        "bihe,the->bhit", position_query, rel_keys, preferred_element_type=jnp.float32
+    )
+    logits = content + shift_offsets(raw_scores, length)
+    row_peak = jnp.max(logits, axis=-1, keepdims=True)
+    log_total = row_peak + jnp.log(jnp.sum(jnp.exp(logits - row_peak), axis=-1, keepdims=True))
+    soft_rows = jnp.exp(logits - log_total)
+    attention = soft_rows.astype(jnp.bfloat16)
+    mixed_heads = jnp.einsum(
+        "bhij,bjhd->bihd", attention, value_rows, preferred_element_type=jnp.float32
+    )
+    mixed_heads = mixed_heads.astype(jnp.bfloat16).reshape(row_count, H * VAL)
+    hidden = flat_tokens + (
+        jnp.dot(mixed_heads, exit_full, preferred_element_type=jnp.float32) + exit_f
+    )
+    normed_mid = layer_norm(hidden, mlp_gain_f, mlp_shift_f).astype(jnp.bfloat16)
+    inner_pre = (
+        jnp.dot(normed_mid, inner_full, preferred_element_type=jnp.float32) + inner_offset_f
+    )
+    active, gelu_pull = jax.vjp(gelu_exact, inner_pre)
+    active_low = active.astype(jnp.bfloat16)
+    result = hidden + (
+        jnp.dot(active_low, outer_full, preferred_element_type=jnp.float32) + outer_offset_f
+    )
+    layer_out = result.astype(jnp.bfloat16).reshape(seq_count, length, model_width)
+    clip_limit = jnp.repeat(thresholds, WIN, axis=1).reshape(row_count, 1)
+    clipped = jnp.clip(
+        cotangent.reshape(row_count, model_width).astype(jnp.float32), -clip_limit, clip_limit
+    )
+    outer_delta = clipped.astype(jnp.bfloat16)
+    outer_bias_grad = column_sums(outer_delta)
+    active_delta = jnp.einsum(
+        "nm,km->nk", outer_delta, outer_full, preferred_element_type=jnp.float32
+    )
+    (inner_grad_pre,) = gelu_pull(active_delta)
+    inner_delta = inner_grad_pre.astype(jnp.bfloat16)
+    inner_bias_grad = column_sums(inner_delta)
+    mid_delta = jnp.einsum("nf,df->nd", inner_delta, inner_full, preferred_element_type=jnp.float32)
+    _, norm_pull = jax.vjp(layer_norm, hidden, mlp_gain_f, mlp_shift_f)
+    hidden_part, mlp_gain_grad, mlp_shift_grad = norm_pull(mid_delta)
+    hidden_delta = clipped + hidden_part
+    branch_delta = hidden_delta.astype(jnp.bfloat16)
+    out_bias_grad = column_sums(branch_delta)
+    mixed_delta = jnp.einsum(
+        "nd,kd->nk", branch_delta, exit_full, preferred_element_type=jnp.float32
+    )
+    mixed_delta = mixed_delta.astype(jnp.bfloat16).reshape(seq_count, length, H, VAL)
+    attention_delta = jnp.einsum(
+        "bihd,bjhd->bhij", mixed_delta, value_rows, preferred_element_type=jnp.float32
+    )
+    value_delta = jnp.einsum(
+        "bhij,bihd->bjhd", attention, mixed_delta, preferred_element_type=jnp.float32
+    )
+    value_delta = value_delta.astype(jnp.bfloat16).reshape(row_count, H * VAL)
+    logit_delta = soft_rows * (
+        attention_delta - jnp.sum(soft_rows * attention_delta, axis=-1, keepdims=True)
+    )
+    logit_delta = logit_delta.astype(jnp.bfloat16)
+    content_delta = jnp.einsum(
+        "bhij,bjhe->bihe", logit_delta, key_rows, preferred_element_type=jnp.float32
+    )
+    key_delta = jnp.einsum(
+        "bhij,bihe->bjhe", logit_delta, content_query, preferred_element_type=jnp.float32
+    )
+    key_delta = key_delta.astype(jnp.bfloat16).reshape(row_count, H * KEY)
+    offset_delta = unshift_offsets(logit_delta, length)
+    position_delta = jnp.einsum(
+        "bhit,the->bihe", offset_delta, rel_keys, preferred_element_type=jnp.float32
+    )
+    rel_delta = jnp.einsum(
+        "bhit,bihe->the", offset_delta, position_query, preferred_element_type=jnp.float32
+    )
+    rel_delta = rel_delta.astype(jnp.bfloat16).reshape(span, H * KEY)
+    relative_weight_grad = jnp.einsum(
+        "tf,tk->fk", basis, rel_delta, preferred_element_type=jnp.float32
+    )
+    content_delta = content_delta.reshape(row_count, H * KEY)
+    position_delta = position_delta.reshape(row_count, H * KEY)
+    content_bias_grad = jnp.sum(content_delta, axis=0)
+    position_bias_grad = jnp.sum(position_delta, axis=0)
+    query_delta = (content_delta + position_delta).astype(jnp.bfloat16) * jnp.asarray(
+        query_scale, jnp.bfloat16
+    )
+    normed_delta = (
+        jnp.einsum("nk,dk->nd", query_delta, query_full, preferred_element_type=jnp.float32)
+        + jnp.einsum("nk,dk->nd", key_delta, key_full, preferred_element_type=jnp.float32)
+        + jnp.einsum("nk,dk->nd", value_delta, value_full, preferred_element_type=jnp.float32)
+    )
+    _, first_pull = jax.vjp(layer_norm, flat_tokens, attn_gain_f, attn_shift_f)
+    tokens_part, attn_gain_grad, attn_shift_grad = first_pull(normed_delta)
+    tokens_grad = (
+        (hidden_delta + tokens_part).astype(jnp.bfloat16).reshape(seq_count, length, model_width)
+    )
+    (xn, xm, xi, xo), (dq, dk, dv, db, di, do) = pair_exchange(
+        (normed, mixed_heads, normed_mid, active_low),
+        (query_delta, key_delta, value_delta, branch_delta, inner_delta, outer_delta),
+    )
+
+    def outer_product(a, b):
+        return jnp.einsum("nk,nm->km", a, b, preferred_element_type=jnp.float32).astype(
+            jnp.bfloat16
+        )
+
+    grads = (
+        outer_product(xo, do),
+        outer_product(xi, di),
+        outer_product(xm, db),
+        outer_product(xn, dv),
+        outer_product(xn, dk),
+        outer_product(xn, dq),
+    )
+    parts = [relative_weight_grad.reshape(NARROW, -1)] + [
+        v.reshape(NARROW, -1)
+        for v in (
+            attn_gain_grad,
+            attn_shift_grad,
+            content_bias_grad,
+            position_bias_grad,
+            out_bias_grad,
+            mlp_gain_grad,
+            mlp_shift_grad,
+            inner_bias_grad,
+            outer_bias_grad,
+        )
+    ]
+    widths = [v.shape[1] for v in parts]
+    extra = jnp.concatenate(parts, axis=1).reshape(NARROW, -1, 128)
+    extra = jnp.pad(extra, ((0, 0), (0, -extra.shape[1] % 8), (0, 0)))
+    sums, extra_sum = reduce_grads(grads, extra)
+    outer_g, inner_g, out_g, value_g, key_g, query_g = (a.astype(jnp.float32) for a in sums)
+    flat = extra_sum.reshape(-1)
+    pieces = []
+    start = 0
+    for width in widths:
+        pieces.append(flat[start : start + width])
+        start += width
+    (
+        relative_weight_grad,
+        attn_gain_grad,
+        attn_shift_grad,
+        content_bias_grad,
+        position_bias_grad,
+        out_bias_grad,
+        mlp_gain_grad,
+        mlp_shift_grad,
+        inner_bias_grad,
+        outer_bias_grad,
+    ) = pieces
+    return (
+        layer_out,
+        tokens_grad,
+        attn_gain_grad,
+        attn_shift_grad,
+        query_g,
+        key_g,
+        value_g,
+        relative_weight_grad.reshape(relative_weight.shape),
+        content_bias_grad,
+        position_bias_grad,
+        out_g,
+        out_bias_grad,
+        mlp_gain_grad,
+        mlp_shift_grad,
+        inner_g,
+        inner_bias_grad,
+        outer_g,
+        outer_bias_grad,
+    )
+
+
 def solution(mesh):
+    body = per_device_generic
+    if mesh.shape[WIDE] == 8 and mesh.shape[DEPTH] == 4:
+        body = per_device_linked
     in_specs = (
-        P(("wide", "narrow"), None, None),
-        P(("wide", "narrow"), None, None),
-        P(("wide", "narrow"), None),
-        P("narrow"),
-        P("narrow"),
-        P("narrow", None),
-        P("narrow", None),
-        P("narrow", None),
-        P("narrow", None),
-        P("narrow"),
-        P("narrow"),
-        P("narrow", None),
-        P("narrow"),
-        P("narrow"),
-        P("narrow"),
-        P("narrow", None),
-        P("narrow"),
-        P("narrow", None),
-        P("narrow"),
+        P((WIDE, DEPTH), None, None),
+        P((WIDE, DEPTH), None, None),
+        P((WIDE, DEPTH), None),
+        P(DEPTH),
+        P(DEPTH),
+        P(DEPTH, None),
+        P(DEPTH, None),
+        P(DEPTH, None),
+        P(DEPTH, None),
+        P(DEPTH),
+        P(DEPTH),
+        P(DEPTH, None),
+        P(DEPTH),
+        P(DEPTH),
+        P(DEPTH),
+        P(DEPTH, None),
+        P(DEPTH),
+        P(DEPTH, None),
+        P(DEPTH),
     )
     out_specs = (
-        P(("wide", "narrow"), None, None),
-        P(("wide", "narrow"), None, None),
-        P("narrow"),
-        P("narrow"),
-        P("narrow", None),
-        P("narrow", None),
-        P("narrow", None),
-        P("narrow", None),
-        P("narrow"),
-        P("narrow"),
-        P("narrow", None),
-        P("narrow"),
-        P("narrow"),
-        P("narrow"),
-        P("narrow", None),
-        P("narrow"),
-        P("narrow", None),
-        P("narrow"),
+        P((WIDE, DEPTH), None, None),
+        P((WIDE, DEPTH), None, None),
+        P(DEPTH),
+        P(DEPTH),
+        P(DEPTH, None),
+        P(DEPTH, None),
+        P(DEPTH, None),
+        P(DEPTH, None),
+        P(DEPTH),
+        P(DEPTH),
+        P(DEPTH, None),
+        P(DEPTH),
+        P(DEPTH),
+        P(DEPTH),
+        P(DEPTH, None),
+        P(DEPTH),
+        P(DEPTH, None),
+        P(DEPTH),
     )
     return jax.shard_map(
-        per_device, mesh=mesh, in_specs=in_specs, out_specs=out_specs, check_vma=False
-    )
+        body, mesh=mesh, in_specs=in_specs, out_specs=out_specs, check_vma=False
+    )

time: 1330 us -> 594 us (0.45)
  waiting for transfers between devices: 889 us -> 0 us
  Pallas kernels: 0 us -> 347 us
  blocking collectives: 190 us -> 0 us
  between operations: 17.5 us -> 2.02 us
  matrix products: 106 us -> 90.7 us
  other arithmetic: 15.8 us -> 30.7 us
    all_gather x10 -> x0, waiting for transfers between devices: 479 us -> none  [the longest x1 160 us: per_device(): lax.all_gather(inner_weight, 'narrow', axis=0, tiled=True)]
    pallas_call x0 -> x3, Pallas kernels: none -> 347 us  [the longest x1 204 us: reduce_grads(): pl.pallas_call(lambda *refs: reduce_kernel(count, *refs), out_shape=tuple...]
    reduce_scatter x8 -> x0, waiting for transfers between devices: 281 us -> none  [the longest x1 77.4 us: per_device(): lax.psum_scatter(outer_weight_grad.astype(jnp.bfloat16), 'wide', scatter_...]
    all_gather x13 -> x0, blocking collectives: 150 us -> none  [the longest x1 16.2 us: per_device(): lax.all_gather(relative_weight, 'narrow', axis=0, tiled=True)]
    unnamed x30 -> x0, waiting for transfers between devices: 130 us -> none
    psum x1 -> x0, blocking collectives: 23.3 us -> none  [per_device(): lax.psum((attn_gain_grad, attn_shift_grad, content_bias_grad, position_bi...]
    unnamed x1 -> x0, blocking collectives: 16.9 us -> none
    dot_general x29, matrix products: 106 us -> 90.7 us  [the longest x6 17.2 us: outer_product(): jnp.einsum('nk,nm->km', a, b, preferred_element_type=jnp.float32)]
  transfers between devices with their start and end apart: 24 -> 0, of which waited for: 17 -> 0; matrix products, arithmetic and copies ran while one was open for 14% -> 0% of each run, Pallas kernels for 0% -> 0%
where the time goes in v1:
time: 594 us; the launch traced here: 584 us
  Pallas kernels  347 us (58%)
  local copies, waits for them, and re-layouts  113 us (19%)
  matrix products  90.7 us (15%)
  other arithmetic  30.7 us (5%)
    pallas_call x1, Pallas kernels, reduce_grads(): pl.pallas_call(lambda *refs: reduce_kernel(count, *refs), out_shape=tuple...  204 us
    pallas_call x1, Pallas kernels, gather_weights(): pl.pallas_call(lambda *refs: gather_kernel(count, *refs), out_shape=tuple...  133 us
    unnamed x179, local copies, waits for them, and re-layouts  57.3 us
    dot_general x6, matrix products, outer_product(): jnp.einsum('nk,nm->km', a, b, preferred_element_type=jnp.float32)  17.2 us
    dot_general x1, matrix products, per_device_linked(): jnp.dot(normed_mid, inner_full, preferred_element_type=jnp.float32)  12.8 us
    convert_element_type x6, other arithmetic, per_device_linked(): a.astype(jnp.float32)  12.7 us

profile of v1, /device:TPU:0, one launch (start us, length us, event | category | flops | bytes accessed | tf_op | source)
XLA Modules:
  0.0 583.9 jit_solution(6518243343393540190)
XLA Ops:
  17.0 132.6 %gather_weights.1 = (bf16[4,384,512]{2,1,0:T(8,128)(2,1)S(1)}, bf16[4,384,512]{2,1,0:T(8,128)(2,1)S(1)}, bf16[4,384,1536]{2,1,0:T(8,128)(2,1)S(1)}, bf16[4,384,1...) custom-call(bf16[384,512]{1,0:T(8,128)(2,1)S(1)} %copy-done.14, ...), custom_call_target="tpu_custom_call" | custom-call | tf_op jit(solution)/shard_map/gather_weights/pallas_call | solution.py:597
  151.9 3.6 copy-done.17
  168.7 5.4 copy.120
  174.0 4.8 pad.21.clone
  178.8 5.0 reshape.557
  183.8 5.4 slice.129
  189.2 8.0 %reshape.558 = f32[1,8,256,511]{3,2,1,0:T(8,128)} reshape(f32[1,8,130816]{2,1,0:T(8,128)} %slice.129) | data formatting | bytes 8372224 | tf_op jit(solution)/shard_map/reshape | solution.py:41
  200.2 3.2 copy.119
  204.4 3.4 fusion.82
  209.8 3.8 convolution_convert_fusion.1
  218.4 3.8 fusion.83
  227.0 12.8 %multiply_convert_fusion = (bf16[256,3072]{1,0:T(8,128)(2,1)}, f32[256,3072]{1,0:T(8,128)S(1)}, f32[256,3072]{1,0:T(8,128)S(1)}) fusion(f32[3072]{0:T(1024)S(1)} %reshape.599, bf16[256,1536]{1,0:T(8,128)(2,1)S(1)} %add_convert_fusion.2.refs_2_, bf16[1536,3072]{1,0:T(8,128)(2,1)} %bitcast.271), kind=kOutput, calls=%fused_computation.9 | convolution fusion | flops 2467823616 | bytes 18100224 | tf_op jit(solution)/shard_map/dot_general | solution.py:1037
  239.9 7.8 %convert_reduce_fusion = (f32[3072]{0:T(1024)}, bf16[256,3072]{1,0:T(8,128)(2,1)S(1)}) fusion(f32[256,3072]{1,0:T(8,128)S(1)} %get-tuple-element.84, f32[256,3072]{1,0:T(8,128)S(1)} %get-tuple-element.121, bf16[3072,1536]{1,0:T(8,128)(2,1)} %bitcast.310, bf16[1,256,1536]{2,1,0:T(8,128)(2,1)S(1)} %copy-done.35, f32[256]{0:T(256)S(1)} %copy-done.64, ...), kind=kOutput, calls=%fused_computation.7 | convolution fusion | flops 2430858240 | bytes 18102272 | tf_op jit(solution)/shard_map/nm,km->nk/dot_general | solution.py:1051
  247.6 6.8 %multiply_reduce_fusion = (f32[1536]{0:T(1024)}, f32[256]{0:T(256)S(1)}, f32[1536]{0:T(1024)}, f32[256,1536]{1,0:T(8,128)S(1)}) fusion(f32[256,1536]{1,0:T(8,128)S(1)} %copy-done.23, f32[256]{0:T(256)S(1)} %fusion.68, f32[256]{0:T(256)S(1)} %broadcast_multiply_fusion, f32[1536]{0:T(1024)S(1)} %reshape.597, ...), kind=kOutput, calls=%fused_computation.80 | convolution fusion | flops 2419061504 | bytes 14177280 | tf_op jit(solution)/shard_map/nf,df->nd/dot_general | solution.py:1057
  272.0 5.2 reshape.610
  277.2 5.1 reshape.567
  300.5 4.1 fusion.86
  312.9 3.8 fusion.26
  329.2 10.2 %pair_exchange.1 = (bf16[2,256,1536]{2,1,0:T(8,128)(2,1)S(1)}, bf16[2,256,1536]{2,1,0:T(8,128)(2,1)S(1)}, bf16[2,256,1536]{2,1,0:T(8,128)(2,1)S(1)}, bf16[2,256,...) custom-call(bf16[256,1536]{1,0:T(8,128)(2,1)S(1)} %copy-done.1, ...), custom_call_target="tpu_custom_call" | custom-call | tf_op jit(solution)/shard_map/pair_exchange/pallas_call | solution.py:659
  348.1 4.3 bitcast_convert_fusion
  352.3 4.3 bitcast_convert_fusion.1
  356.6 204.4 %reduce_grads.1 = (bf16[768,1536]{1,0:T(8,128)(2,1)}, bf16[384,3072]{1,0:T(8,128)(2,1)}, bf16[384,1536]{1,0:T(8,128)(2,1)}, bf16[384,1536]{1,0:T(8,128)(2,1)}, b...) custom-call(bf16[4,2,2,2,96,768]{5,4,3,2,1,0:T(8,128)(2,1)} %bitcast.286, ...), custom_call_target="tpu_custom_call" | custom-call | tf_op jit(solution)/shard_map/reduce_grads/pallas_call | solution.py:913
  561.1 4.6 convert_element_type.326
  576.3 7.2 %fusion.12 = bf16[1,256,1536]{2,1,0:T(8,128)(2,1)} fusion(f32[256,1536]{1,0:T(8,128)S(1)} %copy-done.24, bf16[256,3072]{1,0:T(8,128)(2,1)S(1)} %copy-done.6, bf16[3072,1536]{1,0:T(8,128)(2,1)} %bitcast.311, f32[1536]{0:T(1024)S(1)} %reshape.600), kind=kOutput, calls=%fused_computation.36 | convolution fusion | flops 2417098752 | bytes 13375488 | tf_op jit(solution)/shard_map/dot_general | solution.py:1042
  (272 shorter events, 122.3 us)
Async XLA Ops:
  17.0 143.6 %copy-start.74 = (f32[1,2]{1,0:T(1,128)S(1)}, f32[1,2]{1,0:T(1,128)}, u32[]{:S(2)}) copy-start(f32[1,2]{1,0:T(1,128)} %param.25) | copy-start | bytes 28
  151.9 5.3 copy-start.18
  151.9 12.0 %copy-start.9 = (bf16[4,384,512]{2,1,0:T(8,128)(2,1)}, bf16[4,384,512]{2,1,0:T(8,128)(2,1)S(1)}, u32[]{:S(2)}) copy-start(bf16[4,384,512]{2,1,0:T(8,128)(2,1)S(1)} %get-tuple-element.47) | copy-start | bytes 4718596
  157.8 45.8 %copy-start.56 = (f32[1536]{0:T(1024)}, f32[1536]{0:T(1024)S(1)}, u32[]{:S(2)}) copy-start(f32[1536]{0:T(1024)S(1)} %reshape.593) | copy-start | bytes 18436
  159.1 4.7 copy-start.59
  217.1 5.2 copy-start.30
  226.9 12.9 %copy-start.75 = (f32[1,2]{1,0:T(1,128)S(1)}, f32[1,2]{1,0:T(1,128)}, u32[]{:S(2)}) copy-start(f32[1,2]{1,0:T(1,128)} %param.25) | copy-start | bytes 28
  226.9 12.9 %copy-start.35 = (bf16[1,256,1536]{2,1,0:T(8,128)(2,1)S(1)}, bf16[1,256,1536]{2,1,0:T(8,128)(2,1)}, u32[]{:S(2)}) copy-start(bf16[1,256,1536]{2,1,0:T(8,128)(2,1)} %param.24) | copy-start | bytes 2359300
  226.9 12.9 %copy-start.64 = (f32[256]{0:T(256)S(1)}, f32[256]{0:T(256)}, u32[]{:S(2)}) copy-start(f32[256]{0:T(256)} %get-tuple-element.135) | copy-start | bytes 3076
  239.9 7.8 %copy-start.23 = (f32[256,1536]{1,0:T(8,128)S(1)}, f32[256,1536]{1,0:T(8,128)}, u32[]{:S(2)}) copy-start(f32[256,1536]{1,0:T(8,128)} %copy-done.22) | copy-start | bytes 4718596
  239.9 16.8 %slice-start = ((s8[4718592]{0:T(1024)(128)(4,1)}), s8[524288]{0:T(1024)(128)(4,1)S(1)}, s32[]{:S(2)}) async-start(s8[4718592]{0:T(1024)(128)(4,1)} %bitcast.263), calls=%async_computation | async-start | bytes 1048576
  247.6 6.8 %copy-start.7 = (bf16[256,3072]{1,0:T(8,128)(2,1)}, bf16[256,3072]{1,0:T(8,128)(2,1)S(1)}, u32[]{:S(2)}) copy-start(bf16[256,3072]{1,0:T(8,128)(2,1)S(1)} %get-tuple-element.131.refs_8_) | copy-start | bytes 4718596
  247.6 9.1 %slice-start.1 = ((s8[4718592]{0:T(1024)(128)(4,1)}), s8[4194304]{0:T(1024)(128)(4,1)S(1)}, s32[]{:S(2)}) async-start(s8[4718592]{0:T(1024)(128)(4,1)} %bitcast.263), calls=%async_computation.1 | async-start | bytes 8388608
  293.9 10.7 %copy-start.39 = (bf16[8,64,256]{2,1,0:T(8,128)(2,1)}, bf16[8,64,256]{2,1,0:T(8,128)(2,1)S(1)}, u32[]{:S(2)}) copy-start(bf16[8,64,256]{2,1,0:T(8,128)(2,1)S(1)} %convolution_convert_fusion.5) | copy-start | bytes 786436
  305.6 5.5 copy-start.73
  305.6 6.1 %copy-start.72 = (f32[1536]{0:T(1024)S(1)}, f32[1536]{0:T(1024)}, u32[]{:S(2)}) copy-start(f32[1536]{0:T(1024)} %get-tuple-element.74) | copy-start | bytes 18436
  305.6 6.7 %copy-start.65 = (f32[3072]{0:T(1024)S(1)}, f32[3072]{0:T(1024)}, u32[]{:S(2)}) copy-start(f32[3072]{0:T(1024)} %get-tuple-element.130) | copy-start | bytes 36868
  305.6 7.3 %copy-start.21 = (bf16[1,256,1536]{2,1,0:T(8,128)(2,1)S(1)}, bf16[1,256,1536]{2,1,0:T(8,128)(2,1)}, u32[]{:S(2)}) copy-start(bf16[1,256,1536]{2,1,0:T(8,128)(2,1)} %param.23) | copy-start | bytes 2359300
  305.6 7.3 %copy-start.36 = (bf16[1,256,1536]{2,1,0:T(8,128)(2,1)S(1)}, bf16[1,256,1536]{2,1,0:T(8,128)(2,1)}, u32[]{:S(2)}) copy-start(bf16[1,256,1536]{2,1,0:T(8,128)(2,1)} %param.24) | copy-start | bytes 2359300
  305.6 7.3 %copy-start.58 = (f32[1536]{0:T(1024)S(1)}, f32[1536]{0:T(1024)}, u32[]{:S(2)}) copy-start(f32[1536]{0:T(1024)} %copy-done.56) | copy-start | bytes 18436
  316.7 4.7 copy-start.34
  561.1 4.6 copy-start.37
  570.2 6.1 %copy-start.24 = (f32[256,1536]{1,0:T(8,128)S(1)}, f32[256,1536]{1,0:T(8,128)}, u32[]{:S(2)}) copy-start(f32[256,1536]{1,0:T(8,128)} %copy-done.22) | copy-start | bytes 4718596
  571.9 4.4 copy-start.6
  (54 other events, 122.4 us)

commit v2 on v0

--- a/solution.py
+++ b/solution.py
@@ -1,8 +1,11 @@
 import math
+import types
 
 import jax
 import jax.numpy as jnp
 from jax import lax
+from jax.experimental import pallas as pl
+from jax.experimental.pallas import tpu as pltpu
 from jax.sharding import PartitionSpec as P
 
 H = 8
@@ -60,7 +63,30 @@
     return jnp.sum(values.astype(jnp.float32), axis=0)
 
 
-def per_device(
+WIDE = "wide"
+DEPTH = "narrow"
+
+
+def spread_rows(shard):
+    return lax.all_gather(shard, DEPTH, axis=0, tiled=True)
+
+
+def sum_columns(part):
+    low = part.astype(jnp.bfloat16)
+    return lax.psum_scatter(low, WIDE, scatter_dimension=1, tiled=True).astype(jnp.float32)
+
+
+def sum_rows(part):
+    low = part.astype(jnp.bfloat16)
+    return lax.psum_scatter(low, DEPTH, scatter_dimension=0, tiled=True).astype(jnp.float32)
+
+
+def spread_columns(part):
+    low = part.astype(jnp.bfloat16)
+    return lax.all_gather(low, WIDE, axis=1, tiled=True).astype(jnp.float32)
+
+
+def per_device_generic(
     tokens,
     cotangent,
     thresholds,
@@ -97,24 +123,24 @@
         exit_full,
         exit_bias,
     ) = (
-        lax.all_gather(attn_norm_gain, "narrow", axis=0, tiled=True),
-        lax.all_gather(attn_norm_shift, "narrow", axis=0, tiled=True),
-        lax.all_gather(query_weight, "narrow", axis=0, tiled=True),
-        lax.all_gather(key_weight, "narrow", axis=0, tiled=True),
-        lax.all_gather(value_weight, "narrow", axis=0, tiled=True),
-        lax.all_gather(relative_weight, "narrow", axis=0, tiled=True),
-        lax.all_gather(content_bias, "narrow", axis=0, tiled=True),
-        lax.all_gather(position_bias, "narrow", axis=0, tiled=True),
-        lax.all_gather(out_weight, "narrow", axis=0, tiled=True),
-        lax.all_gather(out_bias, "narrow", axis=0, tiled=True),
+        spread_rows(attn_norm_gain),
+        spread_rows(attn_norm_shift),
+        spread_rows(query_weight),
+        spread_rows(key_weight),
+        spread_rows(value_weight),
+        spread_rows(relative_weight),
+        spread_rows(content_bias),
+        spread_rows(position_bias),
+        spread_rows(out_weight),
+        spread_rows(out_bias),
     )
     mlp_gain, mlp_shift, inner_full, inner_offset, outer_full, outer_offset = (
-        lax.all_gather(mlp_norm_gain, "narrow", axis=0, tiled=True),
-        lax.all_gather(mlp_norm_shift, "narrow", axis=0, tiled=True),
-        lax.all_gather(inner_weight, "narrow", axis=0, tiled=True),
-        lax.all_gather(inner_bias, "narrow", axis=0, tiled=True),
-        lax.all_gather(outer_weight, "narrow", axis=0, tiled=True),
-        lax.all_gather(outer_bias, "narrow", axis=0, tiled=True),
+        spread_rows(mlp_norm_gain),
+        spread_rows(mlp_norm_shift),
+        spread_rows(inner_weight),
+        spread_rows(inner_bias),
+        spread_rows(outer_weight),
+        spread_rows(outer_bias),
     )
     flat_tokens = tokens.reshape(row_count, model_width).astype(jnp.float32)
     attn_gain_f = attn_gain.astype(jnp.float32)
@@ -187,12 +213,12 @@
         cotangent.reshape(row_count, model_width).astype(jnp.float32), -clip_limit, clip_limit
     )
     mlp_gain, mlp_shift, inner_full, inner_offset, outer_full, outer_offset = (
-        lax.all_gather(mlp_norm_gain, "narrow", axis=0, tiled=True),
-        lax.all_gather(mlp_norm_shift, "narrow", axis=0, tiled=True),
-        lax.all_gather(inner_weight, "narrow", axis=0, tiled=True),
-        lax.all_gather(inner_bias, "narrow", axis=0, tiled=True),
-        lax.all_gather(outer_weight, "narrow", axis=0, tiled=True),
-        lax.all_gather(outer_bias, "narrow", axis=0, tiled=True),
+        spread_rows(mlp_norm_gain),
+        spread_rows(mlp_norm_shift),
+        spread_rows(inner_weight),
+        spread_rows(inner_bias),
+        spread_rows(outer_weight),
+        spread_rows(outer_bias),
     )
     mlp_gain_f = mlp_gain.astype(jnp.float32)
     outer_delta = clipped.astype(jnp.bfloat16)
@@ -225,16 +251,16 @@
         exit_full,
         exit_bias,
     ) = (
-        lax.all_gather(attn_norm_gain, "narrow", axis=0, tiled=True),
-        lax.all_gather(attn_norm_shift, "narrow", axis=0, tiled=True),
-        lax.all_gather(query_weight, "narrow", axis=0, tiled=True),
-        lax.all_gather(key_weight, "narrow", axis=0, tiled=True),
-        lax.all_gather(value_weight, "narrow", axis=0, tiled=True),
-        lax.all_gather(relative_weight, "narrow", axis=0, tiled=True),
-        lax.all_gather(content_bias, "narrow", axis=0, tiled=True),
-        lax.all_gather(position_bias, "narrow", axis=0, tiled=True),
-        lax.all_gather(out_weight, "narrow", axis=0, tiled=True),
-        lax.all_gather(out_bias, "narrow", axis=0, tiled=True),
+        spread_rows(attn_norm_gain),
+        spread_rows(attn_norm_shift),
+        spread_rows(query_weight),
+        spread_rows(key_weight),
+        spread_rows(value_weight),
+        spread_rows(relative_weight),
+        spread_rows(content_bias),
+        spread_rows(position_bias),
+        spread_rows(out_weight),
+        spread_rows(out_bias),
     )
     attn_gain_f = attn_gain.astype(jnp.float32)
     branch_delta = hidden_delta.astype(jnp.bfloat16)
@@ -311,27 +337,13 @@
         inner_weight_grad,
         outer_weight_grad,
     ) = (
-        lax.psum_scatter(
-            query_weight_grad.astype(jnp.bfloat16), "wide", scatter_dimension=1, tiled=True
-        ).astype(jnp.float32),
-        lax.psum_scatter(
-            key_weight_grad.astype(jnp.bfloat16), "wide", scatter_dimension=1, tiled=True
-        ).astype(jnp.float32),
-        lax.psum_scatter(
-            value_weight_grad.astype(jnp.bfloat16), "wide", scatter_dimension=1, tiled=True
-        ).astype(jnp.float32),
-        lax.psum_scatter(
-            relative_weight_grad.astype(jnp.bfloat16), "wide", scatter_dimension=1, tiled=True
-        ).astype(jnp.float32),
-        lax.psum_scatter(
-            out_weight_grad.astype(jnp.bfloat16), "wide", scatter_dimension=1, tiled=True
-        ).astype(jnp.float32),
-        lax.psum_scatter(
-            inner_weight_grad.astype(jnp.bfloat16), "wide", scatter_dimension=1, tiled=True
-        ).astype(jnp.float32),
-        lax.psum_scatter(
-            outer_weight_grad.astype(jnp.bfloat16), "wide", scatter_dimension=1, tiled=True
-        ).astype(jnp.float32),
+        sum_columns(query_weight_grad),
+        sum_columns(key_weight_grad),
+        sum_columns(value_weight_grad),
+        sum_columns(relative_weight_grad),
+        sum_columns(out_weight_grad),
+        sum_columns(inner_weight_grad),
+        sum_columns(outer_weight_grad),
     )
     (
         query_weight_grad,
@@ -351,54 +363,22 @@
         inner_bias_grad,
         outer_bias_grad,
     ) = (
-        lax.psum_scatter(
-            query_weight_grad.astype(jnp.bfloat16), "narrow", scatter_dimension=0, tiled=True
-        ).astype(jnp.float32),
-        lax.psum_scatter(
-            key_weight_grad.astype(jnp.bfloat16), "narrow", scatter_dimension=0, tiled=True
-        ).astype(jnp.float32),
-        lax.psum_scatter(
-            value_weight_grad.astype(jnp.bfloat16), "narrow", scatter_dimension=0, tiled=True
-        ).astype(jnp.float32),
-        lax.psum_scatter(
-            relative_weight_grad.astype(jnp.bfloat16), "narrow", scatter_dimension=0, tiled=True
-        ).astype(jnp.float32),
-        lax.psum_scatter(
-            out_weight_grad.astype(jnp.bfloat16), "narrow", scatter_dimension=0, tiled=True
-        ).astype(jnp.float32),
-        lax.psum_scatter(
-            inner_weight_grad.astype(jnp.bfloat16), "narrow", scatter_dimension=0, tiled=True
-        ).astype(jnp.float32),
-        lax.psum_scatter(
-            outer_weight_grad.astype(jnp.bfloat16), "narrow", scatter_dimension=0, tiled=True
-        ).astype(jnp.float32),
-        lax.psum_scatter(
-            attn_gain_grad.astype(jnp.bfloat16), "narrow", scatter_dimension=0, tiled=True
-        ).astype(jnp.float32),
-        lax.psum_scatter(
-            attn_shift_grad.astype(jnp.bfloat16), "narrow", scatter_dimension=0, tiled=True
-        ).astype(jnp.float32),
-        lax.psum_scatter(
-            content_bias_grad.astype(jnp.bfloat16), "narrow", scatter_dimension=0, tiled=True
-        ).astype(jnp.float32),
-        lax.psum_scatter(
-            position_bias_grad.astype(jnp.bfloat16), "narrow", scatter_dimension=0, tiled=True
-        ).astype(jnp.float32),
-        lax.psum_scatter(
-            out_bias_grad.astype(jnp.bfloat16), "narrow", scatter_dimension=0, tiled=True
-        ).astype(jnp.float32),
-        lax.psum_scatter(
-            mlp_gain_grad.astype(jnp.bfloat16), "narrow", scatter_dimension=0, tiled=True
-        ).astype(jnp.float32),
-        lax.psum_scatter(
-            mlp_shift_grad.astype(jnp.bfloat16), "narrow", scatter_dimension=0, tiled=True
-        ).astype(jnp.float32),
-        lax.psum_scatter(
-            inner_bias_grad.astype(jnp.bfloat16), "narrow", scatter_dimension=0, tiled=True
-        ).astype(jnp.float32),
-        lax.psum_scatter(
-            outer_bias_grad.astype(jnp.bfloat16), "narrow", scatter_dimension=0, tiled=True
-        ).astype(jnp.float32),
+        sum_rows(query_weight_grad),
+        sum_rows(key_weight_grad),
+        sum_rows(value_weight_grad),
+        sum_rows(relative_weight_grad),
+        sum_rows(out_weight_grad),
+        sum_rows(inner_weight_grad),
+        sum_rows(outer_weight_grad),
+        sum_rows(attn_gain_grad),
+        sum_rows(attn_shift_grad),
+        sum_rows(content_bias_grad),
+        sum_rows(position_bias_grad),
+        sum_rows(out_bias_grad),
+        sum_rows(mlp_gain_grad),
+        sum_rows(mlp_shift_grad),
+        sum_rows(inner_bias_grad),
+        sum_rows(outer_bias_grad),
     )
     (
         query_weight_grad,
@@ -409,27 +389,13 @@
         inner_weight_grad,
         outer_weight_grad,
     ) = (
-        lax.all_gather(query_weight_grad.astype(jnp.bfloat16), "wide", axis=1, tiled=True).astype(
-            query_weight_grad.dtype
-        ),
-        lax.all_gather(key_weight_grad.astype(jnp.bfloat16), "wide", axis=1, tiled=True).astype(
-            key_weight_grad.dtype
-        ),
-        lax.all_gather(value_weight_grad.astype(jnp.bfloat16), "wide", axis=1, tiled=True).astype(
-            value_weight_grad.dtype
-        ),
-        lax.all_gather(
-            relative_weight_grad.astype(jnp.bfloat16), "wide", axis=1, tiled=True
-        ).astype(relative_weight_grad.dtype),
-        lax.all_gather(out_weight_grad.astype(jnp.bfloat16), "wide", axis=1, tiled=True).astype(
-            out_weight_grad.dtype
-        ),
-        lax.all_gather(inner_weight_grad.astype(jnp.bfloat16), "wide", axis=1, tiled=True).astype(
-            inner_weight_grad.dtype
-        ),
-        lax.all_gather(outer_weight_grad.astype(jnp.bfloat16), "wide", axis=1, tiled=True).astype(
-            outer_weight_grad.dtype
-        ),
+        spread_columns(query_weight_grad),
+        spread_columns(key_weight_grad),
+        spread_columns(value_weight_grad),
+        spread_columns(relative_weight_grad),
+        spread_columns(out_weight_grad),
+        spread_columns(inner_weight_grad),
+        spread_columns(outer_weight_grad),
     )
     (
         attn_gain_grad,
@@ -453,7 +419,7 @@
             inner_bias_grad,
             outer_bias_grad,
         ),
-        "wide",
+        WIDE,
     )
     return (
         layer_out,
@@ -477,48 +443,1406 @@
     )
 
 
+MESH = pl.DeviceIdType.MESH
+NARROW = 4
+
+
+def position():
+    w = lax.axis_index(WIDE)
+    z = lax.axis_index(DEPTH)
+    c = lax.rem(w, 2)
+    p = lax.div(w, 2)
+    x = lax.rem(p, 2)
+    y = lax.div(p, 2)
+    chip = (lambda q: q * 2 + c)
+    return types.SimpleNamespace(
+        w=w,
+        z=z,
+        c=c,
+        p=p,
+        x=x,
+        y=y,
+        px=p + 1 - 2 * x,
+        py=p + 2 - 4 * y,
+        pd=3 - p,
+        sib=(w + 1 - 2 * c, z),
+        xn=(chip(p + 1 - 2 * x), z),
+        yn=(chip(p + 2 - 4 * y), z),
+    )
+
+
+def meet(partners):
+    barrier = pltpu.get_barrier_semaphore()
+    for partner in partners:
+        pl.semaphore_signal(barrier, inc=1, device_id=partner, device_id_type=MESH)
+    pl.semaphore_wait(barrier, len(partners))
+
+
+def remote(src, dst, send, recv, target):
+    return pltpu.make_async_remote_copy(
+        src_ref=src,
+        dst_ref=dst,
+        send_sem=send,
+        recv_sem=recv,
+        device_id=target,
+        device_id_type=MESH,
+    )
+
+
+HBM = pl.BlockSpec(memory_space=pltpu.HBM)
+DMA = pltpu.SemaphoreType.DMA
+
+
+def dot_nn(a, b):
+    return jnp.dot(a, b, preferred_element_type=jnp.float32)
+
+
+def dot_nt(a, b):
+    return lax.dot_general(a, b, (((1,), (1,)), ((), ())), preferred_element_type=jnp.float32)
+
+
+def dot_tn(a, b):
+    return lax.dot_general(a, b, (((0,), (0,)), ((), ())), preferred_element_type=jnp.float32)
+
+
+def low(v):
+    return v.astype(jnp.bfloat16)
+
+
+def wide(v):
+    return v.astype(jnp.float32)
+
+
+def lanes(start, size):
+    return pl.ds(pl.multiple_of(start, 128), size)
+
+
+def arrive(ref, sem):
+    me = (lax.axis_index(WIDE), lax.axis_index(DEPTH))
+    remote(ref, ref, sem, sem, me).wait_recv()
+
+
+def left(ref, sem):
+    me = (lax.axis_index(WIDE), lax.axis_index(DEPTH))
+    remote(ref, ref, sem, sem, me).wait_send()
+
+
+def forward_refs(
+    tok_h,
+    cot_h,
+    lim_h,
+    wq,
+    wk,
+    wv,
+    wo,
+    wu,
+    wi,
+    rel_h,
+    small_h,
+    basis_h,
+    flip_h,
+    out_h,
+    p_h,
+    cq_h,
+    pq_h,
+    k_h,
+    v_h,
+    rr_h,
+    md_h,
+    hd_h,
+    nn_h,
+    fq,
+    fk,
+    fv,
+    vec_h,
+    gu0,
+    gu1,
+    gi0,
+    gi1,
+    go,
+    sums_h,
+    q,
+    k,
+    v,
+    o,
+    u0,
+    u1,
+    i0,
+    i1,
+    rel,
+    small,
+    vec,
+    tok,
+    normed,
+    cq,
+    pq,
+    kr,
+    vr,
+    basis,
+    flip,
+    rk,
+    rr,
+    p,
+    mixed,
+    hidden,
+    nmid,
+    cot,
+    od,
+    odc,
+    ad,
+    act,
+    idl,
+    idc,
+    hd,
+    bd,
+    bdc,
+    md,
+    lo,
+    gst,
+    sums,
+    lim,
+    zr,
+    xr,
+    yr,
+    fxr,
+    fyr,
+    sr,
+    snd,
+    own,
+    ld,
+    mr,
+    ms,
+    ps,
+    pr,
+    st,
+    gs,
+):
+    return types.SimpleNamespace(**locals())
+
+
+def forward_kernel(*refs):
+    t = forward_refs(*refs)
+    at = position()
+    w, z, c, p = at.w, at.z, at.c, at.p
+    depth = [(w, lax.rem(z + d, NARROW)) for d in range(1, NARROW)]
+    meet([at.sib, at.xn, at.yn] + depth)
+    rows_all = t.tok.shape[0]
+    width = t.tok.shape[1]
+
+    plan = (
+        (t.wq, 0, t.q),
+        (t.wk, 0, t.k),
+        (t.wv, 0, t.v),
+        (t.wo, 0, t.o),
+        (t.wu, 0, t.u0),
+        (t.wu, 1, t.u1),
+        (t.wi, 0, t.i0),
+        (t.wi, 1, t.i1),
+    )
+
+    def block(m, zz, pp, half=None):
+        full = plan[m][2]
+        rows, cols = full.shape[1] // 4, full.shape[2] // 2
+        start = pp * rows
+        if half is not None:
+            rows = rows // 2
+            start = start + half * rows
+        return full.at[zz, pl.ds(pl.multiple_of(start, 16), rows), lanes(c * cols, cols)]
+
+    def send(m, ref, recv, target):
+        remote(ref, ref, t.snd.at[m], recv, target).start()
+
+    loads = [
+        pltpu.make_async_copy(src, dst, t.ld.at[k])
+        for k, (src, dst) in enumerate(
+            (
+                (t.tok_h, t.tok),
+                (t.small_h, t.small.at[z]),
+                (t.rel_h, t.rel.at[z]),
+                (t.basis_h, t.basis),
+                (t.cot_h, t.cot),
+                (t.lim_h, t.lim),
+                (t.flip_h, t.flip),
+            )
+        )
+    ]
+    for d in (1, 3, 2):
+        for k, (src, dst) in enumerate(((t.small_h, t.small), (t.rel_h, t.rel))):
+            remote(src, dst.at[z], t.ms.at[k], t.mr.at[k], depth[d - 1]).start()
+    for copy in loads:
+        copy.start()
+    for m, (shard, part, full) in enumerate(plan):
+        rows, cols = full.shape[1] // 4, full.shape[2] // 2
+        piece = shard.at[
+            pl.ds(pl.multiple_of(p * rows, 16), rows),
+            lanes(part * full.shape[2] + c * cols, cols),
+        ]
+        for d in (1, 3, 2):
+            remote(piece, block(m, z, p), t.snd.at[m], t.zr.at[m, d - 1], depth[d - 1]).start()
+    own = []
+    for m, (shard, part, full) in enumerate(plan):
+        copy = pltpu.make_async_copy(
+            shard.at[:, lanes(part * full.shape[2], full.shape[2])], full.at[z], t.own.at[m]
+        )
+        copy.start()
+        own.append(copy)
+
+    def source(d):
+        return lax.rem(z + NARROW - d, NARROW)
+
+    def spread(m, d):
+        mine = block(m, source(d), p)
+        arrive(mine, t.zr.at[m, d - 1])
+        send(m, mine, t.xr.at[m, d - 1], at.xn)
+        send(m, mine, t.yr.at[m, d - 1], at.yn)
+        send(m, mine, t.sr.at[m], at.sib)
+
+    def forward(m, d):
+        zz = source(d)
+        arrive(block(m, zz, at.px), t.xr.at[m, d - 1])
+        send(m, block(m, zz, at.px, 0), t.fxr.at[m, d - 1], at.yn)
+        send(m, block(m, zz, at.px), t.sr.at[m], at.sib)
+        arrive(block(m, zz, at.py), t.yr.at[m, d - 1])
+        send(m, block(m, zz, at.py, 1), t.fyr.at[m, d - 1], at.xn)
+        send(m, block(m, zz, at.py), t.sr.at[m], at.sib)
+
+    def finish(m, d):
+        zz = source(d)
+        arrive(block(m, zz, at.pd, 0), t.fxr.at[m, d - 1])
+        arrive(block(m, zz, at.pd, 1), t.fyr.at[m, d - 1])
+        send(m, block(m, zz, at.pd), t.sr.at[m], at.sib)
+
+    units = [(m, d) for m in range(len(plan)) for d in (1, 3, 2)]
+    events = []
+    for u in range(len(units) + 2):
+        if u < len(units):
+            events.append((spread, units[u]))
+        if 0 <= u - 1 < len(units):
+            events.append((forward, units[u - 1]))
+        if 0 <= u - 2 < len(units):
+            events.append((finish, units[u - 2]))
+    progress = [0]
+
+    def pump(count):
+        for _ in range(count):
+            if progress[0] < len(events):
+                step, unit = events[progress[0]]
+                step(*unit)
+                progress[0] += 1
+
+    def complete(m):
+        goal = events.index((finish, units[3 * m + 2])) + 1
+        pump(goal - progress[0])
+        full = plan[m][2]
+        arrive(full.at[pl.ds(0, 3), :, pl.ds(0, full.shape[2] // 2)], t.sr.at[m])
+        own[m].wait()
+
+    places = ((0, 384), (384, 384), (768, 384), (1152, 384), (1536, 384), (1920, 384), (2304, 768), (3072, 128), (3200, 128))
+
+    def vectors():
+        loads[1].wait()
+        loads[2].wait()
+        for k, full in enumerate((t.small, t.rel)):
+            arrive(full.at[pl.ds(0, 3)], t.mr.at[k])
+        for r, (start, size) in enumerate(places):
+            for zz in range(NARROW):
+                t.vec[r : r + 1, zz * size : (zz + 1) * size] = wide(
+                    t.small[zz, 0:8, start : start + size]
+                )[0:1]
+
+    def norm_rows(src, dst, gain_row):
+        def one(i, _):
+            rows = pl.ds(pl.multiple_of(i * 32, 32), 32)
+            v = wide(src[rows, :])
+            center = v - jnp.mean(v, axis=1, keepdims=True)
+            var = jnp.mean(center * center, axis=1, keepdims=True)
+            gain = t.vec[gain_row : gain_row + 1, 0:width]
+            shift = t.vec[gain_row + 1 : gain_row + 2, 0:width]
+            dst[rows, :] = low(center * lax.rsqrt(var + EPSILON) * gain + shift)
+            return 0
+
+        lax.fori_loop(0, rows_all // 32, one, 0)
+
+    def flat(full):
+        return full[...].reshape(full.shape[0] * full.shape[1], full.shape[2])
+
+    def columns(full, start, size):
+        part = full[:, :, lanes(start, size)]
+        return part.reshape(full.shape[0] * full.shape[1], size)
+
+    def make_queries():
+        queries = dot_nn(t.normed[...], flat(t.q)) * (KEY ** (-0.5))
+        size = H * KEY
+        t.cq[...] = low(queries + t.vec[7:8, 0:size])
+        t.pq[...] = low(queries + t.vec[8:9, 0:size])
+
+    def make_keys():
+        t.kr[...] = low(dot_nn(t.normed[...], flat(t.k)))
+        loads[3].wait()
+        table = t.rel[...].reshape(t.rel.shape[0] * t.rel.shape[1], t.rel.shape[2])
+        t.rk[...] = low(dot_nn(t.basis[...], table))
+        loads[6].wait()
+        t.rr[...] = low(dot_nn(t.flip[...], table))
+
+    def make_values():
+        def one(n, _):
+            t.vr[:, lanes(n * 512, 512)] = low(dot_nn(t.normed[...], columns(t.v, n * 512, 512)))
+            return 0
+
+        lax.fori_loop(0, 3, one, 0)
+
+    def pair_mask(size, split):
+        return lax.broadcasted_iota(jnp.int32, (rows_all, size), 1) < split
+
+    def heads(pair):
+        qs = slice(pair * 2 * KEY, (pair + 1) * 2 * KEY)
+        vs = slice(pair * 2 * VAL, (pair + 1) * 2 * VAL)
+        first = pair_mask(2 * KEY, KEY)
+        keys, rel, vals = t.kr[:, qs], t.rk[:, qs], t.vr[:, vs]
+        mixed = []
+        for side in range(2):
+            keep = first if side == 0 else jnp.logical_not(first)
+            cq = jnp.where(keep, t.cq[:, qs], jnp.zeros_like(t.cq[:, qs]))
+            pq = jnp.where(keep, t.pq[:, qs], jnp.zeros_like(t.pq[:, qs]))
+            raw = dot_nt(pq, rel)
+            shifted = pltpu.roll(raw, rows_all + 1, axis=1, stride=1, stride_axis=0)
+            logits = dot_nt(cq, keys) + shifted[:, :rows_all]
+            grown = jnp.exp(logits - jnp.max(logits, axis=1, keepdims=True))
+            soft = low(grown / jnp.sum(grown, axis=1, keepdims=True))
+            t.p[2 * pair + side] = soft
+            mixed.append(dot_nn(soft, vals))
+        t.mixed[0, :, vs] = low(jnp.where(pair_mask(2 * VAL, VAL), mixed[0], mixed[1]))
+
+    def give(k, src, dst):
+        remote(src, dst, t.ps.at[k], t.pr.at[k], at.sib).start()
+
+    stored = []
+
+    def store(src, dst):
+        copy = pltpu.make_async_copy(src, dst, t.st.at[len(stored)])
+        copy.start()
+        stored.append(copy)
+
+    def attend_out():
+        def one(n, _):
+            cols = lanes(n * 512, 512)
+            t.hidden[:, cols] = (
+                wide(t.tok[:, cols])
+                + dot_nn(t.mixed[0], columns(t.o, n * 512, 512))
+                + t.vec[2:3, cols]
+            )
+            return 0
+
+        lax.fori_loop(0, 3, one, 0)
+        norm_rows(t.hidden, t.nmid.at[0], 3)
+        give(2, t.nmid.at[0], t.nmid.at[1])
+
+    def clip_rows():
+        loads[4].wait()
+        loads[5].wait()
+
+        def one(i, total):
+            rows = pl.ds(pl.multiple_of(i * 32, 32), 32)
+            clipped = low(clip(i * 32, wide(t.cot[rows, :])))
+            t.od[rows, :] = clipped
+            return total + jnp.sum(wide(clipped), axis=0, keepdims=True)
+
+        total = lax.fori_loop(0, rows_all // 32, one, jnp.zeros((1, width), jnp.float32))
+        t.sums[5:6, 0:width] = total
+        half = width // 2
+        t.odc[0] = t.od[:, lanes(c * half, half)]
+        give(0, t.od.at[:, lanes((1 - c) * half, half)], t.odc.at[1])
+
+    def clip(row, values):
+        limit = jnp.where(row < WIN, t.lim[0:1, 0:1], t.lim[0:1, 1:2])
+        return jnp.minimum(jnp.maximum(values, -limit), limit)
+
+    def pull_active(h):
+        full = (t.u0, t.u1)[h]
+        half = width // 2
+        delta = t.od[:, h * half : (h + 1) * half]
+
+        def one(zz, _):
+            cols = lanes(zz * 768, 768)
+            part = dot_nt(delta, full[zz])
+            if h == 0:
+                t.ad[:, cols] = part
+            else:
+                t.ad[:, cols] = t.ad[:, cols] + part
+            return 0
+
+        lax.fori_loop(0, NARROW, one, 0)
+
+    def inner(h):
+        full = (t.i0, t.i1)[h]
+
+        def one(n, _):
+            local = n * 256
+            cols = lanes(h * width + local, 256)
+            pre = dot_nn(t.nmid[0], columns(full, local, 256)) + t.vec[6:7, cols]
+            cdf = 0.5 + 0.5 * lax.erf(pre * (0.5**0.5))
+            slope = cdf + pre * jnp.exp(-0.5 * pre * pre) * (2.0 * math.pi) ** -0.5
+            t.act[0, :, cols] = low(pre * cdf)
+            delta = low(t.ad[:, cols] * slope)
+            t.idl[h, :, lanes(local, 256)] = delta
+            t.sums[6:7, cols] = jnp.sum(wide(delta), axis=0, keepdims=True)
+            return 0
+
+        lax.fori_loop(0, 6, one, 0)
+        cols = pl.ds(h * width, width)
+        give(3 + h, t.act.at[0, :, cols], t.act.at[1, :, cols])
+
+    def finish_out():
+        def one(n, _):
+            cols = lanes(n * 256, 256)
+            for h, full in enumerate((t.u0, t.u1)):
+                spot = lanes(h * 768 + n * 256, 256)
+                t.lo[:, spot] = low(
+                    t.hidden[:, spot]
+                    + dot_nn(t.act[0], columns(full, n * 256, 256))
+                    + t.vec[5:6, spot]
+                )
+            return 0
+
+        lax.fori_loop(0, 3, one, 0)
+        store(t.lo, t.out_h)
+
+    def pull_mid():
+        for zz in range(NARROW):
+            t.hd[:, zz * 384 : (zz + 1) * 384] = dot_nt(t.idl[0], t.i0[zz]) + dot_nt(
+                t.idl[1], t.i1[zz]
+            )
+
+        def one(i, carry):
+            gain_total, shift_total, bias_total = carry
+            rows = pl.ds(pl.multiple_of(i * 32, 32), 32)
+            v = t.hidden[rows, :]
+            center = v - jnp.mean(v, axis=1, keepdims=True)
+            scale = lax.rsqrt(jnp.mean(center * center, axis=1, keepdims=True) + EPSILON)
+            n = center * scale
+            delta = t.hd[rows, :]
+            e = delta * t.vec[3:4, 0:width]
+            back = scale * (
+                e
+                - jnp.mean(e, axis=1, keepdims=True)
+                - n * jnp.mean(e * n, axis=1, keepdims=True)
+            )
+            full = clip(i * 32, wide(t.cot[rows, :])) + back
+            t.hd[rows, :] = full
+            rounded = low(full)
+            t.bd[rows, :] = rounded
+            return (
+                gain_total + jnp.sum(delta * n, axis=0, keepdims=True),
+                shift_total + jnp.sum(delta, axis=0, keepdims=True),
+                bias_total + jnp.sum(wide(rounded), axis=0, keepdims=True),
+            )
+
+        zero = jnp.zeros((1, width), jnp.float32)
+        gain_total, shift_total, bias_total = lax.fori_loop(
+            0, rows_all // 32, one, (zero, zero, zero)
+        )
+        t.sums[3:4, 0:width] = gain_total
+        t.sums[4:5, 0:width] = shift_total
+        t.sums[2:3, 0:width] = bias_total
+        half = width // 2
+        give(6, t.bd.at[:, lanes((1 - c) * half, half)], t.bdc.at[1])
+        t.bdc[0] = t.bd[:, lanes(c * half, half)]
+        store(t.hd, t.hd_h)
+
+    def pull_mixed():
+        for zz in range(NARROW):
+            t.md[:, zz * 384 : (zz + 1) * 384] = low(dot_nt(t.bd[...], t.o[zz]))
+        store(t.md, t.md_h)
+
+    def outer_product(left_ref, right_ref, dst, start, size):
+        steps = left_ref.shape[2] // 256
+        right = right_ref[:, :, start : start + size].reshape(2 * rows_all, size)
+
+        def tile(slot, n):
+            return pltpu.make_async_copy(
+                t.gst.at[slot, :, 0:size],
+                dst.at[pl.ds(pl.multiple_of(n * 256, 256), 256)],
+                t.gs.at[slot],
+            )
+
+        def one(n, _):
+            slot = lax.rem(n, 2)
+
+            @pl.when(n >= 2)
+            def _():
+                tile(slot, n - 2).wait()
+
+            lhs = left_ref[:, :, lanes(n * 256, 256)].reshape(2 * rows_all, 256)
+            t.gst[slot, :, 0:size] = low(dot_tn(lhs, right))
+            tile(slot, n).start()
+            return 0
+
+        lax.fori_loop(0, steps, one, 0)
+        tile(0, steps - 2).wait()
+        tile(1, steps - 1).wait()
+
+    t.sums[...] = jnp.zeros_like(t.sums)
+    t.vec[...] = jnp.zeros_like(t.vec)
+    loads[0].wait()
+    vectors()
+    pump(1)
+    norm_rows(t.tok, t.normed, 0)
+    give(1, t.normed, t.nn_h.at[1])
+    store(t.normed, t.nn_h.at[0])
+    pump(1)
+    clip_rows()
+    complete(0)
+    make_queries()
+    store(t.q, t.fq)
+    store(t.cq, t.cq_h)
+    store(t.pq, t.pq_h)
+    complete(1)
+    make_keys()
+    store(t.k, t.fk)
+    store(t.kr, t.k_h)
+    store(t.rr, t.rr_h)
+    complete(2)
+    make_values()
+    store(t.v, t.fv)
+    store(t.vr, t.v_h)
+    store(t.vec, t.vec_h)
+    for pair in range(4):
+        heads(pair)
+        pump(2)
+    store(t.p, t.p_h)
+    give(5, t.mixed.at[0], t.mixed.at[1])
+    complete(3)
+    attend_out()
+    complete(4)
+    pull_active(0)
+    complete(5)
+    pull_active(1)
+    complete(6)
+    inner(0)
+    complete(7)
+    inner(1)
+    give(7, t.idl.at[1 - c], t.idc.at[1])
+    t.idc[0] = t.idl[c]
+    finish_out()
+    pull_mid()
+    pull_mixed()
+    arrive(t.odc.at[1], t.pr.at[0])
+    for h in range(2):
+        arrive(t.act.at[1, :, pl.ds(0, width)], t.pr.at[3 + h])
+    outer_product(t.act, t.odc, t.gu0, 0, 384)
+    outer_product(t.act, t.odc, t.gu1, 384, 384)
+    arrive(t.nmid.at[1], t.pr.at[2])
+    arrive(t.idc.at[1], t.pr.at[7])
+    outer_product(t.nmid, t.idc, t.gi0, 0, 768)
+    outer_product(t.nmid, t.idc, t.gi1, 768, 768)
+    arrive(t.mixed.at[1], t.pr.at[5])
+    arrive(t.bdc.at[1], t.pr.at[6])
+    outer_product(t.mixed, t.bdc, t.go, 0, 768)
+    store(t.sums, t.sums_h)
+
+    arrive(t.nn_h.at[1], t.pr.at[1])
+    left(t.odc.at[1], t.ps.at[0])
+    left(t.normed, t.ps.at[1])
+    left(t.nmid.at[0], t.ps.at[2])
+    for h in range(2):
+        left(t.act.at[0, :, pl.ds(0, width)], t.ps.at[3 + h])
+    left(t.mixed.at[0], t.ps.at[5])
+    left(t.bdc.at[1], t.ps.at[6])
+    left(t.idc.at[1], t.ps.at[7])
+    for k, full in enumerate((t.small, t.rel)):
+        left(full.at[pl.ds(0, 3)], t.ms.at[k])
+    for m, (_, _, full) in enumerate(plan):
+        left(full.at[pl.ds(0, 3)], t.snd.at[m])
+    for copy in stored:
+        copy.wait()
+
+
+def forward_pass(tokens, cotangent, limits, shards, rel, small, basis, flip):
+    rows, width = tokens.shape
+    bf, f32 = jnp.bfloat16, jnp.float32
+    keys = H * KEY
+    out_shape = (
+        ((rows, width), bf),
+        ((H, rows, rows), bf),
+        ((rows, keys), bf),
+        ((rows, keys), bf),
+        ((rows, keys), bf),
+        ((rows, width), bf),
+        ((2 * rows, keys), bf),
+        ((rows, width), bf),
+        ((rows, width), f32),
+        ((2, rows, width), bf),
+        ((NARROW, width // 4, keys), bf),
+        ((NARROW, width // 4, keys), bf),
+        ((NARROW, width // 4, width), bf),
+        ((16, 2 * width), f32),
+        ((2 * width, width // 4), bf),
+        ((2 * width, width // 4), bf),
+        ((width, width // 2), bf),
+        ((width, width // 2), bf),
+        ((width, width // 2), bf),
+        ((8, 2 * width), f32),
+    )
+    quarter = width // 4
+    vmem = (
+        ((NARROW, quarter, keys), bf),
+        ((NARROW, quarter, keys), bf),
+        ((NARROW, quarter, width), bf),
+        ((NARROW, quarter, width), bf),
+        ((NARROW, 2 * quarter, width // 2), bf),
+        ((NARROW, 2 * quarter, width // 2), bf),
+        ((NARROW, quarter, width), bf),
+        ((NARROW, quarter, width), bf),
+        ((NARROW,) + rel.shape, bf),
+        ((NARROW,) + small.shape, bf),
+        ((16, 2 * width), f32),
+        ((rows, width), bf),
+        ((rows, width), bf),
+        ((rows, keys), bf),
+        ((rows, keys), bf),
+        ((rows, keys), bf),
+        ((rows, width), bf),
+        (basis.shape, bf),
+        (flip.shape, bf),
+        ((2 * rows, keys), bf),
+        ((2 * rows, keys), bf),
+        ((H, rows, rows), bf),
+        ((2, rows, width), bf),
+        ((rows, width), f32),
+        ((2, rows, width), bf),
+        ((rows, width), bf),
+        ((rows, width), bf),
+        ((2, rows, width // 2), bf),
+        ((rows, 2 * width), f32),
+        ((2, rows, 2 * width), bf),
+        ((2, rows, width), bf),
+        ((2, rows, width), bf),
+        ((rows, width), f32),
+        ((rows, width), bf),
+        ((2, rows, width // 2), bf),
+        ((rows, width), bf),
+        ((rows, width), bf),
+        ((2, rows, width // 2), bf),
+        ((8, 2 * width), f32),
+        ((8, 128), f32),
+    )
+    sems = [
+        DMA((8, 3)),
+        DMA((8, 3)),
+        DMA((8, 3)),
+        DMA((8, 3)),
+        DMA((8, 3)),
+        DMA((8,)),
+        DMA((8,)),
+        DMA((8,)),
+        DMA((7,)),
+        DMA((2,)),
+        DMA((2,)),
+        DMA((8,)),
+        DMA((8,)),
+        DMA((20,)),
+        DMA((2,)),
+    ]
+    ins = (tokens, cotangent, limits, *shards, rel, small, basis, flip)
+    return pl.pallas_call(
+        forward_kernel,
+        out_shape=tuple(jax.ShapeDtypeStruct(s, d) for s, d in out_shape),
+        in_specs=[HBM] * len(ins),
+        out_specs=(HBM,) * len(out_shape),
+        scratch_shapes=[pltpu.VMEM(s, d) for s, d in vmem] + sems,
+        compiler_params=pltpu.CompilerParams(
+            collective_id=1, has_side_effects=True, vmem_limit_bytes=60 << 20
+        ),
+        name="forward_pass",
+    )(*ins)
+
+
+UNITS = 8
+
+
+def backward_refs(
+    gu0,
+    gu1,
+    gi0,
+    gi1,
+    go,
+    p_h,
+    cq_h,
+    pq_h,
+    k_h,
+    v_h,
+    rr_h,
+    md_h,
+    hd_h,
+    tok_h,
+    nn_h,
+    fq_h,
+    fk_h,
+    fv_h,
+    vec_h,
+    sums_h,
+    flipt_h,
+    turn_h,
+    ou,
+    oi,
+    oo,
+    ov,
+    ok,
+    oq,
+    tg_h,
+    e_h,
+    rg_h,
+    gv,
+    gk,
+    gq,
+    p,
+    cq,
+    pq,
+    kr,
+    vr,
+    rr,
+    md,
+    hd,
+    tok,
+    nn,
+    fq,
+    fk,
+    fv,
+    vec,
+    sums,
+    flipt,
+    turn,
+    qd,
+    kd,
+    vd,
+    qdc,
+    kdc,
+    vdc,
+    nd,
+    tg,
+    rg,
+    rgk,
+    rgg,
+    rgs,
+    rgo,
+    eb,
+    ek,
+    eg,
+    es,
+    eo,
+    ld,
+    s1,
+    r1,
+    l1,
+    s2,
+    r2,
+    s3,
+    r3,
+    s4,
+    r4,
+    lo,
+    ps,
+    pr,
+    xs,
+    xr,
+    ws,
+    wr,
+    st,
+):
+    return types.SimpleNamespace(**locals())
+
+
+def backward_kernel(*refs):
+    head = 31
+    t = backward_refs(*refs[:head], *refs[head + 5 * UNITS :])
+    keep, got1, got2, got3, last = (
+        refs[head + k * UNITS : head + (k + 1) * UNITS] for k in range(5)
+    )
+    at = position()
+    w, z, c, p, x, y = at.w, at.z, at.c, at.p, at.x, at.y
+    depth = [(w, lax.rem(z + d, NARROW)) for d in range(1, NARROW)]
+    rows_all, width = t.tok.shape
+    meet([at.sib, at.xn, at.yn] + depth)
+
+    plan = (
+        (t.gu0, False, t.ou, 0, width // 2),
+        (t.gu1, False, t.ou, width // 4, width // 2),
+        (t.gi0, False, t.oi, 0, width),
+        (t.gi1, False, t.oi, width // 2, width),
+        (t.go, False, t.oo, 0, width // 2),
+        (t.gv, True, t.ov, 0, width // 2),
+        (t.gk, True, t.ok, 0, H * KEY // 2),
+        (t.gq, True, t.oq, 0, H * KEY // 2),
+    )
+
+    def half(m, h, mine):
+        g = plan[m][0]
+        if h == 0:
+            return g.at[:, :, x if mine else 1 - x, 0]
+        return g.at[:, y if mine else 1 - y, :, 1]
+
+    def stage1(m):
+        for h, target in ((0, at.xn), (1, at.yn)):
+            remote(half(m, h, False), got1[m].at[h], t.s1.at[m, h], t.r1.at[m, h], target).start()
+            if not plan[m][1]:
+                pltpu.make_async_copy(half(m, h, True), keep[m].at[h], t.l1.at[m, h]).start()
+
+    def stage2(m):
+        for h, target, mine in ((0, at.yn, y), (1, at.xn, x)):
+            arrive(got1[m].at[h], t.r1.at[m, h])
+            if not plan[m][1]:
+                arrive(keep[m].at[h], t.l1.at[m, h])
+
+            def add(k, _, h=h):
+                zz, o = lax.div(k, 2), lax.rem(k, 2)
+                if not plan[m][1]:
+                    own = keep[m][h, zz, o]
+                elif h == 0:
+                    own = plan[m][0][zz, o, x, 0]
+                else:
+                    own = plan[m][0][zz, y, o, 1]
+                keep[m][h, zz, o] = low(wide(own) + wide(got1[m][h, zz, o]))
+                return 0
+
+            lax.fori_loop(0, 2 * NARROW, add, 0)
+            remote(
+                keep[m].at[h, :, 1 - mine], got2[m].at[h], t.s2.at[m, h], t.r2.at[m, h], target
+            ).start()
+
+    def stage3(m):
+        for h, mine in ((0, y), (1, x)):
+            arrive(got2[m].at[h], t.r2.at[m, h])
+
+            def add(zz, _, h=h, mine=mine):
+                got2[m][h, zz] = low(wide(keep[m][h, zz, mine]) + wide(got2[m][h, zz]))
+                return 0
+
+            lax.fori_loop(0, NARROW, add, 0)
+        for d in (1, 3, 2):
+            zz = lax.rem(z + d, NARROW)
+            remote(
+                got2[m].at[:, zz],
+                got3[m].at[d - 1],
+                t.s3.at[m, d - 1],
+                t.r3.at[m, d - 1],
+                depth[d - 1],
+            ).start()
+
+    def piece(m, pp, part=None):
+        _, _, out, start, span = plan[m]
+        rows, cols = out.shape[0] // 4, last[m].shape[1]
+        first = pp * rows
+        if part is not None:
+            rows = rows // 2
+            first = first + part * rows
+        return out.at[pl.ds(pl.multiple_of(first, 16), rows), lanes(c * span + start, cols)]
+
+    def stage4(m):
+        for d in (1, 3, 2):
+            arrive(got3[m].at[d - 1], t.r3.at[m, d - 1])
+        rows = last[m].shape[0] // 2
+        for h in range(2):
+            total = wide(got2[m][h, z])
+            for d in range(3):
+                total = total + wide(got3[m][d, h])
+            last[m][h * rows : (h + 1) * rows, :] = low(total)
+        mine = piece(m, p)
+        remote(last[m], mine, t.s4.at[m], t.r4.at[m, 0], at.xn).start()
+        remote(last[m], mine, t.s4.at[m], t.r4.at[m, 1], at.yn).start()
+        remote(last[m], mine, t.s4.at[m], t.r4.at[m, 4], at.sib).start()
+        pltpu.make_async_copy(last[m], mine, t.lo.at[m]).start()
+
+    def stage5(m):
+        for pp, part, slot, target in ((at.px, 0, 0, at.yn), (at.py, 1, 1, at.xn)):
+            arrive(piece(m, pp), t.r4.at[m, slot])
+            some = piece(m, pp, part)
+            remote(some, some, t.s4.at[m], t.r4.at[m, 2 + slot], target).start()
+            some = piece(m, pp)
+            remote(some, some, t.s4.at[m], t.r4.at[m, 4], at.sib).start()
+
+    def stage6(m):
+        arrive(piece(m, at.pd, 0), t.r4.at[m, 2])
+        arrive(piece(m, at.pd, 1), t.r4.at[m, 3])
+        some = piece(m, at.pd)
+        remote(some, some, t.s4.at[m], t.r4.at[m, 4], at.sib).start()
+
+    sources = (
+        (t.p_h, t.p),
+        (t.v_h, t.vr),
+        (t.md_h, t.md),
+        (t.k_h, t.kr),
+        (t.cq_h, t.cq),
+        (t.pq_h, t.pq),
+        (t.rr_h, t.rr),
+        (t.turn_h, t.turn),
+        (t.flipt_h, t.flipt),
+        (t.nn_h, t.nn),
+        (t.fv_h, t.fv),
+        (t.fk_h, t.fk),
+        (t.fq_h, t.fq),
+        (t.tok_h, t.tok),
+        (t.hd_h, t.hd),
+        (t.vec_h, t.vec),
+        (t.sums_h, t.sums),
+    )
+    stage1(0)
+    stage1(1)
+    loads = [pltpu.make_async_copy(s, d, t.ld.at[k]) for k, (s, d) in enumerate(sources)]
+    for copy in loads:
+        copy.start()
+
+    def lane_mask(size, split, rows=rows_all):
+        return lax.broadcasted_iota(jnp.int32, (rows, size), 1) < split
+
+    def heads(pair):
+        qs = slice(pair * 2 * KEY, (pair + 1) * 2 * KEY)
+        vs = slice(pair * 2 * VAL, (pair + 1) * 2 * VAL)
+        vals, mixed = t.vr[:, vs], t.md[:, vs]
+        keys, rel, cq, pq = t.kr[:, qs], t.rr[:, qs], t.cq[:, qs], t.pq[:, qs]
+        first = lane_mask(2 * VAL, VAL)
+        parts = []
+        for side in range(2):
+            mask = first if side == 0 else jnp.logical_not(first)
+            soft = t.p[2 * pair + side]
+            pull = dot_nt(jnp.where(mask, mixed, jnp.zeros_like(mixed)), vals)
+            full = wide(soft)
+            delta = low(full * (pull - jnp.sum(full * pull, axis=1, keepdims=True)))
+            turned = dot_nn(delta, t.turn[...])
+            padded = jnp.concatenate([turned, jnp.zeros_like(turned)], axis=1)
+            slid = low(pltpu.roll(padded, 2 * rows_all, axis=1, stride=1, stride_axis=0))
+            parts.append(
+                (
+                    dot_tn(soft, mixed),
+                    dot_nn(delta, keys),
+                    dot_tn(delta, cq),
+                    dot_nn(slid, rel),
+                    dot_tn(slid, pq),
+                )
+            )
+        t.vd[:, vs] = low(jnp.where(first, parts[0][0], parts[1][0]))
+        narrow = lane_mask(2 * KEY, KEY)
+        content = jnp.where(narrow, parts[0][1], parts[1][1])
+        place = jnp.where(narrow, parts[0][3], parts[1][3])
+        t.kd[:, qs] = low(jnp.where(narrow, parts[0][2], parts[1][2]))
+        rel_delta = low(
+            jnp.where(lane_mask(2 * KEY, KEY, 2 * rows_all), parts[0][4], parts[1][4])
+        )
+        t.qd[:, qs] = low(content + place) * jnp.asarray(KEY ** (-0.5), jnp.bfloat16)
+        t.rg[:, qs] = dot_nn(t.flipt[...], rel_delta)
+        t.sums[7:8, qs] = jnp.sum(content, axis=0, keepdims=True)
+        keys_all = H * KEY
+        there = slice(keys_all + pair * 2 * KEY, keys_all + (pair + 1) * 2 * KEY)
+        t.sums[7:8, there] = jnp.sum(place, axis=0, keepdims=True)
+
+    def trade():
+        for k, (full, pair) in enumerate(((t.vd, t.vdc), (t.kd, t.kdc), (t.qd, t.qdc))):
+            cols = full.shape[1] // 2
+            away = full.at[:, lanes((1 - c) * cols, cols)]
+            remote(away, pair.at[1], t.ps.at[k], t.pr.at[k], at.sib).start()
+            pair[0] = full[:, lanes(c * cols, cols)]
+        cols = t.rg.shape[1] // 2
+        t.rgo[...] = low(t.rg[:, lanes((1 - c) * cols, cols)]).reshape(t.rgo.shape)
+        remote(t.rgo, t.rgg.at[0], t.xs.at[0], t.xr.at[0], at.sib).start()
+        t.rgk[0] = low(t.rg[:, lanes(c * cols, cols)]).reshape(t.rgo.shape)
+
+    def outer_product(pair, dst):
+        def one(zz, _):
+            lhs = t.nn[:, :, lanes(zz * 384, 384)].reshape(2 * rows_all, 384)
+            rhs = pair[...].reshape(2 * rows_all, pair.shape[2])
+            dst[zz] = low(dot_tn(lhs, rhs)).reshape(dst.shape[1:])
+            return 0
+
+        lax.fori_loop(0, NARROW, one, 0)
+
+    def pull_tokens():
+        for zz in range(NARROW):
+            t.nd[:, zz * 384 : (zz + 1) * 384] = (
+                dot_nt(t.qd[...], t.fq[zz])
+                + dot_nt(t.kd[...], t.fk[zz])
+                + dot_nt(t.vd[...], t.fv[zz])
+            )
+
+        def one(i, carry):
+            gain_total, shift_total = carry
+            rows = pl.ds(pl.multiple_of(i * 32, 32), 32)
+            v = wide(t.tok[rows, :])
+            center = v - jnp.mean(v, axis=1, keepdims=True)
+            scale = lax.rsqrt(jnp.mean(center * center, axis=1, keepdims=True) + EPSILON)
+            n = center * scale
+            delta = t.nd[rows, :]
+            e = delta * t.vec[0:1, 0:width]
+            back = scale * (
+                e
+                - jnp.mean(e, axis=1, keepdims=True)
+                - n * jnp.mean(e * n, axis=1, keepdims=True)
+            )
+            t.tg[rows, :] = low(t.hd[rows, :] + back)
+            return (
+                gain_total + jnp.sum(delta * n, axis=0, keepdims=True),
+                shift_total + jnp.sum(delta, axis=0, keepdims=True),
+            )
+
+        zero = jnp.zeros((1, width), jnp.float32)
+        gain_total, shift_total = lax.fori_loop(0, rows_all // 32, one, (zero, zero))
+        t.sums[0:1, 0:width] = gain_total
+        t.sums[1:2, 0:width] = shift_total
+        for zz in range(NARROW):
+            t.eb[zz] = jnp.zeros(t.eb.shape[1:], jnp.float32)
+            t.eb[zz, 0:6, 0:384] = t.sums[0:6, zz * 384 : (zz + 1) * 384]
+            t.eb[zz, 6:7, :] = t.sums[6:7, zz * 768 : (zz + 1) * 768]
+            t.eb[zz, 7:8, 0:128] = t.sums[7:8, zz * 128 : (zz + 1) * 128]
+            t.eb[zz, 7:8, 128:256] = t.sums[7:8, 512 + zz * 128 : 512 + (zz + 1) * 128]
+
+    def sum_steps(keep, got, over, out, sends, recvs):
+        def begin():
+            remote(keep.at[0], got.at[0], sends.at[0], recvs.at[0], at.sib).start()
+
+        def step(k):
+            arrive(got.at[k], recvs.at[k])
+            total = wide(keep[k]) + wide(got[k])
+            keep[k + 1] = total.astype(keep.dtype)
+            if k < 2:
+                target = (at.xn, at.yn)[k]
+                remote(
+                    keep.at[k + 1], got.at[k + 1], sends.at[k + 1], recvs.at[k + 1], target
+                ).start()
+            else:
+                for d in (1, 3, 2):
+                    zz = lax.rem(z + d, NARROW)
+                    remote(
+                        keep.at[3, zz],
+                        over.at[d - 1],
+                        sends.at[2 + d],
+                        recvs.at[2 + d],
+                        depth[d - 1],
+                    ).start()
+
+        def end():
+            total = wide(keep[3, z])
+            for d in (1, 3, 2):
+                arrive(over.at[d - 1], recvs.at[2 + d])
+                total = total + wide(over[d - 1])
+            out[...] = total
+
+        return begin, step, end
+
+    rel_sums = sum_steps(t.rgk, t.rgg, t.rgs, t.rg.at[0:48, 0:256], t.xs, t.xr)
+    row_sums = sum_steps(t.ek, t.eg, t.es, t.eo, t.ws, t.wr)
+
+    stored = []
+
+    def store(src, dst):
+        copy = pltpu.make_async_copy(src, dst, t.st.at[len(stored)])
+        copy.start()
+        stored.append(copy)
+
+    for copy in loads[:9]:
+        copy.wait()
+    loads[16].wait()
+    heads(0)
+    heads(1)
+    stage2(0)
+    stage1(2)
+    heads(2)
+    heads(3)
+    trade()
+    stage2(1)
+    stage1(3)
+    stage3(0)
+    loads[9].wait()
+    for k, (pair, dst) in enumerate(((t.vdc, t.gv), (t.kdc, t.gk), (t.qdc, t.gq))):
+        arrive(pair.at[1], t.pr.at[k])
+        outer_product(pair, dst)
+    rel_sums[1](0)
+    for copy in loads[10:16]:
+        copy.wait()
+    stage2(2)
+    stage1(4)
+    stage3(1)
+    stage4(0)
+    pull_tokens()
+    store(t.tg, t.tg_h)
+    t.ek[0] = t.eb[...]
+    row_sums[0]()
+    for u in range(3, UNITS + 5):
+        if u < UNITS:
+            stage2(u)
+            if u + 2 < UNITS:
+                stage1(u + 2)
+        if u - 3 < 3:
+            if u - 3 < 2:
+                rel_sums[1](u - 2)
+            else:
+                rel_sums[2]()
+            row_sums[1](u - 3)
+        if u == 6:
+            row_sums[2]()
+            store(t.eo, t.e_h)
+            store(t.rg.at[0:48, 0:256], t.rg_h.at[c])
+            remote(t.rg.at[0:48, 0:256], t.rg_h.at[c], t.xs.at[6], t.xr.at[6], at.sib).start()
+        if u - 1 < UNITS:
+            stage3(u - 1)
+        if u - 2 < UNITS:
+            stage4(u - 2)
+        if 0 <= u - 3 < UNITS:
+            stage5(u - 3)
+        if 0 <= u - 4 < UNITS:
+            stage6(u - 4)
+
+    for m in range(UNITS):
+        _, _, out, _, _ = plan[m]
+        cols = last[m].shape[1]
+        arrive(out.at[:, pl.ds(0, cols)], t.r4.at[m, 4])
+        arrive(last[m], t.lo.at[m])
+        for h in range(2):
+            left(got1[m].at[h], t.s1.at[m, h])
+            left(got2[m].at[h], t.s2.at[m, h])
+        for d in range(3):
+            left(got3[m].at[d], t.s3.at[m, d])
+        left(out.at[:, pl.ds(0, cols)], t.s4.at[m])
+        left(out.at[pl.ds(0, 3 * (out.shape[0] // 4)), pl.ds(0, cols)], t.s4.at[m])
+    for k, pair in enumerate((t.vdc, t.kdc, t.qdc)):
+        left(pair.at[1], t.ps.at[k])
+    for got, over, sends in ((t.rgg, t.rgs, t.xs), (t.eg, t.es, t.ws)):
+        for k in range(3):
+            left(got.at[k], sends.at[k])
+            left(over.at[k], sends.at[3 + k])
+    left(t.rg.at[0:48, 0:256], t.xs.at[6])
+    arrive(t.rg_h.at[1 - c], t.xr.at[6])
+    for copy in stored:
+        copy.wait()
+
+
+def backward_pass(grads, saved, tables):
+    bf, f32 = jnp.bfloat16, jnp.float32
+    tokens = saved[8]
+    rows, width = tokens.shape
+    keys = H * KEY
+    views = [g.reshape(4, 2, 2, 2, g.shape[0] // 32, g.shape[1]) for g in grads]
+    shapes = [(g.shape[0], g.shape[1]) for g in grads] + [
+        (width, width // 2),
+        (width, keys // 2),
+        (width, keys // 2),
+    ]
+    out_shape = (
+        ((width // 2, width), bf),
+        ((width // 4, 2 * width), bf),
+        ((width // 4, width), bf),
+        ((width // 4, width), bf),
+        ((width // 4, keys), bf),
+        ((width // 4, keys), bf),
+        ((rows, width), bf),
+        ((8, 768), f32),
+        ((2, 48, 256), f32),
+    )
+    vmem = []
+    for lead in ((2, 4, 2), (2, 4, 2), (2, 4), (3, 2)):
+        vmem += [(lead + (r // 32, n), bf) for r, n in shapes]
+    vmem += [((r // 16, n), bf) for r, n in shapes]
+    vmem += [((4, 2, 2, 2, r // 32, n), bf) for r, n in shapes[5:]]
+    vmem += [(s.shape, s.dtype) for s in saved[:9]]
+    vmem += [(s.shape, s.dtype) for s in saved[9:]]
+    vmem += [(s.shape, s.dtype) for s in tables]
+    vmem += [
+        ((rows, keys), bf),
+        ((rows, keys), bf),
+        ((rows, width), bf),
+        ((2, rows, keys // 2), bf),
+        ((2, rows, keys // 2), bf),
+        ((2, rows, width // 2), bf),
+        ((rows, width), f32),
+        ((rows, width), bf),
+        ((F, keys), f32),
+        ((4, 4, 48, 256), bf),
+        ((3, 4, 48, 256), bf),
+        ((3, 48, 256), bf),
+        ((4, 48, 256), bf),
+        ((4, 8, 768), f32),
+        ((4, 4, 8, 768), f32),
+        ((3, 4, 8, 768), f32),
+        ((3, 8, 768), f32),
+        ((8, 768), f32),
+    ]
+    sems = [
+        DMA((17,)),
+        DMA((UNITS, 2)),
+        DMA((UNITS, 2)),
+        DMA((UNITS, 2)),
+        DMA((UNITS, 2)),
+        DMA((UNITS, 2)),
+        DMA((UNITS, 3)),
+        DMA((UNITS, 3)),
+        DMA((UNITS,)),
+        DMA((UNITS, 5)),
+        DMA((UNITS,)),
+        DMA((3,)),
+        DMA((3,)),
+        DMA((7,)),
+        DMA((7,)),
+        DMA((6,)),
+        DMA((6,)),
+        DMA((3,)),
+    ]
+    ins = (*views, *saved, *tables)
+    return pl.pallas_call(
+        backward_kernel,
+        out_shape=tuple(jax.ShapeDtypeStruct(s, d) for s, d in out_shape),
+        in_specs=[HBM] * len(ins),
+        out_specs=(HBM,) * len(out_shape),
+        scratch_shapes=[pltpu.VMEM(s, d) for s, d in vmem] + sems,
+        compiler_params=pltpu.CompilerParams(
+            collective_id=2, has_side_effects=True, vmem_limit_bytes=60 << 20
+        ),
+        name="backward_pass",
+    )(*ins)
+
+
+def per_device_linked(
+    tokens,
+    cotangent,
+    thresholds,
+    attn_norm_gain,
+    attn_norm_shift,
+    query_weight,
+    key_weight,
+    value_weight,
+    relative_weight,
+    content_bias,
+    position_bias,
+    out_weight,
+    out_bias,
+    mlp_norm_gain,
+    mlp_norm_shift,
+    inner_weight,
+    inner_bias,
+    outer_weight,
+    outer_bias,
+):
+    _, length, width = tokens.shape
+    bf = jnp.bfloat16
+    vectors = (
+        attn_norm_gain,
+        attn_norm_shift,
+        out_bias,
+        mlp_norm_gain,
+        mlp_norm_shift,
+        outer_bias,
+        inner_bias,
+        content_bias,
+        position_bias,
+    )
+    small = jnp.broadcast_to(jnp.concatenate(vectors)[None, :], (8, 3328))
+    limits = jnp.pad(thresholds, ((0, 7), (0, 126)))
+    table = basis_table(length, F)
+    empty = jnp.zeros((1, F), jnp.float32)
+    basis = jnp.concatenate([table, empty]).astype(bf)
+    flip = jnp.concatenate([table[::-1], empty]).astype(bf)
+    turn = jnp.eye(length, dtype=bf)[::-1]
+    flat_tokens = tokens.reshape(length, width)
+    (
+        layer_out,
+        p,
+        cq,
+        pq,
+        k,
+        v,
+        rr,
+        md,
+        hd,
+        nn,
+        fq,
+        fk,
+        fv,
+        vec,
+        gu0,
+        gu1,
+        gi0,
+        gi1,
+        go,
+        sums,
+    ) = forward_pass(
+        flat_tokens,
+        cotangent.reshape(length, width),
+        limits,
+        (query_weight, key_weight, value_weight, out_weight, outer_weight, inner_weight),
+        relative_weight,
+        small,
+        basis,
+        flip,
+    )
+    ou, oi, oo, ov, ok, oq, tokens_grad, rows, rel = backward_pass(
+        (gu0, gu1, gi0, gi1, go),
+        (p, cq, pq, k, v, rr, md, hd, flat_tokens, nn, fq, fk, fv, vec, sums),
+        (flip.T, turn),
+    )
+    f32 = jnp.float32
+    return (
+        layer_out[None],
+        tokens_grad[None],
+        rows[0, :384],
+        rows[1, :384],
+        oq.astype(f32),
+        ok.astype(f32),
+        ov.astype(f32),
+        jnp.concatenate([rel[0], rel[1]], axis=1),
+        rows[7, :128],
+        rows[7, 128:256],
+        oo.astype(f32),
+        rows[2, :384],
+        rows[3, :384],
+        rows[4, :384],
+        oi.astype(f32),
+        rows[6],
+        ou.astype(f32),
+        rows[5, :384],
+    )
+
+
 def solution(mesh):
+    body = per_device_generic
+    if mesh.shape[WIDE] == 8 and mesh.shape[DEPTH] == 4:
+        body = per_device_linked
     in_specs = (
-        P(("wide", "narrow"), None, None),
-        P(("wide", "narrow"), None, None),
-        P(("wide", "narrow"), None),
-        P("narrow"),
-        P("narrow"),
-        P("narrow", None),
-        P("narrow", None),
-        P("narrow", None),
-        P("narrow", None),
-        P("narrow"),
-        P("narrow"),
-        P("narrow", None),
-        P("narrow"),
-        P("narrow"),
-        P("narrow"),
-        P("narrow", None),
-        P("narrow"),
-        P("narrow", None),
-        P("narrow"),
+        P((WIDE, DEPTH), None, None),
+        P((WIDE, DEPTH), None, None),
+        P((WIDE, DEPTH), None),
+        P(DEPTH),
+        P(DEPTH),
+        P(DEPTH, None),
+        P(DEPTH, None),
+        P(DEPTH, None),
+        P(DEPTH, None),
+        P(DEPTH),
+        P(DEPTH),
+        P(DEPTH, None),
+        P(DEPTH),
+        P(DEPTH),
+        P(DEPTH),
+        P(DEPTH, None),
+        P(DEPTH),
+        P(DEPTH, None),
+        P(DEPTH),
     )
     out_specs = (
-        P(("wide", "narrow"), None, None),
-        P(("wide", "narrow"), None, None),
-        P("narrow"),
-        P("narrow"),
-        P("narrow", None),
-        P("narrow", None),
-        P("narrow", None),
-        P("narrow", None),
-        P("narrow"),
-        P("narrow"),
-        P("narrow", None),
-        P("narrow"),
-        P("narrow"),
-        P("narrow"),
-        P("narrow", None),
-        P("narrow"),
-        P("narrow", None),
-        P("narrow"),
+        P((WIDE, DEPTH), None, None),
+        P((WIDE, DEPTH), None, None),
+        P(DEPTH),
+        P(DEPTH),
+        P(DEPTH, None),
+        P(DEPTH, None),
+        P(DEPTH, None),
+        P(DEPTH, None),
+        P(DEPTH),
+        P(DEPTH),
+        P(DEPTH, None),
+        P(DEPTH),
+        P(DEPTH),
+        P(DEPTH),
+        P(DEPTH, None),
+        P(DEPTH),
+        P(DEPTH, None),
+        P(DEPTH),
     )
     return jax.shard_map(
-        per_device, mesh=mesh, in_specs=in_specs, out_specs=out_specs, check_vma=False
-    )
+        body, mesh=mesh, in_specs=in_specs, out_specs=out_specs, check_vma=False
+    )

time: 1330 us -> 400 us (0.30)
  waiting for transfers between devices: 889 us -> 0 us
  Pallas kernels: 0 us -> 362 us
  blocking collectives: 190 us -> 0 us
  matrix products: 106 us -> 0 us
  local copies, waits for them, and re-layouts: 106 us -> 22.3 us
  between operations: 17.5 us -> 0.77 us
    all_gather x10 -> x0, waiting for transfers between devices: 479 us -> none  [the longest x1 160 us: per_device(): lax.all_gather(inner_weight, 'narrow', axis=0, tiled=True)]
    pallas_call x0 -> x2, Pallas kernels: none -> 362 us  [the longest x1 185 us: forward_pass(): pl.pallas_call(forward_kernel, out_shape=tuple((jax.ShapeDtypeStruct(s, d...]
    reduce_scatter x8 -> x0, waiting for transfers between devices: 281 us -> none  [the longest x1 77.4 us: per_device(): lax.psum_scatter(outer_weight_grad.astype(jnp.bfloat16), 'wide', scatter_...]
    all_gather x13 -> x0, blocking collectives: 150 us -> none  [the longest x1 16.2 us: per_device(): lax.all_gather(relative_weight, 'narrow', axis=0, tiled=True)]
    unnamed x30 -> x0, waiting for transfers between devices: 130 us -> none
    dot_general x29 -> x0, matrix products: 106 us -> none  [the longest x1 14.2 us: per_device(): jnp.dot(normed_mid, inner_full, preferred_element_type=jnp.float32)]
    unnamed x155 -> x26, local copies, waits for them, and re-layouts: 67 us -> 11 us
    psum x1 -> x0, blocking collectives: 23.3 us -> none  [per_device(): lax.psum((attn_gain_grad, attn_shift_grad, content_bias_grad, position_bi...]
  transfers between devices with their start and end apart: 24 -> 0, of which waited for: 17 -> 0; matrix products, arithmetic and copies ran while one was open for 14% -> 0% of each run, Pallas kernels for 0% -> 0%
where the time goes in v2:
time: 400 us; the launch traced here: 399 us
  Pallas kernels  362 us (90%)
  local copies, waits for them, and re-layouts  22.3 us (6%)
  other arithmetic  13.9 us (3%)
    pallas_call x1, Pallas kernels, forward_pass(): pl.pallas_call(forward_kernel, out_shape=tuple((jax.ShapeDtypeStruct(s, d...  185 us
    pallas_call x1, Pallas kernels, backward_pass(): pl.pallas_call(backward_kernel, out_shape=tuple((jax.ShapeDtypeStruct(s,...  177 us
    unnamed x26, local copies, waits for them, and re-layouts  11 us

profile of v2, /device:TPU:0, one launch (start us, length us, event | category | flops | bytes accessed | tf_op | source)
XLA Modules:
  0.0 399.3 jit_solution(11303941571681465799)
XLA Ops:
  0.8 1.3 pad.8.refs_2_
  2.1 0.9 dynamic-update-slice
  2.9 0.9 dynamic-update-slice.1
  3.8 0.9 dynamic-update-slice.2
  4.6 0.9 dynamic-update-slice.3
  5.5 0.9 dynamic-update-slice.4
  6.3 0.9 dynamic-update-slice.5
  7.2 0.9 dynamic-update-slice.6
  8.1 0.8 dynamic-update-slice.7
  10.4 1.3 rev.7.refs_21_
  11.9 1.2 reverse
  15.7 185.1 %forward_pass.1 = (bf16[256,1536]{1,0:T(8,128)(2,1)}, bf16[8,256,256]{2,1,0:T(8,128)(2,1)}, bf16[256,512]{1,0:T(8,128)(2,1)}, bf16[256,512]{1,0:T(8,128)(2,1)}, ...) custom-call(bf16[256,1536]{1,0:T(8,128)(2,1)} %bitcast.22, ...), custom_call_target="tpu_custom_call" | custom-call | tf_op jit(solution)/shard_map/forward_pass/pallas_call | solution.py:1147
  200.8 177.2 %backward_pass.1 = (bf16[768,1536]{1,0:T(8,128)(2,1)}, bf16[384,3072]{1,0:T(8,128)(2,1)}, bf16[384,1536]{1,0:T(8,128)(2,1)}, bf16[384,1536]{1,0:T(8,128)(2,1)}, ...) custom-call(bf16[4,2,2,2,96,384]{5,4,3,2,1,0:T(8,128)(2,1)} %bitcast, ...), custom_call_target="tpu_custom_call" | custom-call | tf_op jit(solution)/shard_map/backward_pass/pallas_call | solution.py:1687
  378.0 1.3 slice_bitcast_fusion.2
  379.3 1.3 slice_reduce_fusion
  380.7 1.6 slice_reduce_fusion.1
  383.7 2.0 convert_element_type.26
  385.7 2.1 convert_element_type.27
  387.7 1.7 convert_element_type.28
  389.4 1.7 convert_element_type.29
  392.0 2.8 convert_element_type.30
  394.7 2.8 convert_element_type.31
  397.6 0.9 copy.52
  398.4 0.9 copy.53
  (33 shorter events, 6.6 us)
Async XLA Ops:
  378.0 9.7 %copy-start.3 = (bf16[384,1536]{1,0:T(8,128)(2,1)S(1)}, bf16[384,1536]{1,0:T(8,128)(2,1)}, u32[]{:S(2)}) copy-start(bf16[384,1536]{1,0:T(8,128)(2,1)} %get-tuple-element.73) | copy-start | bytes 3538948
  385.7 3.8 copy-start.2
  389.4 2.5 copy-start.1
  392.0 2.8 copy-start
  394.7 2.8 copy-start.4
  394.7 3.7 copy-start.5

commit v3 on v2

--- a/solution.py
+++ b/solution.py
@@ -1,8 +1,10 @@
+import functools
 import math
 import types
 
 import jax
 import jax.numpy as jnp
+import numpy as np
 from jax import lax
 from jax.experimental import pallas as pl
 from jax.experimental.pallas import tpu as pltpu
@@ -491,6 +493,7 @@
 
 HBM = pl.BlockSpec(memory_space=pltpu.HBM)
 DMA = pltpu.SemaphoreType.DMA
+SMEM = pl.BlockSpec(memory_space=pltpu.SMEM)
 
 
 def dot_nn(a, b):
@@ -535,38 +538,41 @@
     wk,
     wv,
     wo,
+    wi,
     wu,
-    wi,
     rel_h,
     small_h,
     basis_h,
     flip_h,
-    out_h,
     p_h,
     cq_h,
     pq_h,
     k_h,
     v_h,
     rr_h,
-    md_h,
-    hd_h,
+    hid_h,
+    act_h,
+    slope_h,
+    od_h,
     nn_h,
+    nm_h,
+    mx_h,
     fq,
     fk,
     fv,
+    fo,
+    fi0,
+    fi1,
+    fu0,
+    fu1,
     vec_h,
     gu0,
     gu1,
-    gi0,
-    gi1,
-    go,
     sums_h,
     q,
     k,
     v,
     o,
-    u0,
-    u1,
     i0,
     i1,
     rel,
@@ -589,19 +595,12 @@
     cot,
     od,
     odc,
-    ad,
     act,
-    idl,
-    idc,
-    hd,
-    bd,
-    bdc,
-    md,
-    lo,
+    slope,
     gst,
     sums,
-    lim,
     zr,
+    zs,
     xr,
     yr,
     fxr,
@@ -629,25 +628,31 @@
     rows_all = t.tok.shape[0]
     width = t.tok.shape[1]
 
+    keys_all = H * KEY
+    quarter = width // 4
     plan = (
-        (t.wq, 0, t.q),
-        (t.wk, 0, t.k),
-        (t.wv, 0, t.v),
-        (t.wo, 0, t.o),
-        (t.wu, 0, t.u0),
-        (t.wu, 1, t.u1),
-        (t.wi, 0, t.i0),
-        (t.wi, 1, t.i1),
-    )
-
-    def block(m, zz, pp, half=None):
-        full = plan[m][2]
-        rows, cols = full.shape[1] // 4, full.shape[2] // 2
+        (t.wq, 0, 0, t.fq, keys_all),
+        (t.wk, 0, 0, t.fk, keys_all),
+        (t.wv, 0, 0, t.fv, width),
+        (t.wo, 0, 0, t.fo, width),
+        (t.wi, 0, 0, t.fi0, width),
+        (t.wi, 0, width, t.fi1, width),
+        (t.wu, 0, 0, t.fu0, width),
+        (t.wu, quarter, 0, t.fu1, width),
+    )
+
+    def rows_of(m, pp, part=None):
+        rows = quarter // 4
         start = pp * rows
-        if half is not None:
+        if part is not None:
             rows = rows // 2
-            start = start + half * rows
-        return full.at[zz, pl.ds(pl.multiple_of(start, 16), rows), lanes(c * cols, cols)]
+            start = start + part * rows
+        return start, rows
+
+    def block(m, zz, pp, part=None):
+        start, rows = rows_of(m, pp, part)
+        cols = plan[m][4] // 2
+        return plan[m][3].at[zz, pl.ds(pl.multiple_of(start, 16), rows), lanes(c * cols, cols)]
 
     def send(m, ref, recv, target):
         remote(ref, ref, t.snd.at[m], recv, target).start()
@@ -661,66 +666,101 @@
                 (t.rel_h, t.rel.at[z]),
                 (t.basis_h, t.basis),
                 (t.cot_h, t.cot),
-                (t.lim_h, t.lim),
                 (t.flip_h, t.flip),
             )
         )
     ]
-    for d in (1, 3, 2):
-        for k, (src, dst) in enumerate(((t.small_h, t.small), (t.rel_h, t.rel))):
+    def over_z(k, src, dst):
+        for d in (1, 3, 2):
             remote(src, dst.at[z], t.ms.at[k], t.mr.at[k], depth[d - 1]).start()
+
+    over_z(0, t.small_h, t.small)
     for copy in loads:
         copy.start()
-    for m, (shard, part, full) in enumerate(plan):
-        rows, cols = full.shape[1] // 4, full.shape[2] // 2
-        piece = shard.at[
-            pl.ds(pl.multiple_of(p * rows, 16), rows),
-            lanes(part * full.shape[2] + c * cols, cols),
-        ]
-        for d in (1, 3, 2):
-            remote(piece, block(m, z, p), t.snd.at[m], t.zr.at[m, d - 1], depth[d - 1]).start()
-    own = []
-    for m, (shard, part, full) in enumerate(plan):
-        copy = pltpu.make_async_copy(
-            shard.at[:, lanes(part * full.shape[2], full.shape[2])], full.at[z], t.own.at[m]
-        )
-        copy.start()
-        own.append(copy)
-
-    def source(d):
-        return lax.rem(z + NARROW - d, NARROW)
-
-    def spread(m, d):
-        mine = block(m, source(d), p)
+
+    above, below = (w, jnp.minimum(z + 1, NARROW - 1)), (w, jnp.maximum(z - 1, 0))
+    can_rise, can_sink = z < NARROW - 1, z > 0
+
+    def own_piece(m):
+        shard, r0, c0, _, span = plan[m]
+        start, rows = rows_of(m, p)
+        cols = span // 2
+        return shard.at[pl.ds(pl.multiple_of(r0 + start, 16), rows), lanes(c0 + c * cols, cols)]
+
+    def depart(m):
+        @pl.when(can_rise)
+        def _():
+            remote(
+                own_piece(m), block(m, z, p), t.zs.at[m, 3], t.zr.at[m, 0], above
+            ).start()
+
+        @pl.when(can_sink)
+        def _():
+            remote(
+                own_piece(m), block(m, z, p), t.zs.at[m, 4], t.zr.at[m, 2], below
+            ).start()
+
+    def hop(k):
+        first, last = z == 0, z == NARROW - 1
+        if k == 0:
+            return jnp.where(first, 3, 1)
+        if k == 1:
+            return jnp.where(first | last, 2, 3)
+        return jnp.where(first, 1, jnp.where(last, 3, 2))
+
+    def source(k):
+        return lax.rem(z + NARROW - hop(k), NARROW)
+
+    def relay(m, k):
+        d = hop(k)
+        mine = block(m, source(k), p)
+        rise = can_rise & (d <= z)
+        sink = can_sink & (d > z)
+        return mine, d, rise, sink
+
+    def spread(m, k):
+        mine, d, rise, sink = relay(m, k)
         arrive(mine, t.zr.at[m, d - 1])
-        send(m, mine, t.xr.at[m, d - 1], at.xn)
-        send(m, mine, t.yr.at[m, d - 1], at.yn)
+
+        @pl.when(rise)
+        def _():
+            remote(mine, mine, t.zs.at[m, k], t.zr.at[m, jnp.minimum(d, 2)], above).start()
+
+        @pl.when(sink)
+        def _():
+            remote(mine, mine, t.zs.at[m, k], t.zr.at[m, jnp.maximum(d - 2, 0)], below).start()
+
+        send(m, mine, t.xr.at[m, k], at.xn)
+        send(m, mine, t.yr.at[m, k], at.yn)
         send(m, mine, t.sr.at[m], at.sib)
-
-    def forward(m, d):
-        zz = source(d)
-        arrive(block(m, zz, at.px), t.xr.at[m, d - 1])
-        send(m, block(m, zz, at.px, 0), t.fxr.at[m, d - 1], at.yn)
+        if k == 2 and m + 3 < len(plan):
+            depart(m + 3)
+
+    def forward(m, k):
+        zz = source(k)
+        arrive(block(m, zz, at.px), t.xr.at[m, k])
+        send(m, block(m, zz, at.px, 0), t.fxr.at[m, k], at.yn)
         send(m, block(m, zz, at.px), t.sr.at[m], at.sib)
-        arrive(block(m, zz, at.py), t.yr.at[m, d - 1])
-        send(m, block(m, zz, at.py, 1), t.fyr.at[m, d - 1], at.xn)
+        arrive(block(m, zz, at.py), t.yr.at[m, k])
+        send(m, block(m, zz, at.py, 1), t.fyr.at[m, k], at.xn)
         send(m, block(m, zz, at.py), t.sr.at[m], at.sib)
 
-    def finish(m, d):
-        zz = source(d)
-        arrive(block(m, zz, at.pd, 0), t.fxr.at[m, d - 1])
-        arrive(block(m, zz, at.pd, 1), t.fyr.at[m, d - 1])
+    def finish(m, k):
+        zz = source(k)
+        arrive(block(m, zz, at.pd, 0), t.fxr.at[m, k])
+        arrive(block(m, zz, at.pd, 1), t.fyr.at[m, k])
         send(m, block(m, zz, at.pd), t.sr.at[m], at.sib)
 
-    units = [(m, d) for m in range(len(plan)) for d in (1, 3, 2)]
+    for m in range(3):
+        depart(m)
+    over_z(1, t.rel_h, t.rel)
+    units = [(m, k) for m in range(len(plan)) for k in range(3)]
+    steps = ((spread, 0), (forward, 2), (finish, 4))
     events = []
-    for u in range(len(units) + 2):
-        if u < len(units):
-            events.append((spread, units[u]))
-        if 0 <= u - 1 < len(units):
-            events.append((forward, units[u - 1]))
-        if 0 <= u - 2 < len(units):
-            events.append((finish, units[u - 2]))
+    for u in range(len(units) + 4):
+        for step, lag in steps:
+            if 0 <= u - lag < len(units):
+                events.append((step, units[u - lag]))
     progress = [0]
 
     def pump(count):
@@ -731,24 +771,39 @@
                 progress[0] += 1
 
     def complete(m):
-        goal = events.index((finish, units[3 * m + 2])) + 1
+        goal = events.index((finish, (m, 2))) + 1
         pump(goal - progress[0])
-        full = plan[m][2]
-        arrive(full.at[pl.ds(0, 3), :, pl.ds(0, full.shape[2] // 2)], t.sr.at[m])
-        own[m].wait()
-
-    places = ((0, 384), (384, 384), (768, 384), (1152, 384), (1536, 384), (1920, 384), (2304, 768), (3072, 128), (3200, 128))
+        arrive(plan[m][3].at[pl.ds(0, 3), :, pl.ds(0, plan[m][4] // 2)], t.sr.at[m])
+
+    def fetch(m, held):
+        shard, r0, c0, full, span = plan[m]
+        copies = [
+            pltpu.make_async_copy(
+                shard.at[pl.ds(r0, quarter), pl.ds(c0, span)], held.at[z], t.own.at[m, 0]
+            )
+        ]
+        for d in range(1, NARROW):
+            zz = lax.rem(z + d, NARROW)
+            copies.append(pltpu.make_async_copy(full.at[zz], held.at[zz], t.own.at[m, d]))
+        for copy in copies:
+            copy.start()
+        return copies
+
+    def use(copies):
+        for copy in copies:
+            copy.wait()
 
     def vectors():
         loads[1].wait()
-        loads[2].wait()
-        for k, full in enumerate((t.small, t.rel)):
-            arrive(full.at[pl.ds(0, 3)], t.mr.at[k])
-        for r, (start, size) in enumerate(places):
-            for zz in range(NARROW):
-                t.vec[r : r + 1, zz * size : (zz + 1) * size] = wide(
-                    t.small[zz, 0:8, start : start + size]
-                )[0:1]
+        arrive(t.small.at[pl.ds(0, 3)], t.mr.at[0])
+        for zz in range(NARROW):
+            rows = wide(t.small[zz])
+            for r in range(6):
+                t.vec[r : r + 1, zz * 384 : (zz + 1) * 384] = rows[r : r + 1, 0:384]
+            for r in range(2):
+                spot = slice(zz * 768 + r * 384, zz * 768 + (r + 1) * 384)
+                t.vec[6:7, spot] = rows[6 + r : 7 + r, 0:384]
+                t.vec[7 + r : 8 + r, zz * 128 : (zz + 1) * 128] = rows[r : r + 1, 384:512]
 
     def norm_rows(src, dst, gain_row):
         def one(i, _):
@@ -778,10 +833,12 @@
 
     def make_keys():
         t.kr[...] = low(dot_nn(t.normed[...], flat(t.k)))
+        loads[2].wait()
+        arrive(t.rel.at[pl.ds(0, 3)], t.mr.at[1])
         loads[3].wait()
         table = t.rel[...].reshape(t.rel.shape[0] * t.rel.shape[1], t.rel.shape[2])
         t.rk[...] = low(dot_nn(t.basis[...], table))
-        loads[6].wait()
+        loads[5].wait()
         t.rr[...] = low(dot_nn(t.flip[...], table))
 
     def make_values():
@@ -811,7 +868,7 @@
             soft = low(grown / jnp.sum(grown, axis=1, keepdims=True))
             t.p[2 * pair + side] = soft
             mixed.append(dot_nn(soft, vals))
-        t.mixed[0, :, vs] = low(jnp.where(pair_mask(2 * VAL, VAL), mixed[0], mixed[1]))
+        t.mixed[:, vs] = low(jnp.where(pair_mask(2 * VAL, VAL), mixed[0], mixed[1]))
 
     def give(k, src, dst):
         remote(src, dst, t.ps.at[k], t.pr.at[k], at.sib).start()
@@ -828,18 +885,17 @@
             cols = lanes(n * 512, 512)
             t.hidden[:, cols] = (
                 wide(t.tok[:, cols])
-                + dot_nn(t.mixed[0], columns(t.o, n * 512, 512))
+                + dot_nn(t.mixed[...], columns(t.o, n * 512, 512))
                 + t.vec[2:3, cols]
             )
             return 0
 
         lax.fori_loop(0, 3, one, 0)
-        norm_rows(t.hidden, t.nmid.at[0], 3)
-        give(2, t.nmid.at[0], t.nmid.at[1])
+        norm_rows(t.hidden, t.nmid, 3)
+        give(2, t.nmid, t.nm_h.at[1])
 
     def clip_rows():
         loads[4].wait()
-        loads[5].wait()
 
         def one(i, total):
             rows = pl.ds(pl.multiple_of(i * 32, 32), 32)
@@ -854,24 +910,8 @@
         give(0, t.od.at[:, lanes((1 - c) * half, half)], t.odc.at[1])
 
     def clip(row, values):
-        limit = jnp.where(row < WIN, t.lim[0:1, 0:1], t.lim[0:1, 1:2])
+        limit = jnp.where(row < WIN, t.lim_h[0, 0], t.lim_h[0, 1])
         return jnp.minimum(jnp.maximum(values, -limit), limit)
-
-    def pull_active(h):
-        full = (t.u0, t.u1)[h]
-        half = width // 2
-        delta = t.od[:, h * half : (h + 1) * half]
-
-        def one(zz, _):
-            cols = lanes(zz * 768, 768)
-            part = dot_nt(delta, full[zz])
-            if h == 0:
-                t.ad[:, cols] = part
-            else:
-                t.ad[:, cols] = t.ad[:, cols] + part
-            return 0
-
-        lax.fori_loop(0, NARROW, one, 0)
 
     def inner(h):
         full = (t.i0, t.i1)[h]
@@ -879,80 +919,16 @@
         def one(n, _):
             local = n * 256
             cols = lanes(h * width + local, 256)
-            pre = dot_nn(t.nmid[0], columns(full, local, 256)) + t.vec[6:7, cols]
+            pre = dot_nn(t.nmid[...], columns(full, local, 256)) + t.vec[6:7, cols]
             cdf = 0.5 + 0.5 * lax.erf(pre * (0.5**0.5))
             slope = cdf + pre * jnp.exp(-0.5 * pre * pre) * (2.0 * math.pi) ** -0.5
             t.act[0, :, cols] = low(pre * cdf)
-            delta = low(t.ad[:, cols] * slope)
-            t.idl[h, :, lanes(local, 256)] = delta
-            t.sums[6:7, cols] = jnp.sum(wide(delta), axis=0, keepdims=True)
+            t.slope[:, cols] = low(slope)
             return 0
 
         lax.fori_loop(0, 6, one, 0)
         cols = pl.ds(h * width, width)
         give(3 + h, t.act.at[0, :, cols], t.act.at[1, :, cols])
-
-    def finish_out():
-        def one(n, _):
-            cols = lanes(n * 256, 256)
-            for h, full in enumerate((t.u0, t.u1)):
-                spot = lanes(h * 768 + n * 256, 256)
-                t.lo[:, spot] = low(
-                    t.hidden[:, spot]
-                    + dot_nn(t.act[0], columns(full, n * 256, 256))
-                    + t.vec[5:6, spot]
-                )
-            return 0
-
-        lax.fori_loop(0, 3, one, 0)
-        store(t.lo, t.out_h)
-
-    def pull_mid():
-        for zz in range(NARROW):
-            t.hd[:, zz * 384 : (zz + 1) * 384] = dot_nt(t.idl[0], t.i0[zz]) + dot_nt(
-                t.idl[1], t.i1[zz]
-            )
-
-        def one(i, carry):
-            gain_total, shift_total, bias_total = carry
-            rows = pl.ds(pl.multiple_of(i * 32, 32), 32)
-            v = t.hidden[rows, :]
-            center = v - jnp.mean(v, axis=1, keepdims=True)
-            scale = lax.rsqrt(jnp.mean(center * center, axis=1, keepdims=True) + EPSILON)
-            n = center * scale
-            delta = t.hd[rows, :]
-            e = delta * t.vec[3:4, 0:width]
-            back = scale * (
-                e
-                - jnp.mean(e, axis=1, keepdims=True)
-                - n * jnp.mean(e * n, axis=1, keepdims=True)
-            )
-            full = clip(i * 32, wide(t.cot[rows, :])) + back
-            t.hd[rows, :] = full
-            rounded = low(full)
-            t.bd[rows, :] = rounded
-            return (
-                gain_total + jnp.sum(delta * n, axis=0, keepdims=True),
-                shift_total + jnp.sum(delta, axis=0, keepdims=True),
-                bias_total + jnp.sum(wide(rounded), axis=0, keepdims=True),
-            )
-
-        zero = jnp.zeros((1, width), jnp.float32)
-        gain_total, shift_total, bias_total = lax.fori_loop(
-            0, rows_all // 32, one, (zero, zero, zero)
-        )
-        t.sums[3:4, 0:width] = gain_total
-        t.sums[4:5, 0:width] = shift_total
-        t.sums[2:3, 0:width] = bias_total
-        half = width // 2
-        give(6, t.bd.at[:, lanes((1 - c) * half, half)], t.bdc.at[1])
-        t.bdc[0] = t.bd[:, lanes(c * half, half)]
-        store(t.hd, t.hd_h)
-
-    def pull_mixed():
-        for zz in range(NARROW):
-            t.md[:, zz * 384 : (zz + 1) * 384] = low(dot_nt(t.bd[...], t.o[zz]))
-        store(t.md, t.md_h)
 
     def outer_product(left_ref, right_ref, dst, start, size):
         steps = left_ref.shape[2] // 256
@@ -989,70 +965,96 @@
     norm_rows(t.tok, t.normed, 0)
     give(1, t.normed, t.nn_h.at[1])
     store(t.normed, t.nn_h.at[0])
-    pump(1)
+    store(t.vec, t.vec_h)
+    complete(0)
+    queries_here = fetch(0, t.q)
+    pump(2)
     clip_rows()
-    complete(0)
+    store(t.od, t.od_h)
+    use(queries_here)
     make_queries()
-    store(t.q, t.fq)
     store(t.cq, t.cq_h)
     store(t.pq, t.pq_h)
     complete(1)
+    keys_here = fetch(1, t.k)
+    pump(3)
+    use(keys_here)
     make_keys()
-    store(t.k, t.fk)
     store(t.kr, t.k_h)
     store(t.rr, t.rr_h)
     complete(2)
+    values_here = fetch(2, t.v)
+    pump(2)
+    use(values_here)
     make_values()
-    store(t.v, t.fv)
     store(t.vr, t.v_h)
-    store(t.vec, t.vec_h)
     for pair in range(4):
         heads(pair)
         pump(2)
     store(t.p, t.p_h)
-    give(5, t.mixed.at[0], t.mixed.at[1])
+    give(5, t.mixed, t.mx_h.at[1])
+    store(t.mixed, t.mx_h.at[0])
     complete(3)
+    out_here = fetch(3, t.o)
+    pump(2)
+    use(out_here)
     attend_out()
+    store(t.hidden, t.hid_h)
+    store(t.nmid, t.nm_h.at[0])
     complete(4)
-    pull_active(0)
+    inner_here = fetch(4, t.i0)
+    pump(2)
+    use(inner_here)
+    inner(0)
     complete(5)
-    pull_active(1)
-    complete(6)
-    inner(0)
-    complete(7)
+    inner_here = fetch(5, t.i1)
+    pump(2)
+    use(inner_here)
     inner(1)
-    give(7, t.idl.at[1 - c], t.idc.at[1])
-    t.idc[0] = t.idl[c]
-    finish_out()
-    pull_mid()
-    pull_mixed()
+    store(t.act.at[0], t.act_h)
+    store(t.slope, t.slope_h)
+    pump(2)
     arrive(t.odc.at[1], t.pr.at[0])
     for h in range(2):
         arrive(t.act.at[1, :, pl.ds(0, width)], t.pr.at[3 + h])
     outer_product(t.act, t.odc, t.gu0, 0, 384)
+    pump(2)
     outer_product(t.act, t.odc, t.gu1, 384, 384)
-    arrive(t.nmid.at[1], t.pr.at[2])
-    arrive(t.idc.at[1], t.pr.at[7])
-    outer_product(t.nmid, t.idc, t.gi0, 0, 768)
-    outer_product(t.nmid, t.idc, t.gi1, 768, 768)
-    arrive(t.mixed.at[1], t.pr.at[5])
-    arrive(t.bdc.at[1], t.pr.at[6])
-    outer_product(t.mixed, t.bdc, t.go, 0, 768)
     store(t.sums, t.sums_h)
+    complete(6)
+    complete(7)
 
     arrive(t.nn_h.at[1], t.pr.at[1])
+    arrive(t.nm_h.at[1], t.pr.at[2])
+    arrive(t.mx_h.at[1], t.pr.at[5])
     left(t.odc.at[1], t.ps.at[0])
     left(t.normed, t.ps.at[1])
-    left(t.nmid.at[0], t.ps.at[2])
+    left(t.nmid, t.ps.at[2])
     for h in range(2):
         left(t.act.at[0, :, pl.ds(0, width)], t.ps.at[3 + h])
-    left(t.mixed.at[0], t.ps.at[5])
-    left(t.bdc.at[1], t.ps.at[6])
-    left(t.idc.at[1], t.ps.at[7])
+    left(t.mixed, t.ps.at[5])
     for k, full in enumerate((t.small, t.rel)):
         left(full.at[pl.ds(0, 3)], t.ms.at[k])
-    for m, (_, _, full) in enumerate(plan):
-        left(full.at[pl.ds(0, 3)], t.snd.at[m])
+    for m in range(len(plan)):
+        mine = block(m, z, p)
+        for k in range(3):
+            _, _, rise, sink = relay(m, k)
+
+            @pl.when(rise | sink)
+            def _():
+                left(mine, t.zs.at[m, k])
+
+        @pl.when(can_rise)
+        def _():
+            left(mine, t.zs.at[m, 3])
+
+        @pl.when(can_sink)
+        def _():
+            left(mine, t.zs.at[m, 4])
+
+        full, cols = plan[m][3], plan[m][4] // 2
+        left(full.at[pl.ds(0, 3), :, pl.ds(0, cols)], t.snd.at[m])
+        left(full.at[pl.ds(0, 3), pl.ds(0, 3 * quarter // 4), pl.ds(0, cols)], t.snd.at[m])
     for copy in stored:
         copy.wait()
 
@@ -1061,38 +1063,43 @@
     rows, width = tokens.shape
     bf, f32 = jnp.bfloat16, jnp.float32
     keys = H * KEY
+    quarter = width // 4
+    full = ((NARROW, quarter, width), bf)
+    thin = ((NARROW, quarter, keys), bf)
     out_shape = (
-        ((rows, width), bf),
         ((H, rows, rows), bf),
         ((rows, keys), bf),
         ((rows, keys), bf),
         ((rows, keys), bf),
         ((rows, width), bf),
         ((2 * rows, keys), bf),
+        ((rows, width), f32),
+        ((rows, 2 * width), bf),
+        ((rows, 2 * width), bf),
         ((rows, width), bf),
-        ((rows, width), f32),
         ((2, rows, width), bf),
-        ((NARROW, width // 4, keys), bf),
-        ((NARROW, width // 4, keys), bf),
-        ((NARROW, width // 4, width), bf),
+        ((2, rows, width), bf),
+        ((2, rows, width), bf),
+        thin,
+        thin,
+        full,
+        full,
+        full,
+        full,
+        full,
+        full,
         ((16, 2 * width), f32),
         ((2 * width, width // 4), bf),
         ((2 * width, width // 4), bf),
-        ((width, width // 2), bf),
-        ((width, width // 2), bf),
-        ((width, width // 2), bf),
         ((8, 2 * width), f32),
     )
-    quarter = width // 4
     vmem = (
-        ((NARROW, quarter, keys), bf),
-        ((NARROW, quarter, keys), bf),
-        ((NARROW, quarter, width), bf),
-        ((NARROW, quarter, width), bf),
-        ((NARROW, 2 * quarter, width // 2), bf),
-        ((NARROW, 2 * quarter, width // 2), bf),
-        ((NARROW, quarter, width), bf),
-        ((NARROW, quarter, width), bf),
+        thin,
+        thin,
+        full,
+        full,
+        full,
+        full,
         ((NARROW,) + rel.shape, bf),
         ((NARROW,) + small.shape, bf),
         ((16, 2 * width), f32),
@@ -1107,39 +1114,32 @@
         ((2 * rows, keys), bf),
         ((2 * rows, keys), bf),
         ((H, rows, rows), bf),
-        ((2, rows, width), bf),
+        ((rows, width), bf),
         ((rows, width), f32),
-        ((2, rows, width), bf),
+        ((rows, width), bf),
         ((rows, width), bf),
         ((rows, width), bf),
         ((2, rows, width // 2), bf),
-        ((rows, 2 * width), f32),
         ((2, rows, 2 * width), bf),
-        ((2, rows, width), bf),
-        ((2, rows, width), bf),
-        ((rows, width), f32),
-        ((rows, width), bf),
-        ((2, rows, width // 2), bf),
-        ((rows, width), bf),
-        ((rows, width), bf),
+        ((rows, 2 * width), bf),
         ((2, rows, width // 2), bf),
         ((8, 2 * width), f32),
-        ((8, 128), f32),
     )
     sems = [
         DMA((8, 3)),
+        DMA((8, 5)),
         DMA((8, 3)),
         DMA((8, 3)),
         DMA((8, 3)),
         DMA((8, 3)),
         DMA((8,)),
         DMA((8,)),
-        DMA((8,)),
+        DMA((8, 4)),
         DMA((7,)),
         DMA((2,)),
         DMA((2,)),
-        DMA((8,)),
-        DMA((8,)),
+        DMA((6,)),
+        DMA((6,)),
         DMA((20,)),
         DMA((2,)),
     ]
@@ -1147,7 +1147,7 @@
     return pl.pallas_call(
         forward_kernel,
         out_shape=tuple(jax.ShapeDtypeStruct(s, d) for s, d in out_shape),
-        in_specs=[HBM] * len(ins),
+        in_specs=[HBM, HBM, SMEM] + [HBM] * (len(ins) - 3),
         out_specs=(HBM,) * len(out_shape),
         scratch_shapes=[pltpu.VMEM(s, d) for s, d in vmem] + sems,
         compiler_params=pltpu.CompilerParams(
@@ -1158,27 +1158,42 @@
 
 
 UNITS = 8
+CHAINS = (0, 3)
 
 
 def backward_refs(
     gu0,
     gu1,
-    gi0,
-    gi1,
-    go,
     p_h,
     cq_h,
     pq_h,
     k_h,
     v_h,
     rr_h,
-    md_h,
-    hd_h,
+    hid_h,
+    act_h,
+    slope_h,
+    od_h,
+    nn_h,
+    nm_h,
+    mx_h,
+    fq,
+    fk,
+    fv,
+    fo,
+    fi0,
+    fi1,
+    fu0,
+    fu1,
+    wq,
+    wk,
+    wv,
+    wo,
+    wi,
+    wu,
     tok_h,
-    nn_h,
-    fq_h,
-    fk_h,
-    fv_h,
+    cot_h,
+    lim_h,
     vec_h,
     sums_h,
     flipt_h,
@@ -1189,37 +1204,40 @@
     ov,
     ok,
     oq,
+    out_h,
     tg_h,
     e_h,
     rg_h,
+    gi0,
+    gi1,
+    go,
     gv,
     gk,
     gq,
+    s0,
+    s1,
     p,
     cq,
     pq,
     kr,
     vr,
     rr,
-    md,
-    hd,
-    tok,
-    nn,
-    fq,
-    fk,
-    fv,
+    hid,
+    act,
+    slope,
+    od,
+    cat,
+    idc,
+    cot,
     vec,
     sums,
     flipt,
     turn,
-    qd,
-    kd,
-    vd,
+    bdc,
     qdc,
     kdc,
     vdc,
     nd,
-    tg,
     rg,
     rgk,
     rgg,
@@ -1231,7 +1249,8 @@
     es,
     eo,
     ld,
-    s1,
+    own,
+    s1s,
     r1,
     l1,
     s2,
@@ -1241,6 +1260,9 @@
     s4,
     r4,
     lo,
+    zu,
+    zd,
+    zs,
     ps,
     pr,
     xs,
@@ -1253,23 +1275,26 @@
 
 
 def backward_kernel(*refs):
-    head = 31
-    t = backward_refs(*refs[:head], *refs[head + 5 * UNITS :])
-    keep, got1, got2, got3, last = (
-        refs[head + k * UNITS : head + (k + 1) * UNITS] for k in range(5)
+    head = 46
+    held = 2
+    t = backward_refs(*refs[:head], *refs[head + held + 4 * UNITS :])
+    spare = refs[head : head + held + 4 * UNITS]
+    keep = spare[:held]
+    got1, got2, got3, last = (
+        spare[held + k * UNITS : held + (k + 1) * UNITS] for k in range(4)
     )
     at = position()
     w, z, c, p, x, y = at.w, at.z, at.c, at.p, at.x, at.y
     depth = [(w, lax.rem(z + d, NARROW)) for d in range(1, NARROW)]
-    rows_all, width = t.tok.shape
+    rows_all, width = t.cot.shape
     meet([at.sib, at.xn, at.yn] + depth)
 
     plan = (
         (t.gu0, False, t.ou, 0, width // 2),
         (t.gu1, False, t.ou, width // 4, width // 2),
-        (t.gi0, False, t.oi, 0, width),
-        (t.gi1, False, t.oi, width // 2, width),
-        (t.go, False, t.oo, 0, width // 2),
+        (t.gi0, True, t.oi, 0, width),
+        (t.gi1, True, t.oi, width // 2, width),
+        (t.go, True, t.oo, 0, width // 2),
         (t.gv, True, t.ov, 0, width // 2),
         (t.gk, True, t.ok, 0, H * KEY // 2),
         (t.gq, True, t.oq, 0, H * KEY // 2),
@@ -1283,9 +1308,16 @@
 
     def stage1(m):
         for h, target in ((0, at.xn), (1, at.yn)):
-            remote(half(m, h, False), got1[m].at[h], t.s1.at[m, h], t.r1.at[m, h], target).start()
+            remote(half(m, h, False), got1[m].at[h], t.s1s.at[m, h], t.r1.at[m, h], target).start()
             if not plan[m][1]:
                 pltpu.make_async_copy(half(m, h, True), keep[m].at[h], t.l1.at[m, h]).start()
+
+    def kept(m, h, zz, o):
+        if not plan[m][1]:
+            return keep[m].at[h, zz, o]
+        if h == 0:
+            return plan[m][0].at[zz, o, x, 0]
+        return plan[m][0].at[zz, y, o, 1]
 
     def stage2(m):
         for h, target, mine in ((0, at.yn, y), (1, at.xn, x)):
@@ -1295,18 +1327,14 @@
 
             def add(k, _, h=h):
                 zz, o = lax.div(k, 2), lax.rem(k, 2)
-                if not plan[m][1]:
-                    own = keep[m][h, zz, o]
-                elif h == 0:
-                    own = plan[m][0][zz, o, x, 0]
-                else:
-                    own = plan[m][0][zz, y, o, 1]
-                keep[m][h, zz, o] = low(wide(own) + wide(got1[m][h, zz, o]))
+                spot = kept(m, h, zz, o)
+                spot[...] = low(wide(spot[...]) + wide(got1[m][h, zz, o]))
                 return 0
 
             lax.fori_loop(0, 2 * NARROW, add, 0)
+            every = pl.ds(0, NARROW)
             remote(
-                keep[m].at[h, :, 1 - mine], got2[m].at[h], t.s2.at[m, h], t.r2.at[m, h], target
+                kept(m, h, every, 1 - mine), got2[m].at[h], t.s2.at[m, h], t.r2.at[m, h], target
             ).start()
 
     def stage3(m):
@@ -1314,7 +1342,7 @@
             arrive(got2[m].at[h], t.r2.at[m, h])
 
             def add(zz, _, h=h, mine=mine):
-                got2[m][h, zz] = low(wide(keep[m][h, zz, mine]) + wide(got2[m][h, zz]))
+                got2[m][h, zz] = low(wide(kept(m, h, zz, mine)[...]) + wide(got2[m][h, zz]))
                 return 0
 
             lax.fori_loop(0, NARROW, add, 0)
@@ -1346,6 +1374,9 @@
             for d in range(3):
                 total = total + wide(got3[m][d, h])
             last[m][h * rows : (h + 1) * rows, :] = low(total)
+        share(m)
+
+    def share(m):
         mine = piece(m, p)
         remote(last[m], mine, t.s4.at[m], t.r4.at[m, 0], at.xn).start()
         remote(last[m], mine, t.s4.at[m], t.r4.at[m, 1], at.yn).start()
@@ -1366,30 +1397,275 @@
         some = piece(m, at.pd)
         remote(some, some, t.s4.at[m], t.r4.at[m, 4], at.sib).start()
 
+    above, under = (w, jnp.minimum(z + 1, NARROW - 1)), (w, jnp.maximum(z - 1, 0))
+    top = NARROW - 1
+
+    def chain_start(m):
+        g, room = plan[m][0], got1[m]
+        bring(m, 0, rise_to(1))
+        bring(m, 1, sink_to(1))
+
+        @pl.when(z == 0)
+        def _():
+            for i in range(top):
+                there = top - i
+                remote(
+                    g.at[there], room.at[there], t.zs.at[m, i], t.zu.at[m, there], above
+                ).start()
+
+        @pl.when(z == top)
+        def _():
+            for i in range(top):
+                spot = NARROW if i == top - 1 else i
+                remote(g.at[i], room.at[spot], t.zs.at[m, i], t.zd.at[m, i], under).start()
+
+    def bring(m, spot, there):
+        if not plan[m][1]:
+            pltpu.make_async_copy(
+                plan[m][0].at[there], keep[m].at[spot], t.l1.at[m, spot]
+            ).start()
+
+    def brought(m, spot):
+        if not plan[m][1]:
+            pltpu.make_async_copy(keep[m].at[spot], keep[m].at[spot], t.l1.at[m, spot]).wait()
+
+    def own_part(m, spot, there):
+        return plan[m][0].at[there] if plan[m][1] else keep[m].at[spot]
+
+    def join(m, spot, there):
+        own = own_part(m, spot, there)
+
+        def add(k, _):
+            a, b, h = lax.div(k, 4), lax.rem(lax.div(k, 2), 2), lax.rem(k, 2)
+            got1[m][there, a, b, h] = low(wide(got1[m][there, a, b, h]) + wide(own[a, b, h]))
+            return 0
+
+        lax.fori_loop(0, 8, add, 0)
+
+    def rising(slot):
+        return (z >= 1) & (z <= slot)
+
+    def sinking(slot):
+        return (z < top) & (z >= top - slot)
+
+    def rise_to(slot):
+        return jnp.minimum(top + z - slot, top)
+
+    def sink_to(slot):
+        return jnp.maximum(slot - top + z, 0)
+
+    def chain_step(m, slot):
+        room = got1[m]
+        brought(m, 0)
+        brought(m, 1)
+
+        @pl.when(rising(slot))
+        def _():
+            there = rise_to(slot)
+            arrive(room.at[there], t.zu.at[m, there])
+            join(m, 0, there)
+            remote(
+                room.at[there], room.at[there], t.zs.at[m, 2 + slot], t.zu.at[m, there], above
+            ).start()
+
+        @pl.when(sinking(slot))
+        def _():
+            there = sink_to(slot)
+            arrive(room.at[there], t.zd.at[m, there])
+            join(m, 1, there)
+            spot = NARROW if slot == 2 else there
+            remote(
+                room.at[there], room.at[spot], t.zs.at[m, 4 + slot], t.zd.at[m, there], under
+            ).start()
+
+        if slot == 1:
+            bring(m, 0, rise_to(2))
+            bring(m, 1, sink_to(2))
+        else:
+            bring(m, 0, z)
+
+    def chain_end(m):
+        room = got1[m]
+        brought(m, 0)
+
+        @pl.when(z > 0)
+        def _():
+            arrive(room.at[z], t.zu.at[m, z])
+            join(m, 0, z)
+
+        @pl.when(z < top)
+        def _():
+            arrive(room.at[NARROW], t.zd.at[m, z])
+
+        def add(k, _, fresh=False):
+            a, b, h = lax.div(k, 4), lax.rem(lax.div(k, 2), 2), lax.rem(k, 2)
+            own = own_part(m, 0, z)[a, b, h] if fresh else room[z, a, b, h]
+            room[z, a, b, h] = low(wide(own) + wide(room[NARROW, a, b, h]))
+            return 0
+
+        @pl.when((z > 0) & (z < top))
+        def _():
+            lax.fori_loop(0, 8, add, 0)
+
+        @pl.when(z == 0)
+        def _():
+            lax.fori_loop(0, 8, functools.partial(add, fresh=True), 0)
+
+        remote(
+            room.at[z, :, 1 - x, 0], got2[m].at[0], t.s1s.at[m, 0], t.r1.at[m, 0], at.xn
+        ).start()
+        remote(
+            room.at[z, 1 - y, :, 1], got2[m].at[1], t.s1s.at[m, 1], t.r1.at[m, 1], at.yn
+        ).start()
+
+    def chain_plane(m):
+        room = got1[m]
+        for h, target in ((0, at.yn), (1, at.xn)):
+            arrive(got2[m].at[h], t.r1.at[m, h])
+            for o in range(2):
+                spot = room.at[z, o, x, 0] if h == 0 else room.at[z, y, o, 1]
+                spot[...] = low(wide(spot[...]) + wide(got2[m][h, o]))
+            away = room.at[z, 1 - y, x, 0] if h == 0 else room.at[z, y, 1 - x, 1]
+            remote(away, got3[m].at[h], t.s2.at[m, h], t.r2.at[m, h], target).start()
+
+    def chain_last(m):
+        rows = last[m].shape[0] // 2
+        for h in range(2):
+            arrive(got3[m].at[h], t.r2.at[m, h])
+            last[m][h * rows : (h + 1) * rows, :] = low(
+                wide(got1[m][z, y, x, h]) + wide(got3[m][h])
+            )
+        share(m)
+
     sources = (
+        (t.act_h, t.act),
+        (t.od_h, t.od),
+        (t.slope_h, t.slope),
+        (t.hid_h, t.hid),
+        (t.vec_h, t.vec),
+        (t.sums_h, t.sums),
+        (t.cot_h, t.cot),
+        (t.nm_h, t.cat),
         (t.p_h, t.p),
         (t.v_h, t.vr),
-        (t.md_h, t.md),
         (t.k_h, t.kr),
         (t.cq_h, t.cq),
         (t.pq_h, t.pq),
         (t.rr_h, t.rr),
         (t.turn_h, t.turn),
         (t.flipt_h, t.flipt),
-        (t.nn_h, t.nn),
-        (t.fv_h, t.fv),
-        (t.fk_h, t.fk),
-        (t.fq_h, t.fq),
-        (t.tok_h, t.tok),
-        (t.hd_h, t.hd),
-        (t.vec_h, t.vec),
-        (t.sums_h, t.sums),
-    )
-    stage1(0)
+        (t.tok_h, t.cot),
+        (t.mx_h, t.cat),
+        (t.nn_h, t.idc),
+    )
+    quarter = width // 4
+
+    def fetch(k, full, shard, held, row=0, col=0):
+        span = held.shape[2]
+        copies = [
+            pltpu.make_async_copy(
+                shard.at[pl.ds(row, quarter), pl.ds(col, span)], held.at[z], t.own.at[k, 0]
+            )
+        ]
+        for d in range(1, NARROW):
+            zz = lax.rem(z + d, NARROW)
+            copies.append(pltpu.make_async_copy(full.at[zz], held.at[zz], t.own.at[k, d]))
+        for copy in copies:
+            copy.start()
+        return copies
+
+    def use(copies):
+        for copy in copies:
+            copy.wait()
+
+    chain_start(0)
     stage1(1)
+    here0 = fetch(0, t.fu0, t.wu, t.s0)
+    here1 = fetch(1, t.fu1, t.wu, t.s1, row=quarter)
     loads = [pltpu.make_async_copy(s, d, t.ld.at[k]) for k, (s, d) in enumerate(sources)]
-    for copy in loads:
-        copy.start()
+    for k in (*range(9), *range(10, 16)):
+        loads[k].start()
+
+    def give(k, src, dst):
+        remote(src, dst, t.ps.at[k], t.pr.at[k], at.sib).start()
+
+    def clip(row, values):
+        limit = jnp.where(row < WIN, t.lim_h[0, 0], t.lim_h[0, 1])
+        return jnp.minimum(jnp.maximum(values, -limit), limit)
+
+    def leave_mlp(h):
+        full = (t.s0, t.s1)[h]
+        spots = [
+            slice(2 * quarter * zz + quarter * h, 2 * quarter * zz + quarter * (h + 1))
+            for zz in range(NARROW)
+        ]
+        active = jnp.concatenate([t.act[:, spot] for spot in spots], axis=1)
+
+        def one(n, _):
+            cols = lanes(n * 512, 512)
+            part = dot_nn(active, full[:, :, cols].reshape(width, 512))
+            if h == 0:
+                t.nd[:, cols] = t.hid[:, cols] + part + t.vec[5:6, cols]
+            else:
+                t.vr[:, cols] = low(t.nd[:, cols] + part)
+            return 0
+
+        lax.fori_loop(0, 3, one, 0)
+        for zz, spot in enumerate(spots):
+            delta = low(dot_nt(t.od[...], full[zz]) * wide(t.slope[:, spot]))
+            t.act[:, spot] = delta
+            t.sums[6:7, spot] = jnp.sum(wide(delta), axis=0, keepdims=True)
+
+    def pull_mid():
+        for zz in range(NARROW):
+            t.nd[:, zz * quarter : (zz + 1) * quarter] = dot_nt(
+                t.act[:, 0:width], t.s0[zz]
+            ) + dot_nt(t.act[:, width : 2 * width], t.s1[zz])
+
+        def one(i, carry):
+            gain_total, shift_total, bias_total = carry
+            rows = pl.ds(pl.multiple_of(i * 32, 32), 32)
+            v = t.hid[rows, :]
+            center = v - jnp.mean(v, axis=1, keepdims=True)
+            scale = lax.rsqrt(jnp.mean(center * center, axis=1, keepdims=True) + EPSILON)
+            n = center * scale
+            delta = t.nd[rows, :]
+            e = delta * t.vec[3:4, 0:width]
+            back = scale * (
+                e
+                - jnp.mean(e, axis=1, keepdims=True)
+                - n * jnp.mean(e * n, axis=1, keepdims=True)
+            )
+            full = clip(i * 32, wide(t.cot[rows, :])) + back
+            t.hid[rows, :] = full
+            rounded = low(full)
+            bd[rows, :] = rounded
+            return (
+                gain_total + jnp.sum(delta * n, axis=0, keepdims=True),
+                shift_total + jnp.sum(delta, axis=0, keepdims=True),
+                bias_total + jnp.sum(wide(rounded), axis=0, keepdims=True),
+            )
+
+        zero = jnp.zeros((1, width), jnp.float32)
+        gain_total, shift_total, bias_total = lax.fori_loop(
+            0, rows_all // 32, one, (zero, zero, zero)
+        )
+        t.sums[3:4, 0:width] = gain_total
+        t.sums[4:5, 0:width] = shift_total
+        t.sums[2:3, 0:width] = bias_total
+        half = width // 2
+        give(1, bd.at[:, lanes((1 - c) * half, half)], t.bdc.at[1])
+        t.bdc[0] = bd[:, lanes(c * half, half)]
+
+    def pull_mixed():
+        for zz in range(NARROW):
+            md[:, zz * quarter : (zz + 1) * quarter] = low(dot_nt(bd[...], t.s0[zz]))
+
+    bd = t.slope.at[:, 0:width]
+    md = t.od
+    vd = t.act.at[:, 0:width]
+    qd = t.act.at[:, width : width + H * KEY]
+    kd = t.act.at[:, width + H * KEY : width + 2 * H * KEY]
 
     def lane_mask(size, split, rows=rows_all):
         return lax.broadcasted_iota(jnp.int32, (rows, size), 1) < split
@@ -1397,7 +1673,7 @@
     def heads(pair):
         qs = slice(pair * 2 * KEY, (pair + 1) * 2 * KEY)
         vs = slice(pair * 2 * VAL, (pair + 1) * 2 * VAL)
-        vals, mixed = t.vr[:, vs], t.md[:, vs]
+        vals, mixed = t.vr[:, vs], md[:, vs]
         keys, rel, cq, pq = t.kr[:, qs], t.rr[:, qs], t.cq[:, qs], t.pq[:, qs]
         first = lane_mask(2 * VAL, VAL)
         parts = []
@@ -1419,53 +1695,56 @@
                     dot_tn(slid, pq),
                 )
             )
-        t.vd[:, vs] = low(jnp.where(first, parts[0][0], parts[1][0]))
+        vd[:, vs] = low(jnp.where(first, parts[0][0], parts[1][0]))
         narrow = lane_mask(2 * KEY, KEY)
         content = jnp.where(narrow, parts[0][1], parts[1][1])
         place = jnp.where(narrow, parts[0][3], parts[1][3])
-        t.kd[:, qs] = low(jnp.where(narrow, parts[0][2], parts[1][2]))
+        kd[:, qs] = low(jnp.where(narrow, parts[0][2], parts[1][2]))
         rel_delta = low(
             jnp.where(lane_mask(2 * KEY, KEY, 2 * rows_all), parts[0][4], parts[1][4])
         )
-        t.qd[:, qs] = low(content + place) * jnp.asarray(KEY ** (-0.5), jnp.bfloat16)
+        qd[:, qs] = low(content + place) * jnp.asarray(KEY ** (-0.5), jnp.bfloat16)
         t.rg[:, qs] = dot_nn(t.flipt[...], rel_delta)
         t.sums[7:8, qs] = jnp.sum(content, axis=0, keepdims=True)
-        keys_all = H * KEY
         there = slice(keys_all + pair * 2 * KEY, keys_all + (pair + 1) * 2 * KEY)
         t.sums[7:8, there] = jnp.sum(place, axis=0, keepdims=True)
 
     def trade():
-        for k, (full, pair) in enumerate(((t.vd, t.vdc), (t.kd, t.kdc), (t.qd, t.qdc))):
+        for k, (full, pair) in enumerate(((vd, t.vdc), (kd, t.kdc), (qd, t.qdc))):
             cols = full.shape[1] // 2
             away = full.at[:, lanes((1 - c) * cols, cols)]
-            remote(away, pair.at[1], t.ps.at[k], t.pr.at[k], at.sib).start()
+            give(2 + k, away, pair.at[1])
             pair[0] = full[:, lanes(c * cols, cols)]
         cols = t.rg.shape[1] // 2
         t.rgo[...] = low(t.rg[:, lanes((1 - c) * cols, cols)]).reshape(t.rgo.shape)
         remote(t.rgo, t.rgg.at[0], t.xs.at[0], t.xr.at[0], at.sib).start()
         t.rgk[0] = low(t.rg[:, lanes(c * cols, cols)]).reshape(t.rgo.shape)
 
-    def outer_product(pair, dst):
+    def outer_product(rows_from, pair, dst, start=0):
+        size = dst.shape[5]
+
         def one(zz, _):
-            lhs = t.nn[:, :, lanes(zz * 384, 384)].reshape(2 * rows_all, 384)
-            rhs = pair[...].reshape(2 * rows_all, pair.shape[2])
+            lhs = rows_from[:, :, lanes(zz * quarter, quarter)].reshape(2 * rows_all, quarter)
+            rhs = pair[:, :, start : start + size].reshape(2 * rows_all, size)
             dst[zz] = low(dot_tn(lhs, rhs)).reshape(dst.shape[1:])
             return 0
 
         lax.fori_loop(0, NARROW, one, 0)
+
+    keys_all = H * KEY
 
     def pull_tokens():
         for zz in range(NARROW):
             t.nd[:, zz * 384 : (zz + 1) * 384] = (
-                dot_nt(t.qd[...], t.fq[zz])
-                + dot_nt(t.kd[...], t.fk[zz])
-                + dot_nt(t.vd[...], t.fv[zz])
+                dot_nt(qd[...], t.s0[zz, :, 0:keys_all])
+                + dot_nt(kd[...], t.s0[zz, :, keys_all : 2 * keys_all])
+                + dot_nt(vd[...], t.s1[zz])
             )
 
         def one(i, carry):
             gain_total, shift_total = carry
             rows = pl.ds(pl.multiple_of(i * 32, 32), 32)
-            v = wide(t.tok[rows, :])
+            v = wide(t.cot[rows, :])
             center = v - jnp.mean(v, axis=1, keepdims=True)
             scale = lax.rsqrt(jnp.mean(center * center, axis=1, keepdims=True) + EPSILON)
             n = center * scale
@@ -1476,7 +1755,7 @@
                 - jnp.mean(e, axis=1, keepdims=True)
                 - n * jnp.mean(e * n, axis=1, keepdims=True)
             )
-            t.tg[rows, :] = low(t.hd[rows, :] + back)
+            t.od[rows, :] = low(t.hid[rows, :] + back)
             return (
                 gain_total + jnp.sum(delta * n, axis=0, keepdims=True),
                 shift_total + jnp.sum(delta, axis=0, keepdims=True),
@@ -1536,94 +1815,172 @@
         copy.start()
         stored.append(copy)
 
-    for copy in loads[:9]:
+    for copy in loads[:6]:
         copy.wait()
-    loads[16].wait()
+    use(here0)
+    leave_mlp(0)
+    use(here1)
+    leave_mlp(1)
+    store(t.vr, t.out_h)
+    give(0, t.act.at[:, lanes((1 - c) * width, width)], t.idc.at[1])
+    t.idc[0] = t.act[:, lanes(c * width, width)]
+    here0 = fetch(2, t.fi0, t.wi, t.s0)
+    here1 = fetch(3, t.fi1, t.wi, t.s1, col=width)
+    loads[7].wait()
+    arrive(t.idc.at[1], t.pr.at[0])
+    outer_product(t.cat, t.idc, t.gi0)
+    stage1(2)
+    chain_step(0, 1)
+    outer_product(t.cat, t.idc, t.gi1, width // 2)
+    loads[17].start()
+    loads[18].start()
+    stage2(1)
+    loads[6].wait()
+    use(here0)
+    use(here1)
+    pull_mid()
+    stored[0].wait()
+    loads[9].start()
+    loads[16].start()
+    here0 = fetch(4, t.fo, t.wo, t.s0)
+    here1 = fetch(5, t.fv, t.wv, t.s1)
+    use(here0)
+    pull_mixed()
+    here0 = fetch(6, t.fq, t.wq, t.s0.at[:, :, 0:keys_all])
+    here2 = fetch(7, t.fk, t.wk, t.s0.at[:, :, keys_all : 2 * keys_all])
+    loads[17].wait()
+    arrive(t.bdc.at[1], t.pr.at[1])
+    outer_product(t.cat, t.bdc, t.go)
+    stage1(4)
+    stage3(1)
+    chain_start(3)
+    for copy in loads[8:16]:
+        copy.wait()
+    left(t.idc.at[1], t.ps.at[0])
     heads(0)
+    chain_step(0, 2)
+    stage2(2)
     heads(1)
-    stage2(0)
-    stage1(2)
     heads(2)
+    chain_end(0)
     heads(3)
     trade()
-    stage2(1)
-    stage1(3)
-    stage3(0)
-    loads[9].wait()
+    loads[18].wait()
+    loads[16].wait()
     for k, (pair, dst) in enumerate(((t.vdc, t.gv), (t.kdc, t.gk), (t.qdc, t.gq))):
-        arrive(pair.at[1], t.pr.at[k])
-        outer_product(pair, dst)
+        arrive(pair.at[1], t.pr.at[2 + k])
+        outer_product(t.idc, pair, dst)
+        stage1(5 + k)
+    stage2(4)
     rel_sums[1](0)
-    for copy in loads[10:16]:
-        copy.wait()
-    stage2(2)
-    stage1(4)
-    stage3(1)
-    stage4(0)
+    use(here0)
+    use(here1)
+    use(here2)
     pull_tokens()
-    store(t.tg, t.tg_h)
+    store(t.od, t.tg_h)
     t.ek[0] = t.eb[...]
     row_sums[0]()
-    for u in range(3, UNITS + 5):
-        if u < UNITS:
-            stage2(u)
-            if u + 2 < UNITS:
-                stage1(u + 2)
-        if u - 3 < 3:
-            if u - 3 < 2:
-                rel_sums[1](u - 2)
-            else:
-                rel_sums[2]()
-            row_sums[1](u - 3)
-        if u == 6:
-            row_sums[2]()
-            store(t.eo, t.e_h)
-            store(t.rg.at[0:48, 0:256], t.rg_h.at[c])
-            remote(t.rg.at[0:48, 0:256], t.rg_h.at[c], t.xs.at[6], t.xr.at[6], at.sib).start()
-        if u - 1 < UNITS:
-            stage3(u - 1)
-        if u - 2 < UNITS:
-            stage4(u - 2)
-        if 0 <= u - 3 < UNITS:
-            stage5(u - 3)
-        if 0 <= u - 4 < UNITS:
-            stage6(u - 4)
+    stage3(2)
+    chain_step(3, 1)
+    chain_plane(0)
+    stage4(1)
+    rel_sums[1](1)
+    row_sums[1](0)
+    stage2(5)
+    stage3(4)
+    chain_last(0)
+    stage5(1)
+    rel_sums[1](2)
+    row_sums[1](1)
+    chain_step(3, 2)
+    stage2(6)
+    stage2(7)
+    stage6(1)
+    stage5(0)
+    row_sums[1](2)
+    stage3(5)
+    stage3(6)
+    stage3(7)
+    stage4(2)
+    stage6(0)
+    chain_end(3)
+    rel_sums[2]()
+    row_sums[2]()
+    store(t.eo, t.e_h)
+    store(t.rg.at[0:48, 0:256], t.rg_h.at[c])
+    remote(t.rg.at[0:48, 0:256], t.rg_h.at[c], t.xs.at[6], t.xr.at[6], at.sib).start()
+    stage4(4)
+    stage5(2)
+    chain_plane(3)
+    stage4(5)
+    stage5(4)
+    stage6(2)
+    chain_last(3)
+    stage4(6)
+    stage4(7)
+    stage5(5)
+    stage6(4)
+    stage5(3)
+    stage5(6)
+    stage5(7)
+    stage6(5)
+    stage6(3)
+    stage6(6)
+    stage6(7)
 
     for m in range(UNITS):
         _, _, out, _, _ = plan[m]
         cols = last[m].shape[1]
         arrive(out.at[:, pl.ds(0, cols)], t.r4.at[m, 4])
         arrive(last[m], t.lo.at[m])
-        for h in range(2):
-            left(got1[m].at[h], t.s1.at[m, h])
-            left(got2[m].at[h], t.s2.at[m, h])
-        for d in range(3):
-            left(got3[m].at[d], t.s3.at[m, d])
+        if m in CHAINS:
+            room = got1[m]
+            for i in range(top):
+
+                @pl.when((z == 0) | (z == top))
+                def _():
+                    left(room.at[0], t.zs.at[m, i])
+
+            for slot in (1, 2):
+
+                @pl.when(rising(slot))
+                def _():
+                    left(room.at[0], t.zs.at[m, 2 + slot])
+
+                @pl.when(sinking(slot))
+                def _():
+                    left(room.at[0], t.zs.at[m, 4 + slot])
+
+            for h in range(2):
+                left(got2[m].at[h], t.s1s.at[m, h])
+                left(got3[m].at[h], t.s2.at[m, h])
+        else:
+            for h in range(2):
+                left(got1[m].at[h], t.s1s.at[m, h])
+                left(got2[m].at[h], t.s2.at[m, h])
+            for d in range(3):
+                left(got3[m].at[d], t.s3.at[m, d])
         left(out.at[:, pl.ds(0, cols)], t.s4.at[m])
         left(out.at[pl.ds(0, 3 * (out.shape[0] // 4)), pl.ds(0, cols)], t.s4.at[m])
-    for k, pair in enumerate((t.vdc, t.kdc, t.qdc)):
-        left(pair.at[1], t.ps.at[k])
+    for k, pair in enumerate((t.bdc, t.vdc, t.kdc, t.qdc)):
+        left(pair.at[1], t.ps.at[1 + k])
     for got, over, sends in ((t.rgg, t.rgs, t.xs), (t.eg, t.es, t.ws)):
         for k in range(3):
             left(got.at[k], sends.at[k])
             left(over.at[k], sends.at[3 + k])
     left(t.rg.at[0:48, 0:256], t.xs.at[6])
     arrive(t.rg_h.at[1 - c], t.xr.at[6])
-    for copy in stored:
+    for copy in stored[1:]:
         copy.wait()
 
 
-def backward_pass(grads, saved, tables):
+def backward_pass(grads, saved, weights, shards, rest):
     bf, f32 = jnp.bfloat16, jnp.float32
-    tokens = saved[8]
-    rows, width = tokens.shape
+    rows, width = rest[0].shape
     keys = H * KEY
     views = [g.reshape(4, 2, 2, 2, g.shape[0] // 32, g.shape[1]) for g in grads]
-    shapes = [(g.shape[0], g.shape[1]) for g in grads] + [
-        (width, width // 2),
-        (width, keys // 2),
-        (width, keys // 2),
-    ]
+    shapes = [(g.shape[0], g.shape[1]) for g in grads] + [(width, width // 2)] * 4
+    shapes += [(width, keys // 2)] * 2
     out_shape = (
         ((width // 2, width), bf),
         ((width // 4, 2 * width), bf),
@@ -1632,26 +1989,35 @@
         ((width // 4, keys), bf),
         ((width // 4, keys), bf),
         ((rows, width), bf),
+        ((rows, width), bf),
         ((8, 768), f32),
         ((2, 48, 256), f32),
     )
-    vmem = []
-    for lead in ((2, 4, 2), (2, 4, 2), (2, 4), (3, 2)):
-        vmem += [(lead + (r // 32, n), bf) for r, n in shapes]
+    vmem = [
+        (((2, 2, 2, 2) if m in CHAINS else (2, 4, 2)) + (r // 32, n), bf)
+        for m, (r, n) in enumerate(shapes[: len(grads)])
+    ]
+    for plain, chain in (
+        ((2, 4, 2), (5, 2, 2, 2)),
+        ((2, 4), (2, 2)),
+        ((3, 2), (2,)),
+    ):
+        vmem += [
+            ((chain if m in CHAINS else plain) + (r // 32, n), bf)
+            for m, (r, n) in enumerate(shapes)
+        ]
     vmem += [((r // 16, n), bf) for r, n in shapes]
-    vmem += [((4, 2, 2, 2, r // 32, n), bf) for r, n in shapes[5:]]
-    vmem += [(s.shape, s.dtype) for s in saved[:9]]
-    vmem += [(s.shape, s.dtype) for s in saved[9:]]
-    vmem += [(s.shape, s.dtype) for s in tables]
+    vmem += [((4, 2, 2, 2, r // 32, n), bf) for r, n in shapes[len(grads) :]]
+    vmem += [((NARROW, width // 4, width), bf)] * 2
+    vmem += [(a.shape, a.dtype) for a in saved[:10]]
+    vmem += [((2, rows, width), bf)] * 2
+    vmem += [(a.shape, a.dtype) for a in rest[1:] if a.size > 2]
     vmem += [
-        ((rows, keys), bf),
-        ((rows, keys), bf),
-        ((rows, width), bf),
+        ((2, rows, width // 2), bf),
         ((2, rows, keys // 2), bf),
         ((2, rows, keys // 2), bf),
         ((2, rows, width // 2), bf),
         ((rows, width), f32),
-        ((rows, width), bf),
         ((F, keys), f32),
         ((4, 4, 48, 256), bf),
         ((3, 4, 48, 256), bf),
@@ -1664,7 +2030,8 @@
         ((8, 768), f32),
     ]
     sems = [
-        DMA((17,)),
+        DMA((20,)),
+        DMA((8, 4)),
         DMA((UNITS, 2)),
         DMA((UNITS, 2)),
         DMA((UNITS, 2)),
@@ -1675,19 +2042,22 @@
         DMA((UNITS,)),
         DMA((UNITS, 5)),
         DMA((UNITS,)),
-        DMA((3,)),
-        DMA((3,)),
+        DMA((UNITS, NARROW)),
+        DMA((UNITS, NARROW)),
+        DMA((UNITS, 7)),
+        DMA((5,)),
+        DMA((5,)),
         DMA((7,)),
         DMA((7,)),
         DMA((6,)),
         DMA((6,)),
-        DMA((3,)),
+        DMA((4,)),
     ]
-    ins = (*views, *saved, *tables)
+    ins = (*views, *saved, *weights, *shards, *rest)
     return pl.pallas_call(
         backward_kernel,
         out_shape=tuple(jax.ShapeDtypeStruct(s, d) for s, d in out_shape),
-        in_specs=[HBM] * len(ins),
+        in_specs=[SMEM if a.size == 2 else HBM for a in ins],
         out_specs=(HBM,) * len(out_shape),
         scratch_shapes=[pltpu.VMEM(s, d) for s, d in vmem] + sems,
         compiler_params=pltpu.CompilerParams(
@@ -1695,6 +2065,97 @@
         ),
         name="backward_pass",
     )(*ins)
+
+
+def finish_kernel(count, *refs):
+    ins, (rows_h, rel_h), passed = refs[:count], refs[count : count + 2], refs[count + 2 : count + 4]
+    refs = refs[count + 4 :]
+    outs, relative, kept, vectors = (
+        refs[:count],
+        refs[count],
+        refs[count + 1 : count + 3],
+        refs[count + 3 : count + 12],
+    )
+    refs = refs[count + 12 :]
+    low_in, f32_out, through = refs[:count], refs[count : 2 * count], refs[2 * count : 2 * count + 2]
+    into, out = refs[2 * count + 2 :]
+    loads = [
+        pltpu.make_async_copy(src, dst, into.at[k])
+        for k, (src, dst) in enumerate(zip((*ins, *passed), (*low_in, *through)))
+    ]
+    for copy in loads:
+        copy.start()
+    stored = []
+
+    def store(src, dst):
+        copy = pltpu.make_async_copy(src, dst, out.at[len(stored)])
+        copy.start()
+        stored.append(copy)
+
+    size = relative.shape[1] // 2
+    relative[:, 0:size] = rel_h[0]
+    relative[:, size : 2 * size] = rel_h[1]
+    for k, vector in enumerate(vectors):
+        n = vector.shape[0]
+        row, start = (7, 128 * (k - 7)) if k >= 7 else (k, 0)
+        vector[...] = rows_h[row : row + 1, start : start + n].reshape(n)
+    for k in (count, count + 1):
+        loads[k].wait()
+        store(through[k - count], kept[k - count])
+    for k in range(count):
+        loads[k].wait()
+        src, dst, res = low_in[k], f32_out[k], outs[k]
+        half = src.shape[0] // 2
+        for part in range(2):
+
+            def one(i, _):
+                spot = pl.ds(pl.multiple_of(part * half + i * 32, 32), 32)
+                dst[spot, :] = wide(src[spot, :])
+                return 0
+
+            lax.fori_loop(0, half // 32, one, 0)
+            spot = pl.ds(part * half, half)
+            store(dst.at[spot], res.at[spot])
+    for copy in stored:
+        copy.wait()
+
+
+def finish_grads(sums, rows, rel, layer_out, tokens_grad):
+    f32 = jnp.float32
+    vmem = pl.BlockSpec(memory_space=pltpu.VMEM)
+    count = len(sums)
+    lengths = (384, 384, 384, 384, 384, 384, 768, 128, 128)
+    shapes = [(a.shape, f32) for a in sums] + [((rel.shape[1], 2 * rel.shape[2]), f32)]
+    shapes += [(a.shape, a.dtype) for a in (layer_out, tokens_grad)]
+    shapes += [((n,), f32) for n in lengths]
+    through = [(a.shape, a.dtype) for a in (layer_out, tokens_grad)]
+    scratch = [(a.shape, a.dtype) for a in sums] + [(a.shape, f32) for a in sums] + through
+    return pl.pallas_call(
+        lambda *refs: finish_kernel(count, *refs),
+        out_shape=tuple(jax.ShapeDtypeStruct(s, d) for s, d in shapes),
+        in_specs=[HBM] * count + [vmem] * 2 + [HBM] * 2,
+        out_specs=(HBM,) * count + (vmem,) + (HBM,) * 2 + (vmem,) * len(lengths),
+        scratch_shapes=[pltpu.VMEM(s, d) for s, d in scratch]
+        + [DMA((count + 2,)), DMA((2 * count + 2,))],
+        compiler_params=pltpu.CompilerParams(vmem_limit_bytes=60 << 20),
+        name="finish_grads",
+    )(*sums, rows, rel, layer_out, tokens_grad)
+
+
+def basis_rows(length, features):
+    f32 = np.float32
+    family = features // 6
+    offsets = np.arange(2 * length - 1, dtype=f32) - f32(length - 1)
+    distance = np.abs(offsets)[:, None]
+    halves = f32(2.0) ** np.linspace(3.0, math.log2(length), family, dtype=f32)
+    decays = np.exp(f32(-math.log(2.0)) / halves[None, :] * distance)
+    widths = f32(2.0) ** np.arange(1, family + 1, dtype=f32) - f32(1.0)
+    central = np.where(widths[None, :] > distance, f32(1.0), f32(0.0))
+    centers = np.linspace(0.0, float(length), family, dtype=f32)
+    spread = f32(length / family)
+    bump_rows = np.exp(f32(-0.5) * ((distance - centers[None, :]) / spread) ** 2)
+    positive = np.concatenate([decays, central, bump_rows], axis=1)
+    return np.concatenate([positive, np.sign(offsets)[:, None] * positive], axis=1)
 
 
 def per_device_linked(
@@ -1721,80 +2182,65 @@
     _, length, width = tokens.shape
     bf = jnp.bfloat16
     vectors = (
-        attn_norm_gain,
-        attn_norm_shift,
-        out_bias,
-        mlp_norm_gain,
-        mlp_norm_shift,
-        outer_bias,
-        inner_bias,
-        content_bias,
-        position_bias,
-    )
-    small = jnp.broadcast_to(jnp.concatenate(vectors)[None, :], (8, 3328))
-    limits = jnp.pad(thresholds, ((0, 7), (0, 126)))
-    table = basis_table(length, F)
-    empty = jnp.zeros((1, F), jnp.float32)
-    basis = jnp.concatenate([table, empty]).astype(bf)
-    flip = jnp.concatenate([table[::-1], empty]).astype(bf)
-    turn = jnp.eye(length, dtype=bf)[::-1]
+        (attn_norm_gain, 0, 0),
+        (attn_norm_shift, 1, 0),
+        (out_bias, 2, 0),
+        (mlp_norm_gain, 3, 0),
+        (mlp_norm_shift, 4, 0),
+        (outer_bias, 5, 0),
+        (inner_bias, 6, 0),
+        (content_bias, 0, 384),
+        (position_bias, 1, 384),
+    )
+    small = jnp.zeros((8, 512), bf)
+    for vector, row, col in vectors:
+        table = vector.reshape(-1, min(vector.shape[0], 384))
+        n, m = table.shape
+        small = small + jnp.pad(table, ((row, 8 - row - n), (col, 512 - col - m)))
+    limits = thresholds
+    table = basis_rows(length, F)
+    empty = np.zeros((1, F), np.float32)
+    basis = jnp.asarray(np.concatenate([table, empty]), bf)
+    flip = jnp.asarray(np.concatenate([table[::-1], empty]), bf)
+    flip_t = jnp.asarray(np.concatenate([table[::-1], empty]).T, bf)
+    turn = jnp.asarray(np.eye(length)[::-1], bf)
     flat_tokens = tokens.reshape(length, width)
-    (
-        layer_out,
-        p,
-        cq,
-        pq,
-        k,
-        v,
-        rr,
-        md,
-        hd,
-        nn,
-        fq,
-        fk,
-        fv,
-        vec,
-        gu0,
-        gu1,
-        gi0,
-        gi1,
-        go,
-        sums,
-    ) = forward_pass(
-        flat_tokens,
-        cotangent.reshape(length, width),
-        limits,
-        (query_weight, key_weight, value_weight, out_weight, outer_weight, inner_weight),
-        relative_weight,
-        small,
-        basis,
-        flip,
-    )
-    ou, oi, oo, ov, ok, oq, tokens_grad, rows, rel = backward_pass(
-        (gu0, gu1, gi0, gi1, go),
-        (p, cq, pq, k, v, rr, md, hd, flat_tokens, nn, fq, fk, fv, vec, sums),
-        (flip.T, turn),
-    )
-    f32 = jnp.float32
+    flat_cotangent = cotangent.reshape(length, width)
+    shards = (query_weight, key_weight, value_weight, out_weight, inner_weight, outer_weight)
+    outs = forward_pass(
+        flat_tokens, flat_cotangent, limits, shards, relative_weight, small, basis, flip
+    )
+    saved, weights, (vec, gu0, gu1, sums) = outs[:13], outs[13:21], outs[21:]
+    ou, oi, oo, ov, ok, oq, layer_out, tokens_grad, rows, rel = backward_pass(
+        (gu0, gu1),
+        saved,
+        weights,
+        shards,
+        (flat_tokens, flat_cotangent, limits, vec, sums, flip_t, turn),
+    )
+    outer, inner, out, value, key, query, relative, layer_out, tokens_grad, *vectors = finish_grads(
+        (ou, oi, oo, ov, ok, oq), rows, rel, layer_out, tokens_grad
+    )
+    gain, shift, out_b, mlp_gain, mlp_shift, outer_b, inner_b, content_b, position_b = vectors
     return (
         layer_out[None],
         tokens_grad[None],
-        rows[0, :384],
-        rows[1, :384],
-        oq.astype(f32),
-        ok.astype(f32),
-        ov.astype(f32),
-        jnp.concatenate([rel[0], rel[1]], axis=1),
-        rows[7, :128],
-        rows[7, 128:256],
-        oo.astype(f32),
-        rows[2, :384],
-        rows[3, :384],
-        rows[4, :384],
-        oi.astype(f32),
-        rows[6],
-        ou.astype(f32),
-        rows[5, :384],
+        gain,
+        shift,
+        query,
+        key,
+        value,
+        relative,
+        content_b,
+        position_b,
+        out,
+        out_b,
+        mlp_gain,
+        mlp_shift,
+        inner,
+        inner_b,
+        outer,
+        outer_b,
     )
 
 

time: 400 us -> 324 us (0.81)
  Pallas kernels: 362 us -> 316 us
  local copies, waits for them, and re-layouts: 22.3 us -> 4.79 us
  other arithmetic: 13.9 us -> 1.29 us
    pallas_call x1, Pallas kernels: 185 us -> 129 us  [forward_pass(): pl.pallas_call(forward_kernel, out_shape=tuple((jax.ShapeDtypeStruct(s, d...]
    convert_element_type x7 -> x0, other arithmetic: 13 us -> none  [the longest x1 2.82 us: per_device_linked(): ou.astype(f32)]
    pallas_call x0 -> x1, Pallas kernels: none -> 11.3 us  [finish_grads(): pl.pallas_call(lambda *refs: finish_kernel(count, *refs), out_shape=tuple...]
    unnamed x26 -> x0, local copies, waits for them, and re-layouts: 11 us -> none
    reshape x0 -> x7, local copies, waits for them, and re-layouts: none -> 4.79 us  [per_device_linked(): table = vector.reshape(-1, min(vector.shape[0], 384))]
where the time goes in v3:
time: 324 us; the launch traced here: 323 us
  Pallas kernels  316 us (98%)
  local copies, waits for them, and re-layouts  4.79 us (1%)
    pallas_call x1, Pallas kernels, backward_pass(): pl.pallas_call(backward_kernel, out_shape=tuple((jax.ShapeDtypeStruct(s,...  176 us
    pallas_call x1, Pallas kernels, forward_pass(): pl.pallas_call(forward_kernel, out_shape=tuple((jax.ShapeDtypeStruct(s, d...  129 us
    pallas_call x1, Pallas kernels, finish_grads(): pl.pallas_call(lambda *refs: finish_kernel(count, *refs), out_shape=tuple...  11.3 us

profile of v3, /device:TPU:0, one launch (start us, length us, event | category | flops | bytes accessed | tf_op | source)
XLA Modules:
  0.0 322.9 jit_solution(13123518860140797812)
XLA Ops:
  0.7 0.7 reshape.77
  1.3 0.7 reshape.78
  2.0 0.7 reshape.79
  2.7 0.7 reshape.80
  3.4 0.7 reshape.81
  4.1 0.7 reshape.83
  4.8 0.7 reshape.82
  5.4 1.3 pad_add_fusion.refs_10_
  6.7 128.9 %forward_pass.1 = (bf16[8,256,256]{2,1,0:T(8,128)(2,1)}, bf16[256,512]{1,0:T(8,128)(2,1)}, bf16[256,512]{1,0:T(8,128)(2,1)}, bf16[256,512]{1,0:T(8,128)(2,1)}, b...) custom-call(bf16[256,1536]{1,0:T(8,128)(2,1)} %bitcast.8, ...), custom_call_target="tpu_custom_call" | custom-call | tf_op jit(solution)/shard_map/forward_pass/pallas_call | solution.py:1147
  135.7 175.8 %backward_pass.1 = (bf16[768,1536]{1,0:T(8,128)(2,1)}, bf16[384,3072]{1,0:T(8,128)(2,1)}, bf16[384,1536]{1,0:T(8,128)(2,1)}, bf16[384,1536]{1,0:T(8,128)(2,1)}, ...) custom-call(bf16[4,2,2,2,96,384]{5,4,3,2,1,0:T(8,128)(2,1)} %bitcast, ...), custom_call_target="tpu_custom_call" | custom-call | tf_op jit(solution)/shard_map/backward_pass/pallas_call | solution.py:2057
  311.4 11.3 %finish_grads.1 = (f32[768,1536]{1,0:T(8,128)}, f32[384,3072]{1,0:T(8,128)}, f32[384,1536]{1,0:T(8,128)}, f32[384,1536]{1,0:T(8,128)}, f32[384,512]{1,0:T(8,128)...) custom-call(bf16[768,1536]{1,0:T(8,128)(2,1)} %get-tuple-element.96., ...), custom_call_target="tpu_custom_call" | custom-call | tf_op jit(solution)/shard_map/finish_grads/pallas_call | solution.py:2133

commit v4 on v3

--- a/solution.py
+++ b/solution.py
@@ -733,8 +733,6 @@
         send(m, mine, t.xr.at[m, k], at.xn)
         send(m, mine, t.yr.at[m, k], at.yn)
         send(m, mine, t.sr.at[m], at.sib)
-        if k == 2 and m + 3 < len(plan):
-            depart(m + 3)
 
     def forward(m, k):
         zz = source(k)
@@ -751,31 +749,14 @@
         arrive(block(m, zz, at.pd, 1), t.fyr.at[m, k])
         send(m, block(m, zz, at.pd), t.sr.at[m], at.sib)
 
-    for m in range(3):
-        depart(m)
+    depart(2)
+    depart(0)
     over_z(1, t.rel_h, t.rel)
-    units = [(m, k) for m in range(len(plan)) for k in range(3)]
-    steps = ((spread, 0), (forward, 2), (finish, 4))
-    events = []
-    for u in range(len(units) + 4):
-        for step, lag in steps:
-            if 0 <= u - lag < len(units):
-                events.append((step, units[u - lag]))
-    progress = [0]
-
-    def pump(count):
-        for _ in range(count):
-            if progress[0] < len(events):
-                step, unit = events[progress[0]]
-                step(*unit)
-                progress[0] += 1
-
-    def complete(m):
-        goal = events.index((finish, (m, 2))) + 1
-        pump(goal - progress[0])
+    def all_here(m):
         arrive(plan[m][3].at[pl.ds(0, 3), :, pl.ds(0, plan[m][4] // 2)], t.sr.at[m])
 
     def fetch(m, held):
+        all_here(m)
         shard, r0, c0, full, span = plan[m]
         copies = [
             pltpu.make_async_copy(
@@ -959,70 +940,135 @@
 
     t.sums[...] = jnp.zeros_like(t.sums)
     t.vec[...] = jnp.zeros_like(t.vec)
+    here = {}
+    spread(2, 0)
+    spread(2, 1)
+    spread(0, 0)
+    depart(1)
+    spread(0, 1)
+    spread(2, 2)
+    spread(0, 2)
+    spread(1, 0)
+    depart(3)
+    spread(1, 1)
+    spread(1, 2)
+    forward(0, 2)
+    forward(2, 0)
+    depart(5)
+    forward(0, 0)
+    depart(4)
+    forward(2, 2)
+    forward(0, 1)
     loads[0].wait()
     vectors()
-    pump(1)
     norm_rows(t.tok, t.normed, 0)
     give(1, t.normed, t.nn_h.at[1])
     store(t.normed, t.nn_h.at[0])
     store(t.vec, t.vec_h)
-    complete(0)
-    queries_here = fetch(0, t.q)
-    pump(2)
     clip_rows()
     store(t.od, t.od_h)
-    use(queries_here)
+    forward(1, 0)
+    forward(1, 1)
+    forward(1, 2)
+    spread(3, 0)
+    forward(2, 1)
+    finish(2, 2)
+    finish(0, 2)
+    finish(0, 0)
+    finish(0, 1)
+    spread(3, 1)
+    here[0] = fetch(0, t.q)
+    finish(1, 1)
+    spread(5, 0)
+    use(here[0])
     make_queries()
     store(t.cq, t.cq_h)
     store(t.pq, t.pq_h)
-    complete(1)
-    keys_here = fetch(1, t.k)
-    pump(3)
-    use(keys_here)
+    finish(1, 2)
+    spread(5, 1)
+    finish(2, 0)
+    finish(1, 0)
+    here[1] = fetch(1, t.k)
+    use(here[1])
     make_keys()
     store(t.kr, t.k_h)
     store(t.rr, t.rr_h)
-    complete(2)
-    values_here = fetch(2, t.v)
-    pump(2)
-    use(values_here)
+    finish(2, 1)
+    here[2] = fetch(2, t.v)
+    spread(3, 2)
+    use(here[2])
     make_values()
     store(t.vr, t.v_h)
-    for pair in range(4):
-        heads(pair)
-        pump(2)
+    forward(3, 1)
+    forward(3, 0)
+    spread(5, 2)
+    spread(4, 0)
+    depart(7)
+    heads(0)
+    spread(4, 1)
+    finish(3, 1)
+    depart(6)
+    heads(1)
+    spread(4, 2)
+    forward(3, 2)
+    finish(3, 0)
+    spread(7, 0)
+    heads(2)
+    forward(5, 2)
+    forward(4, 1)
+    forward(4, 0)
+    forward(5, 0)
+    forward(4, 2)
+    forward(5, 1)
+    spread(6, 0)
+    spread(6, 1)
+    heads(3)
     store(t.p, t.p_h)
     give(5, t.mixed, t.mx_h.at[1])
     store(t.mixed, t.mx_h.at[0])
-    complete(3)
-    out_here = fetch(3, t.o)
-    pump(2)
-    use(out_here)
+    finish(3, 2)
+    here[3] = fetch(3, t.o)
+    spread(6, 2)
+    use(here[3])
     attend_out()
     store(t.hidden, t.hid_h)
     store(t.nmid, t.nm_h.at[0])
-    complete(4)
-    inner_here = fetch(4, t.i0)
-    pump(2)
-    use(inner_here)
+    finish(4, 0)
+    finish(5, 0)
+    finish(4, 1)
+    finish(4, 2)
+    here[4] = fetch(4, t.i0)
+    spread(7, 1)
+    use(here[4])
     inner(0)
-    complete(5)
-    inner_here = fetch(5, t.i1)
-    pump(2)
-    use(inner_here)
+    finish(5, 2)
+    forward(7, 0)
+    spread(7, 2)
+    forward(6, 2)
+    finish(5, 1)
+    here[5] = fetch(5, t.i1)
+    forward(6, 0)
+    use(here[5])
     inner(1)
     store(t.act.at[0], t.act_h)
     store(t.slope, t.slope_h)
-    pump(2)
+    finish(7, 0)
+    forward(7, 1)
+    forward(6, 1)
     arrive(t.odc.at[1], t.pr.at[0])
     for h in range(2):
         arrive(t.act.at[1, :, pl.ds(0, width)], t.pr.at[3 + h])
     outer_product(t.act, t.odc, t.gu0, 0, 384)
-    pump(2)
+    forward(7, 2)
     outer_product(t.act, t.odc, t.gu1, 384, 384)
     store(t.sums, t.sums_h)
-    complete(6)
-    complete(7)
+    finish(6, 2)
+    finish(6, 1)
+    finish(6, 0)
+    finish(7, 1)
+    finish(7, 2)
+    all_here(6)
+    all_here(7)
 
     arrive(t.nn_h.at[1], t.pr.at[1])
     arrive(t.nm_h.at[1], t.pr.at[2])
@@ -1578,8 +1624,6 @@
         for copy in copies:
             copy.wait()
 
-    chain_start(0)
-    stage1(1)
     here0 = fetch(0, t.fu0, t.wu, t.s0)
     here1 = fetch(1, t.fu1, t.wu, t.s1, row=quarter)
     loads = [pltpu.make_async_copy(s, d, t.ld.at[k]) for k, (s, d) in enumerate(sources)]
@@ -1815,6 +1859,8 @@
         copy.start()
         stored.append(copy)
 
+    chain_start(0)
+    stage1(1)
     for copy in loads[:6]:
         copy.wait()
     use(here0)
@@ -1826,6 +1872,7 @@
     t.idc[0] = t.act[:, lanes(c * width, width)]
     here0 = fetch(2, t.fi0, t.wi, t.s0)
     here1 = fetch(3, t.fi1, t.wi, t.s1, col=width)
+    stage2(1)
     loads[7].wait()
     arrive(t.idc.at[1], t.pr.at[0])
     outer_product(t.cat, t.idc, t.gi0)
@@ -1834,7 +1881,7 @@
     outer_product(t.cat, t.idc, t.gi1, width // 2)
     loads[17].start()
     loads[18].start()
-    stage2(1)
+    stage3(1)
     loads[6].wait()
     use(here0)
     use(here1)
@@ -1851,28 +1898,36 @@
     loads[17].wait()
     arrive(t.bdc.at[1], t.pr.at[1])
     outer_product(t.cat, t.bdc, t.go)
+    chain_step(0, 2)
     stage1(4)
-    stage3(1)
     chain_start(3)
     for copy in loads[8:16]:
         copy.wait()
     left(t.idc.at[1], t.ps.at[0])
     heads(0)
-    chain_step(0, 2)
+    heads(1)
     stage2(2)
-    heads(1)
     heads(2)
+    stage4(1)
     chain_end(0)
+    chain_step(3, 1)
+    stage2(4)
     heads(3)
     trade()
     loads[18].wait()
     loads[16].wait()
-    for k, (pair, dst) in enumerate(((t.vdc, t.gv), (t.kdc, t.gk), (t.qdc, t.gq))):
-        arrive(pair.at[1], t.pr.at[2 + k])
-        outer_product(t.idc, pair, dst)
-        stage1(5 + k)
-    stage2(4)
-    rel_sums[1](0)
+    arrive(t.vdc.at[1], t.pr.at[2])
+    outer_product(t.idc, t.vdc, t.gv)
+    stage1(5)
+    arrive(t.kdc.at[1], t.pr.at[3])
+    outer_product(t.idc, t.kdc, t.gk)
+    stage3(4)
+    chain_step(3, 2)
+    arrive(t.qdc.at[1], t.pr.at[4])
+    outer_product(t.idc, t.qdc, t.gq)
+    stage3(2)
+    stage5(1)
+    stage1(6)
     use(here0)
     use(here1)
     use(here2)
@@ -1880,52 +1935,48 @@
     store(t.od, t.tg_h)
     t.ek[0] = t.eb[...]
     row_sums[0]()
-    stage3(2)
-    chain_step(3, 1)
+    rel_sums[1](0)
+    stage2(5)
+    row_sums[1](0)
+    stage1(7)
+    stage3(5)
+    stage2(6)
+    chain_end(3)
     chain_plane(0)
-    stage4(1)
+    stage2(7)
     rel_sums[1](1)
-    row_sums[1](0)
-    stage2(5)
-    stage3(4)
+    stage4(4)
+    row_sums[1](1)
     chain_last(0)
-    stage5(1)
+    chain_plane(3)
+    stage5(4)
+    stage5(0)
+    stage3(6)
+    chain_last(3)
+    stage4(2)
     rel_sums[1](2)
-    row_sums[1](1)
-    chain_step(3, 2)
-    stage2(6)
-    stage2(7)
+    stage3(7)
+    row_sums[1](2)
+    stage4(5)
+    stage6(0)
+    stage5(3)
+    stage4(6)
+    stage5(5)
     stage6(1)
-    stage5(0)
-    row_sums[1](2)
-    stage3(5)
-    stage3(6)
-    stage3(7)
-    stage4(2)
-    stage6(0)
-    chain_end(3)
+    stage5(6)
+    stage4(7)
     rel_sums[2]()
+    store(t.rg.at[0:48, 0:256], t.rg_h.at[c])
+    remote(t.rg.at[0:48, 0:256], t.rg_h.at[c], t.xs.at[6], t.xr.at[6], at.sib).start()
+    stage5(2)
     row_sums[2]()
     store(t.eo, t.e_h)
-    store(t.rg.at[0:48, 0:256], t.rg_h.at[c])
-    remote(t.rg.at[0:48, 0:256], t.rg_h.at[c], t.xs.at[6], t.xr.at[6], at.sib).start()
-    stage4(4)
-    stage5(2)
-    chain_plane(3)
-    stage4(5)
-    stage5(4)
+    stage5(7)
+    stage6(6)
+    stage6(5)
     stage6(2)
-    chain_last(3)
-    stage4(6)
-    stage4(7)
-    stage5(5)
+    stage6(3)
     stage6(4)
-    stage5(3)
-    stage5(6)
-    stage5(7)
-    stage6(5)
-    stage6(3)
-    stage6(6)
     stage6(7)
 
     for m in range(UNITS):

time: 324 us -> 301 us (0.929)
  Pallas kernels: 316 us -> 294 us
    pallas_call x1, Pallas kernels: 176 us -> 157 us  [backward_pass(): pl.pallas_call(backward_kernel, out_shape=tuple((jax.ShapeDtypeStruct(s,...]
    pallas_call x1, Pallas kernels: 129 us -> 125 us  [forward_pass(): pl.pallas_call(forward_kernel, out_shape=tuple((jax.ShapeDtypeStruct(s, d...]
where the time goes in v4:
time: 301 us
  Pallas kernels  294 us (98%)
  local copies, waits for them, and re-layouts  4.79 us (2%)
    pallas_call x1, Pallas kernels, backward_pass(): pl.pallas_call(backward_kernel, out_shape=tuple((jax.ShapeDtypeStruct(s,...  157 us
    pallas_call x1, Pallas kernels, forward_pass(): pl.pallas_call(forward_kernel, out_shape=tuple((jax.ShapeDtypeStruct(s, d...  125 us
    pallas_call x1, Pallas kernels, finish_grads(): pl.pallas_call(lambda *refs: finish_kernel(count, *refs), out_shape=tuple...  11.3 us

profile of v4, /device:TPU:0, one launch (start us, length us, event | category | flops | bytes accessed | tf_op | source)
XLA Modules:
  0.0 300.8 jit_solution(16316518004647170423)
XLA Ops:
  0.7 0.7 reshape.77
  1.3 0.7 reshape.78
  2.0 0.7 reshape.79
  2.7 0.7 reshape.80
  3.4 0.7 reshape.81
  4.1 0.7 reshape.83
  4.8 0.7 reshape.82
  5.4 1.3 pad_add_fusion.refs_10_
  6.7 125.5 %forward_pass.1 = (bf16[8,256,256]{2,1,0:T(8,128)(2,1)}, bf16[256,512]{1,0:T(8,128)(2,1)}, bf16[256,512]{1,0:T(8,128)(2,1)}, bf16[256,512]{1,0:T(8,128)(2,1)}, b...) custom-call(bf16[256,1536]{1,0:T(8,128)(2,1)} %bitcast.8, ...), custom_call_target="tpu_custom_call" | custom-call | tf_op jit(solution)/shard_map/forward_pass/pallas_call | solution.py:1193
  132.2 157.2 %backward_pass.1 = (bf16[768,1536]{1,0:T(8,128)(2,1)}, bf16[384,3072]{1,0:T(8,128)(2,1)}, bf16[384,1536]{1,0:T(8,128)(2,1)}, bf16[384,1536]{1,0:T(8,128)(2,1)}, ...) custom-call(bf16[4,2,2,2,96,384]{5,4,3,2,1,0:T(8,128)(2,1)} %bitcast, ...), custom_call_target="tpu_custom_call" | custom-call | tf_op jit(solution)/shard_map/backward_pass/pallas_call | solution.py:2108
  289.4 11.3 %finish_grads.1 = (f32[768,1536]{1,0:T(8,128)}, f32[384,3072]{1,0:T(8,128)}, f32[384,1536]{1,0:T(8,128)}, f32[384,1536]{1,0:T(8,128)}, f32[384,512]{1,0:T(8,128)...) custom-call(bf16[768,1536]{1,0:T(8,128)(2,1)} %get-tuple-element.96., ...), custom_call_target="tpu_custom_call" | custom-call | tf_op jit(solution)/shard_map/finish_grads/pallas_call | solution.py:2184

commit v5 on v4

--- a/solution.py
+++ b/solution.py
@@ -749,8 +749,9 @@
         arrive(block(m, zz, at.pd, 1), t.fyr.at[m, k])
         send(m, block(m, zz, at.pd), t.sr.at[m], at.sib)
 
+    depart(0)
+    depart(1)
     depart(2)
-    depart(0)
     over_z(1, t.rel_h, t.rel)
     def all_here(m):
         arrive(plan[m][3].at[pl.ds(0, 3), :, pl.ds(0, plan[m][4] // 2)], t.sr.at[m])
@@ -941,23 +942,17 @@
     t.sums[...] = jnp.zeros_like(t.sums)
     t.vec[...] = jnp.zeros_like(t.vec)
     here = {}
+    spread(0, 0)
+    spread(1, 0)
+    spread(0, 1)
+    forward(0, 0)
+    spread(1, 1)
     spread(2, 0)
+    forward(1, 0)
+    spread(0, 2)
     spread(2, 1)
-    spread(0, 0)
-    depart(1)
-    spread(0, 1)
-    spread(2, 2)
-    spread(0, 2)
-    spread(1, 0)
+    spread(1, 2)
     depart(3)
-    spread(1, 1)
-    spread(1, 2)
-    forward(0, 2)
-    forward(2, 0)
-    depart(5)
-    forward(0, 0)
-    depart(4)
-    forward(2, 2)
     forward(0, 1)
     loads[0].wait()
     vectors()
@@ -967,104 +962,109 @@
     store(t.vec, t.vec_h)
     clip_rows()
     store(t.od, t.od_h)
-    forward(1, 0)
+    forward(0, 2)
     forward(1, 1)
+    spread(2, 2)
     forward(1, 2)
-    spread(3, 0)
     forward(2, 1)
-    finish(2, 2)
-    finish(0, 2)
+    finish(1, 1)
+    depart(4)
     finish(0, 0)
     finish(0, 1)
-    spread(3, 1)
+    finish(0, 2)
+    finish(1, 0)
     here[0] = fetch(0, t.q)
-    finish(1, 1)
-    spread(5, 0)
+    forward(2, 0)
+    depart(5)
     use(here[0])
     make_queries()
     store(t.cq, t.cq_h)
     store(t.pq, t.pq_h)
+    spread(3, 0)
     finish(1, 2)
-    spread(5, 1)
-    finish(2, 0)
-    finish(1, 0)
     here[1] = fetch(1, t.k)
+    forward(2, 2)
+    spread(3, 1)
     use(here[1])
     make_keys()
     store(t.kr, t.k_h)
     store(t.rr, t.rr_h)
     finish(2, 1)
+    spread(4, 0)
+    spread(5, 0)
+    spread(4, 1)
+    finish(2, 2)
+    depart(6)
+    finish(2, 0)
     here[2] = fetch(2, t.v)
-    spread(3, 2)
     use(here[2])
     make_values()
     store(t.vr, t.v_h)
+    forward(3, 0)
+    spread(5, 1)
+    heads(0)
+    spread(3, 2)
+    heads(1)
     forward(3, 1)
-    forward(3, 0)
+    forward(4, 1)
+    spread(4, 2)
+    heads(2)
+    forward(3, 2)
     spread(5, 2)
-    spread(4, 0)
     depart(7)
-    heads(0)
-    spread(4, 1)
     finish(3, 1)
-    depart(6)
-    heads(1)
-    spread(4, 2)
-    forward(3, 2)
-    finish(3, 0)
-    spread(7, 0)
-    heads(2)
-    forward(5, 2)
-    forward(4, 1)
+    forward(5, 1)
     forward(4, 0)
-    forward(5, 0)
-    forward(4, 2)
-    forward(5, 1)
-    spread(6, 0)
-    spread(6, 1)
     heads(3)
     store(t.p, t.p_h)
     give(5, t.mixed, t.mx_h.at[1])
     store(t.mixed, t.mx_h.at[0])
+    forward(4, 2)
     finish(3, 2)
+    spread(6, 0)
+    spread(6, 1)
+    forward(5, 0)
+    finish(3, 0)
     here[3] = fetch(3, t.o)
-    spread(6, 2)
     use(here[3])
     attend_out()
     store(t.hidden, t.hid_h)
     store(t.nmid, t.nm_h.at[0])
+    spread(6, 2)
+    finish(4, 1)
     finish(4, 0)
-    finish(5, 0)
-    finish(4, 1)
+    forward(5, 2)
+    spread(7, 0)
     finish(4, 2)
     here[4] = fetch(4, t.i0)
-    spread(7, 1)
     use(here[4])
     inner(0)
+    finish(5, 1)
+    forward(6, 0)
+    spread(7, 1)
+    forward(6, 1)
+    finish(5, 0)
+    forward(6, 2)
     finish(5, 2)
-    forward(7, 0)
-    spread(7, 2)
-    forward(6, 2)
-    finish(5, 1)
     here[5] = fetch(5, t.i1)
-    forward(6, 0)
     use(here[5])
     inner(1)
     store(t.act.at[0], t.act_h)
     store(t.slope, t.slope_h)
-    finish(7, 0)
+    spread(7, 2)
     forward(7, 1)
-    forward(6, 1)
+    finish(6, 1)
+    forward(7, 0)
     arrive(t.odc.at[1], t.pr.at[0])
     for h in range(2):
         arrive(t.act.at[1, :, pl.ds(0, width)], t.pr.at[3 + h])
     outer_product(t.act, t.odc, t.gu0, 0, 384)
+    finish(6, 2)
+    finish(6, 0)
     forward(7, 2)
     outer_product(t.act, t.odc, t.gu1, 384, 384)
     store(t.sums, t.sums_h)
-    finish(6, 2)
-    finish(6, 1)
-    finish(6, 0)
+    finish(7, 0)
     finish(7, 1)
     finish(7, 2)
     all_here(6)
@@ -1859,8 +1859,8 @@
         copy.start()
         stored.append(copy)
 
+    stage1(1)
     chain_start(0)
-    stage1(1)
     for copy in loads[:6]:
         copy.wait()
     use(here0)
@@ -1873,11 +1873,11 @@
     here0 = fetch(2, t.fi0, t.wi, t.s0)
     here1 = fetch(3, t.fi1, t.wi, t.s1, col=width)
     stage2(1)
+    chain_step(0, 1)
     loads[7].wait()
     arrive(t.idc.at[1], t.pr.at[0])
     outer_product(t.cat, t.idc, t.gi0)
     stage1(2)
-    chain_step(0, 1)
     outer_product(t.cat, t.idc, t.gi1, width // 2)
     loads[17].start()
     loads[18].start()
@@ -1895,39 +1895,44 @@
     pull_mixed()
     here0 = fetch(6, t.fq, t.wq, t.s0.at[:, :, 0:keys_all])
     here2 = fetch(7, t.fk, t.wk, t.s0.at[:, :, keys_all : 2 * keys_all])
+    chain_start(3)
+    chain_step(0, 2)
+    stage2(2)
     loads[17].wait()
     arrive(t.bdc.at[1], t.pr.at[1])
     outer_product(t.cat, t.bdc, t.go)
-    chain_step(0, 2)
     stage1(4)
-    chain_start(3)
     for copy in loads[8:16]:
         copy.wait()
     left(t.idc.at[1], t.ps.at[0])
     heads(0)
     heads(1)
-    stage2(2)
+    chain_end(0)
+    stage3(2)
+    stage4(1)
     heads(2)
-    stage4(1)
-    chain_end(0)
+    chain_plane(0)
     chain_step(3, 1)
+    stage5(1)
     stage2(4)
     heads(3)
     trade()
     loads[18].wait()
     loads[16].wait()
+    chain_last(0)
     arrive(t.vdc.at[1], t.pr.at[2])
     outer_product(t.idc, t.vdc, t.gv)
     stage1(5)
+    stage3(4)
     arrive(t.kdc.at[1], t.pr.at[3])
     outer_product(t.idc, t.kdc, t.gk)
-    stage3(4)
-    chain_step(3, 2)
     arrive(t.qdc.at[1], t.pr.at[4])
     outer_product(t.idc, t.qdc, t.gq)
-    stage3(2)
-    stage5(1)
+    chain_step(3, 2)
+    stage1(7)
     stage1(6)
+    stage2(5)
+    stage2(7)
     use(here0)
     use(here1)
     use(here2)
@@ -1936,47 +1941,42 @@
     t.ek[0] = t.eb[...]
     row_sums[0]()
     rel_sums[1](0)
-    stage2(5)
+    stage6(1)
     row_sums[1](0)
-    stage1(7)
+    chain_end(3)
+    stage2(6)
     stage3(5)
-    stage2(6)
-    chain_end(3)
-    chain_plane(0)
-    stage2(7)
+    stage5(0)
+    stage4(4)
+    stage3(6)
     rel_sums[1](1)
-    stage4(4)
+    chain_plane(3)
     row_sums[1](1)
-    chain_last(0)
-    chain_plane(3)
+    stage4(2)
+    chain_last(3)
     stage5(4)
-    stage5(0)
-    stage3(6)
-    chain_last(3)
-    stage4(2)
+    stage5(2)
+    stage3(7)
+    stage4(5)
+    stage4(6)
     rel_sums[1](2)
-    stage3(7)
+    stage5(3)
     row_sums[1](2)
-    stage4(5)
     stage6(0)
-    stage5(3)
-    stage4(6)
+    stage4(7)
+    stage6(2)
+    stage5(6)
     stage5(5)
-    stage6(1)
-    stage5(6)
-    stage4(7)
+    stage5(7)
+    stage6(4)
+    stage6(3)
     rel_sums[2]()
     store(t.rg.at[0:48, 0:256], t.rg_h.at[c])
     remote(t.rg.at[0:48, 0:256], t.rg_h.at[c], t.xs.at[6], t.xr.at[6], at.sib).start()
-    stage5(2)
+    stage6(5)
     row_sums[2]()
     store(t.eo, t.e_h)
-    stage5(7)
     stage6(6)
-    stage6(5)
-    stage6(2)
-    stage6(3)
-    stage6(4)
     stage6(7)
 
     for m in range(UNITS):

time: 301 us -> 292 us (0.970)
  Pallas kernels: 294 us -> 285 us
    pallas_call x1, Pallas kernels: 125 us -> 120 us  [forward_pass(): pl.pallas_call(forward_kernel, out_shape=tuple((jax.ShapeDtypeStruct(s, d...]
    pallas_call x1, Pallas kernels: 157 us -> 153 us  [backward_pass(): pl.pallas_call(backward_kernel, out_shape=tuple((jax.ShapeDtypeStruct(s,...]
where the time goes in v5:
time: 292 us
  Pallas kernels  285 us (98%)
  local copies, waits for them, and re-layouts  4.79 us (2%)
    pallas_call x1, Pallas kernels, backward_pass(): pl.pallas_call(backward_kernel, out_shape=tuple((jax.ShapeDtypeStruct(s,...  153 us
    pallas_call x1, Pallas kernels, forward_pass(): pl.pallas_call(forward_kernel, out_shape=tuple((jax.ShapeDtypeStruct(s, d...  120 us
    pallas_call x1, Pallas kernels, finish_grads(): pl.pallas_call(lambda *refs: finish_kernel(count, *refs), out_shape=tuple...  11.3 us

profile of v5, /device:TPU:0, one launch (start us, length us, event | category | flops | bytes accessed | tf_op | source)
XLA Modules:
  0.0 291.7 jit_solution(15708273531263734619)
XLA Ops:
  0.7 0.7 reshape.77
  1.3 0.7 reshape.78
  2.0 0.7 reshape.79
  2.7 0.7 reshape.80
  3.4 0.7 reshape.81
  4.1 0.7 reshape.83
  4.8 0.7 reshape.82
  5.4 1.3 pad_add_fusion.refs_10_
  6.7 120.3 %forward_pass.1 = (bf16[8,256,256]{2,1,0:T(8,128)(2,1)}, bf16[256,512]{1,0:T(8,128)(2,1)}, bf16[256,512]{1,0:T(8,128)(2,1)}, bf16[256,512]{1,0:T(8,128)(2,1)}, b...) custom-call(bf16[256,1536]{1,0:T(8,128)(2,1)} %bitcast.8, ...), custom_call_target="tpu_custom_call" | custom-call | tf_op jit(solution)/shard_map/forward_pass/pallas_call | solution.py:1193
  127.1 153.2 %backward_pass.1 = (bf16[768,1536]{1,0:T(8,128)(2,1)}, bf16[384,3072]{1,0:T(8,128)(2,1)}, bf16[384,1536]{1,0:T(8,128)(2,1)}, bf16[384,1536]{1,0:T(8,128)(2,1)}, ...) custom-call(bf16[4,2,2,2,96,384]{5,4,3,2,1,0:T(8,128)(2,1)} %bitcast, ...), custom_call_target="tpu_custom_call" | custom-call | tf_op jit(solution)/shard_map/backward_pass/pallas_call | solution.py:2108
  280.2 11.3 %finish_grads.1 = (f32[768,1536]{1,0:T(8,128)}, f32[384,3072]{1,0:T(8,128)}, f32[384,1536]{1,0:T(8,128)}, f32[384,1536]{1,0:T(8,128)}, f32[384,512]{1,0:T(8,128)...) custom-call(bf16[768,1536]{1,0:T(8,128)(2,1)} %get-tuple-element.96., ...), custom_call_target="tpu_custom_call" | custom-call | tf_op jit(solution)/shard_map/finish_grads/pallas_call | solution.py:2184

commit v6 on v5

--- a/solution.py
+++ b/solution.py
@@ -630,18 +630,22 @@
 
     keys_all = H * KEY
     quarter = width // 4
+    half_width = width // 2
     plan = (
-        (t.wq, 0, 0, t.fq, keys_all),
-        (t.wk, 0, 0, t.fk, keys_all),
-        (t.wv, 0, 0, t.fv, width),
-        (t.wo, 0, 0, t.fo, width),
-        (t.wi, 0, 0, t.fi0, width),
-        (t.wi, 0, width, t.fi1, width),
-        (t.wu, 0, 0, t.fu0, width),
-        (t.wu, quarter, 0, t.fu1, width),
+        (t.wq, 0, 0, t.fq, 0, keys_all, False),
+        (t.wk, 0, 0, t.fk, 0, keys_all, False),
+        (t.wv, 0, 0, t.fv, 0, width, False),
+        (t.wo, 0, 0, t.fo, 0, width, False),
+        (t.wi, 0, 0, t.fi0, 0, width, False),
+        (t.wi, 0, width, t.fi1, 0, width, False),
+        (t.wu, quarter, half_width, t.fu1, half_width, half_width, True),
+        (t.wu, quarter, 0, t.fu1, 0, half_width, False),
+        (t.wu, 0, 0, t.fu0, 0, width, False),
     )
 
     def rows_of(m, pp, part=None):
+        if plan[m][6]:
+            return 0, quarter
         rows = quarter // 4
         start = pp * rows
         if part is not None:
@@ -651,8 +655,10 @@
 
     def block(m, zz, pp, part=None):
         start, rows = rows_of(m, pp, part)
-        cols = plan[m][4] // 2
-        return plan[m][3].at[zz, pl.ds(pl.multiple_of(start, 16), rows), lanes(c * cols, cols)]
+        _, _, _, full, first, span, _ = plan[m]
+        cols = span // 2
+        rows = pl.ds(pl.multiple_of(start, 16), rows)
+        return full.at[zz, rows, lanes(first + c * cols, cols)]
 
     def send(m, ref, recv, target):
         remote(ref, ref, t.snd.at[m], recv, target).start()
@@ -682,7 +688,7 @@
     can_rise, can_sink = z < NARROW - 1, z > 0
 
     def own_piece(m):
-        shard, r0, c0, _, span = plan[m]
+        shard, r0, c0, _, _, span, _ = plan[m]
         start, rows = rows_of(m, p)
         cols = span // 2
         return shard.at[pl.ds(pl.multiple_of(r0 + start, 16), rows), lanes(c0 + c * cols, cols)]
@@ -730,8 +736,9 @@
         def _():
             remote(mine, mine, t.zs.at[m, k], t.zr.at[m, jnp.maximum(d - 2, 0)], below).start()
 
-        send(m, mine, t.xr.at[m, k], at.xn)
-        send(m, mine, t.yr.at[m, k], at.yn)
+        if not plan[m][6]:
+            send(m, mine, t.xr.at[m, k], at.xn)
+            send(m, mine, t.yr.at[m, k], at.yn)
         send(m, mine, t.sr.at[m], at.sib)
 
     def forward(m, k):
@@ -754,11 +761,11 @@
     depart(2)
     over_z(1, t.rel_h, t.rel)
     def all_here(m):
-        arrive(plan[m][3].at[pl.ds(0, 3), :, pl.ds(0, plan[m][4] // 2)], t.sr.at[m])
+        arrive(plan[m][3].at[pl.ds(0, 3), :, pl.ds(0, plan[m][5] // 2)], t.sr.at[m])
 
     def fetch(m, held):
         all_here(m)
-        shard, r0, c0, full, span = plan[m]
+        shard, r0, c0, full, _, span, _ = plan[m]
         copies = [
             pltpu.make_async_copy(
                 shard.at[pl.ds(r0, quarter), pl.ds(c0, span)], held.at[z], t.own.at[m, 0]
@@ -944,16 +951,15 @@
     here = {}
     spread(0, 0)
     spread(1, 0)
+    spread(1, 1)
+    forward(0, 0)
     spread(0, 1)
-    forward(0, 0)
-    spread(1, 1)
     spread(2, 0)
-    forward(1, 0)
+    spread(2, 1)
     spread(0, 2)
-    spread(2, 1)
+    forward(0, 1)
+    depart(3)
     spread(1, 2)
-    depart(3)
-    forward(0, 1)
     loads[0].wait()
     vectors()
     norm_rows(t.tok, t.normed, 0)
@@ -962,113 +968,119 @@
     store(t.vec, t.vec_h)
     clip_rows()
     store(t.od, t.od_h)
+    spread(2, 2)
+    forward(1, 1)
+    finish(0, 0)
     forward(0, 2)
-    forward(1, 1)
-    spread(2, 2)
+    depart(4)
+    forward(1, 0)
     forward(1, 2)
-    forward(2, 1)
-    finish(1, 1)
-    depart(4)
-    finish(0, 0)
+    depart(5)
     finish(0, 1)
+    depart(8)
+    forward(2, 2)
+    finish(1, 0)
+    spread(3, 0)
     finish(0, 2)
-    finish(1, 0)
     here[0] = fetch(0, t.q)
     forward(2, 0)
-    depart(5)
+    forward(2, 1)
     use(here[0])
     make_queries()
     store(t.cq, t.cq_h)
     store(t.pq, t.pq_h)
-    spread(3, 0)
     finish(1, 2)
+    spread(3, 1)
+    finish(1, 1)
     here[1] = fetch(1, t.k)
-    forward(2, 2)
-    spread(3, 1)
+    finish(2, 2)
     use(here[1])
     make_keys()
     store(t.kr, t.k_h)
     store(t.rr, t.rr_h)
+    finish(2, 0)
+    forward(3, 0)
     finish(2, 1)
+    spread(3, 2)
+    here[2] = fetch(2, t.v)
     spread(4, 0)
-    spread(5, 0)
     spread(4, 1)
-    finish(2, 2)
-    depart(6)
-    finish(2, 0)
-    here[2] = fetch(2, t.v)
     use(here[2])
     make_values()
     store(t.vr, t.v_h)
-    forward(3, 0)
+    forward(3, 1)
+    spread(4, 2)
+    depart(6)
+    heads(0)
+    forward(3, 2)
+    depart(7)
+    spread(5, 0)
+    forward(4, 0)
+    heads(1)
+    finish(3, 0)
+    finish(3, 1)
+    heads(2)
     spread(5, 1)
-    heads(0)
-    spread(3, 2)
-    heads(1)
-    forward(3, 1)
-    forward(4, 1)
-    spread(4, 2)
-    heads(2)
-    forward(3, 2)
-    spread(5, 2)
-    depart(7)
-    finish(3, 1)
-    forward(5, 1)
-    forward(4, 0)
     heads(3)
     store(t.p, t.p_h)
     give(5, t.mixed, t.mx_h.at[1])
     store(t.mixed, t.mx_h.at[0])
+    spread(5, 2)
     forward(4, 2)
     finish(3, 2)
-    spread(6, 0)
-    spread(6, 1)
-    forward(5, 0)
-    finish(3, 0)
+    forward(4, 1)
     here[3] = fetch(3, t.o)
+    spread(7, 0)
+    spread(7, 1)
     use(here[3])
     attend_out()
     store(t.hidden, t.hid_h)
     store(t.nmid, t.nm_h.at[0])
-    spread(6, 2)
+    finish(4, 0)
+    forward(5, 1)
+    forward(5, 2)
+    forward(5, 0)
+    spread(7, 2)
+    spread(8, 0)
+    spread(6, 0)
+    spread(8, 1)
+    finish(4, 2)
     finish(4, 1)
-    finish(4, 0)
-    forward(5, 2)
-    spread(7, 0)
-    finish(4, 2)
     here[4] = fetch(4, t.i0)
     use(here[4])
     inner(0)
+    spread(8, 2)
+    finish(5, 2)
     finish(5, 1)
-    forward(6, 0)
-    spread(7, 1)
-    forward(6, 1)
     finish(5, 0)
-    forward(6, 2)
-    finish(5, 2)
     here[5] = fetch(5, t.i1)
     use(here[5])
     inner(1)
     store(t.act.at[0], t.act_h)
     store(t.slope, t.slope_h)
-    spread(7, 2)
+    forward(7, 0)
+    spread(6, 1)
+    forward(8, 0)
+    forward(7, 2)
     forward(7, 1)
-    finish(6, 1)
-    forward(7, 0)
+    forward(8, 1)
     arrive(t.odc.at[1], t.pr.at[0])
     for h in range(2):
         arrive(t.act.at[1, :, pl.ds(0, width)], t.pr.at[3 + h])
     outer_product(t.act, t.odc, t.gu0, 0, 384)
-    finish(6, 2)
-    finish(6, 0)
-    forward(7, 2)
+    forward(8, 2)
+    finish(7, 0)
     outer_product(t.act, t.odc, t.gu1, 384, 384)
     store(t.sums, t.sums_h)
-    finish(7, 0)
     finish(7, 1)
+    finish(8, 0)
+    spread(6, 2)
+    finish(8, 2)
+    finish(8, 1)
     finish(7, 2)
     all_here(6)
     all_here(7)
+    all_here(8)
 
     arrive(t.nn_h.at[1], t.pr.at[1])
     arrive(t.nm_h.at[1], t.pr.at[2])
@@ -1098,9 +1110,10 @@
         def _():
             left(mine, t.zs.at[m, 4])
 
-        full, cols = plan[m][3], plan[m][4] // 2
+        full, cols = plan[m][3], plan[m][5] // 2
         left(full.at[pl.ds(0, 3), :, pl.ds(0, cols)], t.snd.at[m])
-        left(full.at[pl.ds(0, 3), pl.ds(0, 3 * quarter // 4), pl.ds(0, cols)], t.snd.at[m])
+        if not plan[m][6]:
+            left(full.at[pl.ds(0, 3), pl.ds(0, 3 * quarter // 4), pl.ds(0, cols)], t.snd.at[m])
     for copy in stored:
         copy.wait()
 
@@ -1172,15 +1185,15 @@
         ((8, 2 * width), f32),
     )
     sems = [
-        DMA((8, 3)),
-        DMA((8, 5)),
-        DMA((8, 3)),
-        DMA((8, 3)),
-        DMA((8, 3)),
-        DMA((8, 3)),
-        DMA((8,)),
-        DMA((8,)),
-        DMA((8, 4)),
+        DMA((9, 3)),
+        DMA((9, 5)),
+        DMA((9, 3)),
+        DMA((9, 3)),
+        DMA((9, 3)),
+        DMA((9, 3)),
+        DMA((9,)),
+        DMA((9,)),
+        DMA((9, 4)),
         DMA((7,)),
         DMA((2,)),
         DMA((2,)),

time: 292 us -> 290 us (level)
  Pallas kernels: 285 us -> 282 us
where the time goes in v6:
time: 290 us; the launch traced here: 289 us
  Pallas kernels  282 us (97%)
  local copies, waits for them, and re-layouts  4.79 us (2%)
    pallas_call x1, Pallas kernels, backward_pass(): pl.pallas_call(backward_kernel, out_shape=tuple((jax.ShapeDtypeStruct(s,...  152 us
    pallas_call x1, Pallas kernels, forward_pass(): pl.pallas_call(forward_kernel, out_shape=tuple((jax.ShapeDtypeStruct(s, d...  119 us
    pallas_call x1, Pallas kernels, finish_grads(): pl.pallas_call(lambda *refs: finish_kernel(count, *refs), out_shape=tuple...  11.3 us

profile of v6, /device:TPU:0, one launch (start us, length us, event | category | flops | bytes accessed | tf_op | source)
XLA Modules:
  0.0 289.2 jit_solution(15410879661125837347)
XLA Ops:
  0.7 0.7 reshape.77
  1.3 0.7 reshape.78
  2.0 0.7 reshape.79
  2.7 0.7 reshape.80
  3.4 0.7 reshape.81
  4.1 0.7 reshape.83
  4.8 0.7 reshape.82
  5.4 1.3 pad_add_fusion.refs_10_
  6.7 119.2 %forward_pass.1 = (bf16[8,256,256]{2,1,0:T(8,128)(2,1)}, bf16[256,512]{1,0:T(8,128)(2,1)}, bf16[256,512]{1,0:T(8,128)(2,1)}, bf16[256,512]{1,0:T(8,128)(2,1)}, b...) custom-call(bf16[256,1536]{1,0:T(8,128)(2,1)} %bitcast.8, ...), custom_call_target="tpu_custom_call" | custom-call | tf_op jit(solution)/shard_map/forward_pass/pallas_call | solution.py:1206
  126.0 151.8 %backward_pass.1 = (bf16[768,1536]{1,0:T(8,128)(2,1)}, bf16[384,3072]{1,0:T(8,128)(2,1)}, bf16[384,1536]{1,0:T(8,128)(2,1)}, bf16[384,1536]{1,0:T(8,128)(2,1)}, ...) custom-call(bf16[4,2,2,2,96,384]{5,4,3,2,1,0:T(8,128)(2,1)} %bitcast, ...), custom_call_target="tpu_custom_call" | custom-call | tf_op jit(solution)/shard_map/backward_pass/pallas_call | solution.py:2121
  277.7 11.3 %finish_grads.1 = (f32[768,1536]{1,0:T(8,128)}, f32[384,3072]{1,0:T(8,128)}, f32[384,1536]{1,0:T(8,128)}, f32[384,1536]{1,0:T(8,128)}, f32[384,512]{1,0:T(8,128)...) custom-call(bf16[768,1536]{1,0:T(8,128)(2,1)} %get-tuple-element.96., ...), custom_call_target="tpu_custom_call" | custom-call | tf_op jit(solution)/shard_map/finish_grads/pallas_call | solution.py:2197
